TPU v7x, 32 devices: a whole 2x2x4 slice. The times are simulated.
32 devices in a mesh: seq: 8 (over z, core), shard: 4 (over y, x).
Axes of the slice: x: 2, y: 2, z: 4, core: 2. Of those that a mesh axis runs over, the one named last changes fastest.
Arguments:
- images: bfloat16 [4, 2304, 1024], P('shard', 'seq'), may hold values from -6 to 6
- norm1_scale: bfloat16 [2, 1024], P(None, 'shard'), may hold values from 0.5 to 1.5
- norm1_shift: bfloat16 [2, 1024], P(None, 'shard'), may hold values from -1.5 to 1.5
- qkv_weight: bfloat16 [2, 1024, 3072], P(None, 'shard'), may hold values from -0.25 to 0.25
- qv_bias: bfloat16 [2, 2048], P(None, 'shard'), may hold values from -1.5 to 1.5
- out_weight: bfloat16 [2, 1024, 1024], P(None, 'shard'), may hold values from -0.75 to 0.75
- out_bias: bfloat16 [2, 1024], P(None, 'shard'), may hold values from -1.5 to 1.5
- norm2_scale: bfloat16 [2, 1024], P(None, 'shard'), may hold values from 0.5 to 1.5
- norm2_shift: bfloat16 [2, 1024], P(None, 'shard'), may hold values from -1.5 to 1.5
- up_weight: bfloat16 [2, 1024, 4096], P(None, 'shard'), may hold values from -0.1875 to 0.1875
- up_bias: bfloat16 [2, 4096], P(None, 'shard'), may hold values from -2.5 to 2.5
- down_weight: bfloat16 [2, 4096, 1024], P(None, 'shard'), may hold values from -0.125 to 0.125
- down_bias: bfloat16 [2, 1024], P(None, 'shard'), may hold values from -1.5 to 1.5
- cotangent: bfloat16 [4, 2304, 1024], P('shard', 'seq'), may hold values from -6 to 6
Outputs:
- outputs: bfloat16 [4, 2304, 1024], P('shard', 'seq')
- input_grad: float32 [4, 2304, 1024], P('shard', 'seq')
- grad_norm1_scale: float32 [2, 1024], P(None, 'shard')
- grad_norm1_shift: float32 [2, 1024], P(None, 'shard')
- grad_qkv_weight: float32 [2, 1024, 3072], P(None, 'shard')
- grad_qv_bias: float32 [2, 2048], P(None, 'shard')
- grad_out_weight: float32 [2, 1024, 1024], P(None, 'shard')
- grad_out_bias: float32 [2, 1024], P(None, 'shard')
- grad_norm2_scale: float32 [2, 1024], P(None, 'shard')
- grad_norm2_shift: float32 [2, 1024], P(None, 'shard')
- grad_up_weight: float32 [2, 1024, 4096], P(None, 'shard')
- grad_up_bias: float32 [2, 4096], P(None, 'shard')
- grad_down_weight: float32 [2, 4096, 1024], P(None, 'shard')
- grad_down_bias: float32 [2, 1024], P(None, 'shard')
All inputs are finite; a program needn't handle non-finite values.
Results may differ from a plain program's by a relative error of at most 0.015.
Values may be sent and summed in bfloat16 or wider, within the bound.
No kernel may reach another device: no remote copies, remote signals or barrier semaphores. Data moves between devices by JAX's collectives and lax.ppermute only.
A program may use at most 320 MiB of HBM per device.

v0:
```python
from functools import partial

import jax
import jax.numpy as jnp
from jax import lax
from jax.sharding import PartitionSpec as P

HD = 64


def outer_sum(left, right):
    return lax.dot_general(
        left, right, (((0,), (0,)), ((), ())), preferred_element_type=jnp.float32
    )


def times_transposed(left, right):
    return lax.dot_general(
        left, right, (((1,), (1,)), ((), ())), preferred_element_type=jnp.float32
    )


def norm_forward(stream, scales, offset):
    average = jnp.mean(stream, axis=-1, keepdims=True)
    centered = stream - average
    variance = jnp.mean(centered * centered, axis=-1, keepdims=True)
    inverse = lax.rsqrt(variance + 1e-06)
    return ((centered * inverse * scales + offset).astype(jnp.bfloat16), inverse)


def norm_backward(stream, inverse, scales, upstream):
    average = jnp.mean(stream, axis=-1, keepdims=True)
    unit_rows = (stream - average) * inverse
    grad_scale = jnp.sum(upstream * unit_rows, axis=0)
    grad_shift = jnp.sum(upstream, axis=0)
    scaled_grad = upstream * scales
    stream_grad = inverse * (
        scaled_grad
        - jnp.mean(scaled_grad, axis=-1, keepdims=True)
        - unit_rows * jnp.mean(scaled_grad * unit_rows, axis=-1, keepdims=True)
    )
    return (stream_grad, grad_scale, grad_shift)


def attend_items(received):
    seq_len = received.shape[1]
    local_heads = received.shape[3] // HD
    query_rows = 768
    blocks = seq_len // query_rows
    score_scale = HD ** (-0.5)

    def one_image(item_data):
        queries = item_data[:, 0].reshape(blocks, query_rows, local_heads, HD)
        key_heads = item_data[:, 1].reshape(seq_len, local_heads, HD)
        value_heads = item_data[:, 2].reshape(seq_len, local_heads, HD)

        def one_one_block(query_block):
            scores = (
                jnp.einsum(
                    "qhd,khd->hqk", query_block, key_heads, preferred_element_type=jnp.float32
                )
                * score_scale
            )
            row_max = jnp.max(scores, axis=-1, keepdims=True)
            exponent = jnp.exp(scores - row_max)
            row_total = jnp.sum(exponent, axis=-1, keepdims=True)
            probability = (exponent / row_total).astype(jnp.bfloat16)
            head_mixed = jnp.einsum(
                "hqk,khd->qhd", probability, value_heads, preferred_element_type=jnp.float32
            )
            return (
                head_mixed.astype(jnp.bfloat16).reshape(query_rows, local_heads * HD),
                (row_max + jnp.log(row_total))[..., 0],
            )

        head_mixed, log_total = lax.map(one_one_block, queries)
        log_total = jnp.transpose(log_total, (1, 0, 2)).reshape(local_heads, seq_len)
        return (head_mixed.reshape(seq_len, local_heads * HD), log_total)

    head_mixed, log_total = lax.map(one_image, received)
    return (head_mixed, log_total, received)


def attend_back(item_data):
    received, log_total, head_grad = item_data
    seq_len = received.shape[0]
    local_heads = received.shape[2] // HD
    query_rows = 768
    blocks = seq_len // query_rows
    score_scale = HD ** (-0.5)
    queries = received[:, 0].reshape(blocks, query_rows, local_heads, HD)
    key_heads = received[:, 1].reshape(seq_len, local_heads, HD)
    value_heads = received[:, 2].reshape(seq_len, local_heads, HD)
    log_blocks = jnp.transpose(log_total.reshape(local_heads, blocks, query_rows), (1, 0, 2))
    grad_blocks = head_grad.reshape(blocks, query_rows, local_heads, HD)

    def attend_one_block(running, block_data):
        key_grad, value_grad = running
        query_block, log_block, out_block = block_data
        scores = (
            jnp.einsum("qhd,khd->hqk", query_block, key_heads, preferred_element_type=jnp.float32)
            * score_scale
        )
        probability = jnp.exp(scores - log_block[..., None])
        value_grad = value_grad + jnp.einsum(
            "hqk,qhd->khd",
            probability.astype(jnp.bfloat16),
            out_block,
            preferred_element_type=jnp.float32,
        )
        probability_grad = jnp.einsum(
            "qhd,khd->hqk", out_block, value_heads, preferred_element_type=jnp.float32
        )
        row_inner = jnp.sum(probability * probability_grad, axis=-1, keepdims=True)
        dscore = (probability * (probability_grad - row_inner)).astype(jnp.bfloat16)
        dquery = (
            jnp.einsum("hqk,khd->qhd", dscore, key_heads, preferred_element_type=jnp.float32)
            * score_scale
        )
        key_grad = (
            key_grad
            + jnp.einsum("hqk,qhd->khd", dscore, query_block, preferred_element_type=jnp.float32)
            * score_scale
        )
        return ((key_grad, value_grad), dquery.astype(jnp.bfloat16))

    zeros_start = jnp.zeros((seq_len, local_heads, HD), jnp.float32)
    (key_grad, value_grad), query_grad = lax.scan(
        attend_one_block, (zeros_start, zeros_start), (queries, log_blocks, grad_blocks)
    )
    return jnp.stack(
        [
            query_grad.reshape(seq_len, local_heads * HD),
            key_grad.astype(jnp.bfloat16).reshape(seq_len, local_heads * HD),
            value_grad.astype(jnp.bfloat16).reshape(seq_len, local_heads * HD),
        ],
        axis=1,
    )


def reorder_rows(gradient, seq_count, shard_count):
    row_total = gradient.shape[0]
    regrouped = gradient.reshape(
        (shard_count, seq_count, row_total // (seq_count * shard_count)) + gradient.shape[1:]
    )
    return jnp.swapaxes(regrouped, 0, 1).reshape(gradient.shape)


def body(
    images,
    norm1_scale,
    norm1_shift,
    qkv_weight,
    qv_bias,
    out_weight,
    out_bias,
    norm2_scale,
    norm2_shift,
    up_weight,
    up_bias,
    down_weight,
    down_bias,
    cotangent,
):
    shards = (
        norm1_scale,
        norm1_shift,
        qkv_weight,
        qv_bias,
        out_weight,
        out_bias,
        norm2_scale,
        norm2_shift,
        up_weight,
        up_bias,
        down_weight,
        down_bias,
    )
    image_count, local_len, model_width = images.shape
    seq_count = lax.axis_size("seq")
    shard_count = lax.axis_size("shard")
    layer_total = norm1_scale.shape[0]
    stream = images.astype(jnp.float32).reshape(-1, model_width)
    saved_layers = []
    for layer_index in range(layer_total):
        layer_parts = [member[layer_index] for member in shards]
        weights = (
            lax.all_gather(layer_parts[0], "shard", axis=0, tiled=True),
            lax.all_gather(layer_parts[1], "shard", axis=0, tiled=True),
            lax.all_gather(layer_parts[2], "shard", axis=0, tiled=True),
            lax.all_gather(layer_parts[3], "shard", axis=0, tiled=True),
            lax.all_gather(layer_parts[4], "shard", axis=0, tiled=True),
            lax.all_gather(layer_parts[5], "shard", axis=0, tiled=True),
            lax.all_gather(layer_parts[6], "shard", axis=0, tiled=True),
            lax.all_gather(layer_parts[7], "shard", axis=0, tiled=True),
            lax.all_gather(layer_parts[8], "shard", axis=0, tiled=True),
            lax.all_gather(layer_parts[9], "shard", axis=0, tiled=True),
            lax.all_gather(layer_parts[10], "shard", axis=0, tiled=True),
            lax.all_gather(layer_parts[11], "shard", axis=0, tiled=True),
        )
        (
            scale_one,
            shift_one,
            qkv_full,
            qv_full,
            out_full,
            out_shift,
            scale_two,
            shift_two,
            up_full,
            up_shift,
            down_full,
            down_shift,
        ) = weights
        normed_one, inverse_one = norm_forward(stream, scale_one, shift_one)
        zero_keys = jnp.zeros((model_width,), jnp.float32)
        bias_full = jnp.concatenate(
            [
                qv_full[:model_width].astype(jnp.float32),
                zero_keys,
                qv_full[model_width:].astype(jnp.float32),
            ]
        )
        projected = (
            jnp.dot(normed_one, qkv_full, preferred_element_type=jnp.float32) + bias_full
        ).astype(jnp.bfloat16)
        packed = projected.reshape(image_count, local_len, 3, model_width)
        head_mixed, log_total, received = attend_items(
            lax.all_to_all(packed, "seq", split_axis=3, concat_axis=1, tiled=True)
        )
        attended = lax.all_to_all(
            head_mixed, "seq", split_axis=1, concat_axis=2, tiled=True
        ).reshape(-1, model_width)
        middle = (
            stream + jnp.dot(attended, out_full, preferred_element_type=jnp.float32) + out_shift
        )
        normed_two, inverse_two = norm_forward(middle, scale_two, shift_two)
        pre_act = jnp.dot(normed_two, up_full, preferred_element_type=jnp.float32) + up_shift
        hidden = jax.nn.gelu(pre_act, approximate=False).astype(jnp.bfloat16)
        kept_weights = None
        saved_layers.append(
            (
                stream,
                normed_one,
                inverse_one,
                received,
                log_total,
                attended,
                middle,
                normed_two,
                inverse_two,
                pre_act,
                hidden,
                kept_weights,
            )
        )
        stream = (
            middle + jnp.dot(hidden, down_full, preferred_element_type=jnp.float32) + down_shift
        )
    results = stream.astype(jnp.bfloat16).reshape(image_count, local_len, model_width)
    grad_stream = cotangent.astype(jnp.float32).reshape(-1, model_width)
    grad_layers = []
    for layer_index in reversed(range(layer_total)):
        (
            stream_in,
            normed_one,
            inverse_one,
            received,
            log_total,
            attended,
            middle,
            normed_two,
            inverse_two,
            pre_act,
            hidden,
            kept_weights,
        ) = saved_layers[layer_index]
        layer_parts = [member[layer_index] for member in shards]
        weights = (
            lax.all_gather(layer_parts[0], "shard", axis=0, tiled=True),
            lax.all_gather(layer_parts[1], "shard", axis=0, tiled=True),
            lax.all_gather(layer_parts[2], "shard", axis=0, tiled=True),
            lax.all_gather(layer_parts[3], "shard", axis=0, tiled=True),
            lax.all_gather(layer_parts[4], "shard", axis=0, tiled=True),
            lax.all_gather(layer_parts[5], "shard", axis=0, tiled=True),
            lax.all_gather(layer_parts[6], "shard", axis=0, tiled=True),
            lax.all_gather(layer_parts[7], "shard", axis=0, tiled=True),
            lax.all_gather(layer_parts[8], "shard", axis=0, tiled=True),
            lax.all_gather(layer_parts[9], "shard", axis=0, tiled=True),
            lax.all_gather(layer_parts[10], "shard", axis=0, tiled=True),
            lax.all_gather(layer_parts[11], "shard", axis=0, tiled=True),
        )
        (
            scale_one,
            shift_one,
            qkv_full,
            qv_full,
            out_full,
            out_shift,
            scale_two,
            shift_two,
            up_full,
            up_shift,
            down_full,
            down_shift,
        ) = weights
        branch_grad = grad_stream.astype(jnp.bfloat16)
        grad_down_w = outer_sum(hidden, branch_grad)
        grad_down_b = jnp.sum(branch_grad.astype(jnp.float32), axis=0)
        hidden_grad = times_transposed(branch_grad, down_full)
        unused_value, gelu_pull = jax.vjp(partial(jax.nn.gelu, approximate=False), pre_act)
        pre_grad = gelu_pull(hidden_grad)[0].astype(jnp.bfloat16)
        grad_up_w = outer_sum(normed_two, pre_grad)
        grad_up_b = jnp.sum(pre_grad.astype(jnp.float32), axis=0)
        two_grad = times_transposed(pre_grad, up_full)
        middle_back, grad_scale_two, grad_shift_two = norm_backward(
            middle, inverse_two, scale_two, two_grad
        )
        middle_grad = grad_stream + middle_back
        out_grad = middle_grad.astype(jnp.bfloat16)
        grad_out_w = outer_sum(attended, out_grad)
        grad_out_b = jnp.sum(out_grad.astype(jnp.float32), axis=0)
        attended_grad = (
            times_transposed(out_grad, out_full)
            .astype(jnp.bfloat16)
            .reshape(image_count, local_len, model_width)
        )
        head_grad = lax.all_to_all(attended_grad, "seq", split_axis=2, concat_axis=1, tiled=True)
        heads_back = lax.map(attend_back, (received, log_total, head_grad))
        projected_grad = lax.all_to_all(
            heads_back, "seq", split_axis=1, concat_axis=3, tiled=True
        ).reshape(-1, 3 * model_width)
        grad_qkv_w = outer_sum(normed_one, projected_grad)
        column_sums = jnp.sum(projected_grad.astype(jnp.float32), axis=0)
        grad_qv_b = jnp.concatenate([column_sums[:model_width], column_sums[2 * model_width :]])
        one_grad = times_transposed(projected_grad, qkv_full)
        stream_back, grad_scale_one, grad_shift_one = norm_backward(
            stream_in, inverse_one, scale_one, one_grad
        )
        grad_stream = middle_grad + stream_back
        full_grads = (
            grad_scale_one,
            grad_shift_one,
            grad_qkv_w,
            grad_qv_b,
            grad_out_w,
            grad_out_b,
            grad_scale_two,
            grad_shift_two,
            grad_up_w,
            grad_up_b,
            grad_down_w,
            grad_down_b,
        )
        ordered = [reorder_rows(member, seq_count, shard_count) for member in full_grads]
        pieces = (
            lax.psum_scatter(ordered[0], ("seq", "shard"), scatter_dimension=0, tiled=True),
            lax.psum_scatter(ordered[1], ("seq", "shard"), scatter_dimension=0, tiled=True),
            lax.psum_scatter(ordered[2], ("seq", "shard"), scatter_dimension=0, tiled=True),
            lax.psum_scatter(ordered[3], ("seq", "shard"), scatter_dimension=0, tiled=True),
            lax.psum_scatter(ordered[4], ("seq", "shard"), scatter_dimension=0, tiled=True),
            lax.psum_scatter(ordered[5], ("seq", "shard"), scatter_dimension=0, tiled=True),
            lax.psum_scatter(ordered[6], ("seq", "shard"), scatter_dimension=0, tiled=True),
            lax.psum_scatter(ordered[7], ("seq", "shard"), scatter_dimension=0, tiled=True),
            lax.psum_scatter(ordered[8], ("seq", "shard"), scatter_dimension=0, tiled=True),
            lax.psum_scatter(ordered[9], ("seq", "shard"), scatter_dimension=0, tiled=True),
            lax.psum_scatter(ordered[10], ("seq", "shard"), scatter_dimension=0, tiled=True),
            lax.psum_scatter(ordered[11], ("seq", "shard"), scatter_dimension=0, tiled=True),
        )
        reduced = (
            lax.all_gather(pieces[0].astype(jnp.bfloat16), "seq", axis=0, tiled=True).astype(
                jnp.float32
            ),
            lax.all_gather(pieces[1].astype(jnp.bfloat16), "seq", axis=0, tiled=True).astype(
                jnp.float32
            ),
            lax.all_gather(pieces[2].astype(jnp.bfloat16), "seq", axis=0, tiled=True).astype(
                jnp.float32
            ),
            lax.all_gather(pieces[3].astype(jnp.bfloat16), "seq", axis=0, tiled=True).astype(
                jnp.float32
            ),
            lax.all_gather(pieces[4].astype(jnp.bfloat16), "seq", axis=0, tiled=True).astype(
                jnp.float32
            ),
            lax.all_gather(pieces[5].astype(jnp.bfloat16), "seq", axis=0, tiled=True).astype(
                jnp.float32
            ),
            lax.all_gather(pieces[6].astype(jnp.bfloat16), "seq", axis=0, tiled=True).astype(
                jnp.float32
            ),
            lax.all_gather(pieces[7].astype(jnp.bfloat16), "seq", axis=0, tiled=True).astype(
                jnp.float32
            ),
            lax.all_gather(pieces[8].astype(jnp.bfloat16), "seq", axis=0, tiled=True).astype(
                jnp.float32
            ),
            lax.all_gather(pieces[9].astype(jnp.bfloat16), "seq", axis=0, tiled=True).astype(
                jnp.float32
            ),
            lax.all_gather(pieces[10].astype(jnp.bfloat16), "seq", axis=0, tiled=True).astype(
                jnp.float32
            ),
            lax.all_gather(pieces[11].astype(jnp.bfloat16), "seq", axis=0, tiled=True).astype(
                jnp.float32
            ),
        )
        grad_layers.insert(0, reduced)
    input_grad = grad_stream.reshape(image_count, local_len, model_width)
    stacked = [
        jnp.stack([layer_grads[position] for layer_grads in grad_layers]) for position in range(12)
    ]
    return (
        results,
        input_grad,
        stacked[0],
        stacked[1],
        stacked[2],
        stacked[3],
        stacked[4],
        stacked[5],
        stacked[6],
        stacked[7],
        stacked[8],
        stacked[9],
        stacked[10],
        stacked[11],
    )


def solution(mesh):
    placed = (
        P("shard", "seq", None),
        P(None, "shard"),
        P(None, "shard"),
        P(None, "shard", None),
        P(None, "shard"),
        P(None, "shard", None),
        P(None, "shard"),
        P(None, "shard"),
        P(None, "shard"),
        P(None, "shard", None),
        P(None, "shard"),
        P(None, "shard", None),
        P(None, "shard"),
        P("shard", "seq", None),
    )
    return jax.shard_map(
        body,
        mesh=mesh,
        in_specs=placed,
        out_specs=(
            P("shard", "seq", None),
            P("shard", "seq", None),
            P(None, "shard"),
            P(None, "shard"),
            P(None, "shard", None),
            P(None, "shard"),
            P(None, "shard", None),
            P(None, "shard"),
            P(None, "shard"),
            P(None, "shard"),
            P(None, "shard", None),
            P(None, "shard"),
            P(None, "shard", None),
            P(None, "shard"),
        ),
        check_vma=False,
    )
```

profile of v0, /device:TPU:0, one launch (start us, length us, event | category | flops | bytes accessed | tf_op | source)
XLA Modules:
  0.0 3241.6 jit_solution(16049061169961415393)
XLA Ops:
  23.2 9.6 all-gather.15
  58.3 26.0 all-gather.53.cloned.1.call-done
  105.1 70.8 %all-to-all-done = bf16[1,288,3,1024]{1,2,0,3:T(4,128)(2,1)S(1)} async-done(((bf16[1,288,3,1024]{1,2,0,3:T(4,128)(2,1)}), bf16[1,288,3,1024]{1,2,0,3:T(4,128)(2,1)S(1)}, u32[]{:S(2)}, u32[]{:S(2)}) %all-to-all-start) | async-done | bytes 1769504 | tf_op jit(solution)/shard_map/all_to_all | solution.py:229
  183.5 66.4 %while.90 = (s32[]{:T(128)}, bf16[3,768,128]{2,1,0:T(8,128)(2,1)S(1)}, f32[3,2,768]{2,1,0:T(2,128)S(1)}, bf16[3,768,2,64]{1,3,2,0:T(8,128)(2,1)S(1)}, bf16[2304,...) while((s32[]{:T(128)}, bf16[3,768,128]{2,1,0:T(8,128)(2,1)S(1)}, ...), condition=%wide.region_5.0_spmd, body=%wide.region_2.5_spmd.sunk | while | flops 937916928 | bytes 44875872 | solution.py:76
  219.5 8.7 fusion.329
  257.2 14.1 reduce.3
  343.0 17.2 multiply_convert_fusion.3
  397.9 70.8 %all-to-all-done.2 = bf16[1,288,3,1024]{1,2,0,3:T(4,128)(2,1)S(1)} async-done(((bf16[1,288,3,1024]{1,2,0,3:T(4,128)(2,1)}), bf16[1,288,3,1024]{1,2,0,3:T(4,128)(2,1)S(1)}, u32[]{:S(2)}, u32[]{:S(2)}) %all-to-all-start.2) | async-done | bytes 1769504 | tf_op jit(solution)/shard_map/all_to_all | solution.py:229
  476.4 65.4 %while.91 = (s32[]{:T(128)}, bf16[3,768,128]{2,1,0:T(8,128)(2,1)S(1)}, f32[3,2,768]{2,1,0:T(2,128)S(1)}, bf16[3,768,2,64]{1,3,2,0:T(8,128)(2,1)S(1)}, bf16[2304,...) while((s32[]{:T(128)}, bf16[3,768,128]{2,1,0:T(8,128)(2,1)S(1)}, ...), condition=%wide.region_13.14_spmd, body=%wide.region_10.13_spmd.sunk | while | flops 937916928 | bytes 44875872 | solution.py:76
  542.4 9.9 copy.377
  552.3 13.9 reduce.4
  617.6 17.0 convert_reduce_fusion
  656.5 16.9 all-to-all-done.4
  694.9 103.4 %while.92 = (s32[]{:T(128)}, f32[2304,2,64]{0,2,1:T(8,128)S(1)}, f32[2304,2,64]{0,2,1:T(8,128)S(1)}, bf16[3,768,2,64]{1,3,2,0:T(8,128)(2,1)}, bf16[3,768,2,64]{1...) while((s32[]{:T(128)}, f32[2304,2,64]{0,2,1:T(8,128)S(1)}, ...), condition=%wide.region_20.21_spmd.clone, body=%wide.region_18.20_spmd.clone.sunk | while | flops 2309061120 | bytes 250521904 | solution.py:128
  706.2 9.2 multiply_convert_fusion.15
  740.7 9.2 multiply_convert_fusion.15
  775.1 9.2 multiply_convert_fusion.15
  806.4 57.5 %all_to_all.120 = bf16[1,2304,3,128]{3,2,0,1:T(4,128)(2,1)S(1)} all-to-all(bf16[1,2304,3,128]{3,2,0,1:T(4,128)(2,1)S(1)} %copy.292), channel_id=1, replica_groups=mesh['seq'=8,'shard'=4] {'seq'}, dimensions={1} | all-to-all | bytes 3538944 | tf_op jit(solution)/shard_map/all_to_all | solution.py:330
  874.3 12.8 convert_reduce_fusion.1
  915.6 9.8 convolution_bitcast_fusion.1
  925.3 10.9 copy.311
  956.1 106.8 %while.93 = (s32[]{:T(128)}, f32[2304,2,64]{0,2,1:T(8,128)S(1)}, f32[2304,2,64]{0,2,1:T(8,128)S(1)}, bf16[3,768,2,64]{1,3,2,0:T(8,128)(2,1)}, bf16[3,768,2,64]{1...) while((s32[]{:T(128)}, f32[2304,2,64]{0,2,1:T(8,128)S(1)}, ...), condition=%wide.region_27.28_spmd.clone, body=%wide.region_25.27_spmd.clone.sunk | while | flops 2309061120 | bytes 250521904 | solution.py:128
  958.9 9.1 multiply_reduce_fusion.24
  968.9 9.8 multiply_convert_fusion.16
  1004.5 9.4 multiply_convert_fusion.16
  1030.9 8.9 multiply_reduce_fusion.24
  1039.7 9.2 multiply_convert_fusion.16
  1071.1 68.2 %all_to_all.121 = bf16[1,2304,3,128]{3,2,0,1:T(4,128)(2,1)S(1)} all-to-all(bf16[1,2304,3,128]{3,2,0,1:T(4,128)(2,1)S(1)} %copy.301), channel_id=1, replica_groups=mesh['seq'=8,'shard'=4] {'seq'}, dimensions={1} | all-to-all | bytes 3538944 | tf_op jit(solution)/shard_map/all_to_all | solution.py:330
  1158.1 10.8 copy.309
  1196.0 11.4 fusion.151
  1243.9 78.9 %reduce-scatter.9.cloned.1.call-done = f32[32,3072]{1,0:T(8,128)} async-done(((f32[1024,3072]{1,0:T(8,128)}), f32[32,3072]{1,0:T(8,128)}) %reduce-scatter.9.cloned.1.call-update) | async-done | bytes 393232 | tf_op jit(solution)/shard_map/reduce_scatter | solution.py:359
  1324.5 357.3 %reduce-scatter.19.cloned.1.call-done = f32[32,4096]{1,0:T(8,128)} async-done(((f32[1024,4096]{1,0:T(8,128)}), f32[32,4096]{1,0:T(8,128)}) %reduce-scatter.19.cloned.1.call-update) | async-done | bytes 524304 | tf_op jit(solution)/shard_map/reduce_scatter | solution.py:365
  1683.7 359.4 %reduce-scatter.17.cloned.1.call-done = f32[32,4096]{1,0:T(8,128)} async-done(((f32[1024,4096]{1,0:T(8,128)}), f32[32,4096]{1,0:T(8,128)}) %reduce-scatter.17.cloned.1.call-update) | async-done | bytes 524304 | tf_op jit(solution)/shard_map/reduce_scatter | solution.py:365
  2058.3 346.2 %reduce-scatter.23.cloned.1.call-done = f32[128,1024]{1,0:T(8,128)} async-done(((f32[4096,1024]{1,0:T(8,128)}), f32[128,1024]{1,0:T(8,128)}) %reduce-scatter.23.cloned.1.call-update) | async-done | bytes 524304 | tf_op jit(solution)/shard_map/reduce_scatter | solution.py:367
  2406.6 15.8 fusion.208
  2434.3 44.0 %all-reduce.30 = (bf16[1024]{0:T(1024)(128)(2,1)S(1)}, bf16[1024]{0:T(1024)(128)(2,1)S(1)}, bf16[1024]{0:T(1024)(128)(2,1)S(1)}, bf16[1024]{0:T(1024)(128)(2,1)S...) all-reduce(f32[1024]{0:T(1024)} %reshape.459, ...), channel_id=27, replica_groups=mesh['seq'=8,'shard'=4] {'seq','shard'}, use_global_device_ids=true, to_apply=%region_33.34.clone | all-reduce | flops 24576 | bytes 147456
  2482.4 16.3 all-reduce.31
  2498.9 268.1 %reduce-scatter.21.cloned.1.call-done = f32[128,1024]{1,0:T(8,128)} async-done(((f32[4096,1024]{1,0:T(8,128)}), f32[128,1024]{1,0:T(8,128)}) %reduce-scatter.21.cloned.1.call-update) | async-done | bytes 524304 | tf_op jit(solution)/shard_map/reduce_scatter | solution.py:367
  2768.9 12.6 all-gather.25
  2799.0 114.1 %reduce-scatter.15.cloned.1.call-done = f32[32,1024]{1,0:T(8,128)} async-done(((f32[1024,1024]{1,0:T(8,128)}), f32[32,1024]{1,0:T(8,128)}) %reduce-scatter.15.cloned.1.call-update) | async-done | bytes 131088 | tf_op jit(solution)/shard_map/reduce_scatter | solution.py:361
  2914.1 15.0 all_gather.189
  2929.1 126.7 %reduce-scatter.13.cloned.1.call-done = f32[32,1024]{1,0:T(8,128)} async-done(((f32[1024,1024]{1,0:T(8,128)}), f32[32,1024]{1,0:T(8,128)}) %reduce-scatter.13.cloned.1.call-update) | async-done | bytes 131088 | tf_op jit(solution)/shard_map/reduce_scatter | solution.py:361
  3056.7 16.7 all_gather.188
  3082.1 25.1 all-gather.41.cloned.1.call-done
  3112.2 25.3 all-gather.47.cloned.1.call-done
  3137.5 30.1 all-gather.45.cloned.1.call-done
  3173.8 24.1 all-gather.51.cloned.1.call-done
  3197.8 30.2 all-gather.49.cloned.1.call-done
  (722 shorter events, 787.1 us)
Async XLA Ops:
  7.2 77.1 %all-gather.53.cloned.1.call-start = ((), (), s32[]{:S(2)}) async-start(), calls=%async_computation.30 | async-start | bytes 7864320 | tf_op jit(solution)/shard_map/all_gather | solution.py:190
  11.1 328.8 %all-gather.55.cloned.1.call-start = ((), (), s32[]{:S(2)}) async-start(), calls=%async_computation.31 | async-start | bytes 2621440 | tf_op jit(solution)/shard_map/all_gather | solution.py:192
  12.2 330.7 %all-gather.57.cloned.1.call-start = ((), (), s32[]{:S(2)}) async-start(), calls=%async_computation.32 | async-start | bytes 10485760 | tf_op jit(solution)/shard_map/all_gather | solution.py:196
  17.1 343.1 %all-gather.59.cloned.1.call-start = ((), (), s32[]{:S(2)}) async-start(), calls=%async_computation.33 | async-start | bytes 10485760 | tf_op jit(solution)/shard_map/all_gather | solution.py:198
  22.0 351.6 %all-gather.61.cloned.1.call-start = ((), (), s32[]{:S(2)}) async-start(), calls=%async_computation.34 | async-start | bytes 7864320 | tf_op jit(solution)/shard_map/all_gather | solution.py:190
  22.6 584.1 %all-gather.63.cloned.1.call-start = ((), (), s32[]{:S(2)}) async-start(), calls=%async_computation.35 | async-start | bytes 2621440 | tf_op jit(solution)/shard_map/all_gather | solution.py:192
  99.8 76.1 %all-to-all-start = ((bf16[1,288,3,1024]{1,2,0,3:T(4,128)(2,1)}), bf16[1,288,3,1024]{1,2,0,3:T(4,128)(2,1)S(1)}, u32[]{:S(2)}, u32[]{:S(2)}) async-start(bf16[1,288,3,1024]{1,2,0,3:T(4,128)(2,1)} %copy.266), calls=%async_computation | async-start | bytes 6291456 | tf_op jit(solution)/shard_map/all_to_all | solution.py:229
  104.4 505.3 %all-gather.65.cloned.1.call-start = ((), (), s32[]{:S(2)}) async-start(), calls=%async_computation.36 | async-start | bytes 10485760 | tf_op jit(solution)/shard_map/all_gather | solution.py:196
  249.9 89.6 %copy-start.4 = (bf16[2304,2,64]{0,2,1:T(8,128)(2,1)}, bf16[2304,2,64]{0,2,1:T(8,128)(2,1)S(1)}, u32[]{:S(2)}) copy-start(bf16[2304,2,64]{0,2,1:T(8,128)(2,1)S(1)} %get-tuple-element.962) | copy-start | bytes 1769476
  249.9 89.6 %copy-start.6 = (bf16[3,768,2,64]{1,3,2,0:T(8,128)(2,1)}, bf16[3,768,2,64]{1,3,2,0:T(8,128)(2,1)S(1)}, u32[]{:S(2)}) copy-start(bf16[3,768,2,64]{1,3,2,0:T(8,128)(2,1)S(1)} %get-tuple-element.976) | copy-start | bytes 1769476
  249.9 89.6 %copy-start.8 = (bf16[2304,2,64]{0,2,1:T(8,128)(2,1)}, bf16[2304,2,64]{0,2,1:T(8,128)(2,1)S(1)}, u32[]{:S(2)}) copy-start(bf16[2304,2,64]{0,2,1:T(8,128)(2,1)S(1)} %get-tuple-element.978) | copy-start | bytes 1769476
  250.0 45.5 %copy-start.94 = (bf16[2,1024]{1,0:T(2,128)(2,1)S(1)}, bf16[2,1024]{1,0:T(2,128)(2,1)}, u32[]{:S(2)}) copy-start(bf16[2,1024]{1,0:T(2,128)(2,1)} %param.32) | copy-start | bytes 12292
  250.0 54.9 %copy-start.105 = (bf16[2,256]{1,0:T(2,128)(2,1)S(1)}, bf16[2,256]{1,0:T(2,128)(2,1)}, u32[]{:S(2)}) copy-start(bf16[2,256]{1,0:T(2,128)(2,1)} %param.30) | copy-start | bytes 3076
  256.6 83.3 %copy-start.34 = (bf16[1,288,1024]{2,1,0:T(8,128)(2,1)S(1)}, bf16[1,288,1024]{2,1,0:T(8,128)(2,1)}, u32[]{:S(2)}) copy-start(bf16[1,288,1024]{2,1,0:T(8,128)(2,1)} %param.22) | copy-start | bytes 1769476
  273.8 63.3 %all-to-all-start.1 = ((bf16[8,2,18432]{2,1,0:T(2,128)(2,1)}), bf16[8,2,18432]{2,1,0:T(2,128)(2,1)}, u32[]{:S(2)}, u32[]{:S(2)}) async-start(bf16[8,2,18432]{2,1,0:T(2,128)(2,1)} %reshape.630), calls=%async_computation.1 | async-start | bytes 1179648 | tf_op jit(solution)/shard_map/all_to_all | solution.py:231
  392.6 76.1 %all-to-all-start.2 = ((bf16[1,288,3,1024]{1,2,0,3:T(4,128)(2,1)}), bf16[1,288,3,1024]{1,2,0,3:T(4,128)(2,1)S(1)}, u32[]{:S(2)}, u32[]{:S(2)}) async-start(bf16[1,288,3,1024]{1,2,0,3:T(4,128)(2,1)} %copy.276), calls=%async_computation.2 | async-start | bytes 6291456 | tf_op jit(solution)/shard_map/all_to_all | solution.py:229
  397.2 220.4 %all-gather.67.cloned.1.call-start = ((), (), s32[]{:S(2)}) async-start(), calls=%async_computation.37 | async-start | bytes 10485760 | tf_op jit(solution)/shard_map/all_gather | solution.py:198
  541.8 63.8 %copy-start.10 = (bf16[2304,2,64]{0,2,1:T(8,128)(2,1)}, bf16[2304,2,64]{0,2,1:T(8,128)(2,1)S(1)}, u32[]{:S(2)}) copy-start(bf16[2304,2,64]{0,2,1:T(8,128)(2,1)S(1)} %get-tuple-element.979) | copy-start | bytes 1769476
  541.9 44.9 %copy-start.108 = (bf16[1,256]{1,0:T(2,128)(2,1)S(1)}, bf16[1,256]{1,0:T(2,128)(2,1)}, u32[]{:S(2)}) copy-start(bf16[1,256]{1,0:T(2,128)(2,1)} %get-tuple-element.609) | copy-start | bytes 1540
  552.3 54.4 %copy-start.31 = (f32[288,1024]{1,0:T(8,128)S(1)}, f32[288,1024]{1,0:T(8,128)}, u32[]{:S(2)}) copy-start(f32[288,1024]{1,0:T(8,128)} %copy-done.30) | copy-start | bytes 3538948
  567.1 34.8 %all-to-all-start.3 = ((bf16[8,2,18432]{2,1,0:T(2,128)(2,1)}), bf16[8,2,18432]{2,1,0:T(2,128)(2,1)S(1)}, u32[]{:S(2)}, u32[]{:S(2)}) async-start(bf16[8,2,18432]{2,1,0:T(2,128)(2,1)} %reshape.632), calls=%async_computation.3 | async-start | bytes 1179648 | tf_op jit(solution)/shard_map/all_to_all | solution.py:231
  651.5 21.9 all-to-all-start.4
  907.0 29.3 all-to-all-start.6
  910.5 331.6 %reduce-scatter.11.cloned.1.call-start = ((), (), s32[]{:S(2)}) async-start(), calls=%async_computation.18 | async-start | bytes 12976128 | tf_op jit(solution)/shard_map/reduce_scatter | solution.py:359
  936.2 386.6 %reduce-scatter.9.cloned.1.call-start = ((), (), s32[]{:S(2)}) async-start(), calls=%async_computation.16 | async-start | bytes 12976128 | tf_op jit(solution)/shard_map/reduce_scatter | solution.py:359
  1169.0 512.9 %reduce-scatter.19.cloned.1.call-start = ((), (), s32[]{:S(2)}) async-start(), calls=%async_computation.24 | async-start | bytes 17301504 | tf_op jit(solution)/shard_map/reduce_scatter | solution.py:365
  1182.4 860.8 %reduce-scatter.17.cloned.1.call-start = ((), (), s32[]{:S(2)}) async-start(), calls=%async_computation.22 | async-start | bytes 17301504 | tf_op jit(solution)/shard_map/reduce_scatter | solution.py:365
  1195.9 1208.5 %reduce-scatter.23.cloned.1.call-start = ((), (), s32[]{:S(2)}) async-start(), calls=%async_computation.28 | async-start | bytes 17301504 | tf_op jit(solution)/shard_map/reduce_scatter | solution.py:367
  1219.0 1548.0 %reduce-scatter.21.cloned.1.call-start = ((), (), s32[]{:S(2)}) async-start(), calls=%async_computation.26 | async-start | bytes 17301504 | tf_op jit(solution)/shard_map/reduce_scatter | solution.py:367
  1232.0 1681.2 %reduce-scatter.15.cloned.1.call-start = ((), (), s32[]{:S(2)}) async-start(), calls=%async_computation.21 | async-start | bytes 4325376 | tf_op jit(solution)/shard_map/reduce_scatter | solution.py:361
  1237.1 1818.7 %reduce-scatter.13.cloned.1.call-start = ((), (), s32[]{:S(2)}) async-start(), calls=%async_computation.20 | async-start | bytes 4325376 | tf_op jit(solution)/shard_map/reduce_scatter | solution.py:361
  1241.9 803.0 %copy-start.106 = (bf16[1,256]{1,0:T(2,128)(2,1)S(1)}, bf16[1,256]{1,0:T(2,128)(2,1)}, u32[]{:S(2)}) copy-start(bf16[1,256]{1,0:T(2,128)(2,1)} %get-tuple-element.605) | copy-start | bytes 1540
  1242.0 810.8 %copy-start.112 = (u32[32]{0:T(128)S(1)}, u32[32]{0:T(128)}, u32[]{:S(2)}) copy-start(u32[32]{0:T(128)} %constant.213) | copy-start | bytes 388
  1242.0 812.7 %copy-start.87 = (f32[1024]{0:T(1024)S(1)}, f32[1024]{0:T(1024)}, u32[]{:S(2)}) copy-start(f32[1024]{0:T(1024)} %get-tuple-element.562) | copy-start | bytes 12292
  1242.0 813.4 %copy-start.99 = (f32[1024]{0:T(1024)S(1)}, f32[1024]{0:T(1024)}, u32[]{:S(2)}) copy-start(f32[1024]{0:T(1024)} %get-tuple-element.454) | copy-start | bytes 12292
  1242.0 814.2 %copy-start.98 = (f32[1024]{0:T(1024)S(1)}, f32[1024]{0:T(1024)}, u32[]{:S(2)}) copy-start(f32[1024]{0:T(1024)} %get-tuple-element.465) | copy-start | bytes 12292
  1242.0 814.9 %copy-start.92 = (f32[4096]{0:T(1024)S(1)}, f32[4096]{0:T(1024)}, u32[]{:S(2)}) copy-start(f32[4096]{0:T(1024)} %get-tuple-element.626) | copy-start | bytes 49156
  1242.0 815.5 %copy-start.86 = (f32[1024]{0:T(1024)S(1)}, f32[1024]{0:T(1024)}, u32[]{:S(2)}) copy-start(f32[1024]{0:T(1024)} %get-tuple-element.590) | copy-start | bytes 12292
  1242.0 1840.1 %all-gather.43.cloned.1.call-start = ((), (), s32[]{:S(2)}) async-start(), calls=%async_computation.19 | async-start | bytes 1769472 | tf_op jit(solution)/shard_map/all_gather | solution.py:377
  1243.8 1863.4 %all-gather.41.cloned.1.call-start = ((), (), s32[]{:S(2)}) async-start(), calls=%async_computation.17 | async-start | bytes 1769472 | tf_op jit(solution)/shard_map/all_gather | solution.py:377
  1324.5 1813.0 %all-gather.47.cloned.1.call-start = ((), (), s32[]{:S(2)}) async-start(), calls=%async_computation.25 | async-start | bytes 2359296 | tf_op jit(solution)/shard_map/all_gather | solution.py:395
  1683.6 1484.0 %all-gather.45.cloned.1.call-start = ((), (), s32[]{:S(2)}) async-start(), calls=%async_computation.23 | async-start | bytes 2359296 | tf_op jit(solution)/shard_map/all_gather | solution.py:395
  2044.9 1152.9 %all-gather.51.cloned.1.call-start = ((), (), s32[]{:S(2)}) async-start(), calls=%async_computation.29 | async-start | bytes 2359296 | tf_op jit(solution)/shard_map/all_gather | solution.py:401
  2406.3 821.8 %all-gather.49.cloned.1.call-start = ((), (), s32[]{:S(2)}) async-start(), calls=%async_computation.27 | async-start | bytes 2359296 | tf_op jit(solution)/shard_map/all_gather | solution.py:401
  2426.6 369.6 %copy-start.73 = (f32[1,1024]{1,0:T(1,128)S(1)}, f32[1,1024]{1,0:T(1,128)}, u32[]{:S(2)}) copy-start(f32[1,1024]{1,0:T(1,128)} %copy-done.71) | copy-start | bytes 12292
  2426.6 369.6 %copy-start.78 = (f32[288]{0:T(512)S(1)}, f32[288]{0:T(512)}, u32[]{:S(2)}) copy-start(f32[288]{0:T(512)} %copy-done.76) | copy-start | bytes 3460
  2426.6 369.6 %copy-start.83 = (f32[288]{0:T(512)S(1)}, f32[288]{0:T(512)}, u32[]{:S(2)}) copy-start(f32[288]{0:T(512)} %copy-done.81) | copy-start | bytes 3460
  2427.6 368.5 %copy-start.26 = (f32[288,1024]{1,0:T(8,128)S(1)}, f32[288,1024]{1,0:T(8,128)}, u32[]{:S(2)}) copy-start(f32[288,1024]{1,0:T(8,128)} %copy-done.24) | copy-start | bytes 3538948
  (117 other events, 1302.3 us)
Sparse Core Ops, SparseCore 0:
  11.2 73.0 all-gather.52
  86.7 35.3 all-gather.54
  124.5 87.5 all-gather.56
  213.8 87.7 all-gather.58
  303.3 70.2 all-gather.60
  375.3 35.2 all-gather.62
  413.0 87.5 all-gather.64
  502.5 87.8 all-gather.66
  936.3 163.9 reduce-scatter.10
  1169.1 153.6 reduce-scatter.8
  1325.1 356.6 reduce-scatter.18
  1684.0 359.1 reduce-scatter.16
  2045.4 359.0 reduce-scatter.22
  2406.6 360.2 reduce-scatter.20
  2769.7 143.4 reduce-scatter.14
  2915.9 139.8 reduce-scatter.12
  3057.3 24.7 all-gather.42
  3083.6 23.5 all-gather.40
  3108.9 28.6 all-gather.46
  3139.0 28.5 all-gather.44
  3169.2 28.5 all-gather.50
  3199.4 28.5 all-gather.48
where the time goes:
time: 3250 us; the launch traced here: 3240 us
  waiting for transfers between devices  1990 us (61%)
  matrix products  372 us (11%)
  blocking collectives  364 us (11%)
  local copies, waits for them, and re-layouts  266 us (8%)
  other arithmetic  207 us (6%)
    reduce_scatter x2, waiting for transfers between devices, body(): lax.psum_scatter(ordered[8], ('seq', 'shard'), scatter_dimension=0, tiled...  717 us
    reduce_scatter x2, waiting for transfers between devices, body(): lax.psum_scatter(ordered[10], ('seq', 'shard'), scatter_dimension=0, tile...  614 us
    reduce_scatter x2, waiting for transfers between devices, body(): lax.psum_scatter(ordered[4], ('seq', 'shard'), scatter_dimension=0, tiled...  241 us
    all_to_all x2, waiting for transfers between devices, body(): lax.all_to_all(packed, 'seq', split_axis=3, concat_axis=1, tiled=True)  142 us
    all_to_all x2, blocking collectives, body(): lax.all_to_all(heads_back, 'seq', split_axis=1, concat_axis=3, tiled=True)  126 us
    reduce_scatter x2, waiting for transfers between devices, body(): lax.psum_scatter(ordered[2], ('seq', 'shard'), scatter_dimension=0, tiled...  78.9 us
  transfers between devices with their start and end apart: 28, of which 18 were waited for; matrix products, arithmetic and copies ran while one was open for 19% of the time, Pallas kernels for 0%

commit v1 on v0

v1 whole, which is shorter than its diff:
```python
from functools import partial

import jax
import jax.numpy as jnp
from jax import lax
from jax.experimental import pallas as pl
from jax.experimental.pallas import tpu as pltpu
from jax.sharding import Mesh
from jax.sharding import PartitionSpec as P

HD = 64
SCALE = HD ** (-0.5)
F32 = jnp.float32
BF16 = jnp.bfloat16
VMEM_BYTES = 56 * 1024 * 1024


def matmul(left, right):
    return jnp.dot(left, right, preferred_element_type=F32)


def outer_sum(left, right):
    return lax.dot_general(left, right, (((0,), (0,)), ((), ())), preferred_element_type=F32)


def times_transposed(left, right):
    return lax.dot_general(left, right, (((1,), (1,)), ((), ())), preferred_element_type=F32)


def norm_forward(stream, scales, offset):
    average = jnp.mean(stream, axis=-1, keepdims=True)
    centered = stream - average
    variance = jnp.mean(centered * centered, axis=-1, keepdims=True)
    inverse = lax.rsqrt(variance + 1e-06)
    return (centered * inverse * scales + offset).astype(BF16), average, inverse


def norm_backward(stream, average, inverse, scales, upstream):
    unit_rows = (stream - average) * inverse
    grad_scale = jnp.sum(upstream * unit_rows, axis=0)
    grad_shift = jnp.sum(upstream, axis=0)
    scaled_grad = upstream * scales
    stream_grad = inverse * (
        scaled_grad
        - jnp.mean(scaled_grad, axis=-1, keepdims=True)
        - unit_rows * jnp.mean(scaled_grad * unit_rows, axis=-1, keepdims=True)
    )
    return stream_grad, grad_scale, grad_shift


def block_rows(tokens):
    for rows in (288, 192, 144, 96, 48, 16):
        if tokens % rows == 0:
            return rows
    return tokens


def lane_head(width):
    return lax.broadcasted_iota(jnp.int32, (1, width), 1) // HD


def attend_kernel(q_ref, k_ref, v_ref, o_ref, lse_ref, ext_ref):
    width = q_ref.shape[-1]
    seq = ext_ref.shape[0]

    @pl.when((pl.program_id(0) == 0) & (pl.program_id(1) == 0))
    def _():
        ext_ref[:, :width] = v_ref[:, 0].reshape(seq, width)
        ext_ref[:, width:] = jnp.ones((seq, ext_ref.shape[1] - width), BF16)

    queries = q_ref[0, 0] * SCALE
    keys = k_ref[:, 0].reshape(seq, width)
    lane = lane_head(width)
    mixed = jnp.zeros(queries.shape, F32)
    logs = jnp.zeros(queries.shape, F32)
    for head in range(width // HD):
        own = lane == head
        scores = times_transposed(jnp.where(own, queries, 0).astype(BF16), keys)
        row_max = jnp.max(scores, axis=1, keepdims=True)
        weight = jnp.exp(scores - row_max).astype(BF16)
        total = matmul(weight, ext_ref[...])
        row_total = total[:, width : 2 * width]
        mixed = jnp.where(own, total[:, :width] / row_total, mixed)
        logs = jnp.where(own, row_max + jnp.log(row_total), logs)
    o_ref[0] = mixed.astype(BF16)
    lse_ref[0] = logs


def attend(packed):
    parts, _, tokens, width = packed.shape
    rows = block_rows(tokens)
    return pl.pallas_call(
        attend_kernel,
        name="attend",
        grid=(parts, tokens // rows),
        in_specs=[
            pl.BlockSpec((1, 1, rows, width), lambda i, j: (i, 0, j, 0)),
            pl.BlockSpec((parts, 1, tokens, width), lambda i, j: (0, 1, 0, 0)),
            pl.BlockSpec((parts, 1, tokens, width), lambda i, j: (0, 2, 0, 0)),
        ],
        out_specs=[
            pl.BlockSpec((1, rows, width), lambda i, j: (i, j, 0)),
            pl.BlockSpec((1, rows, width), lambda i, j: (i, j, 0)),
        ],
        out_shape=[
            jax.ShapeDtypeStruct((parts, tokens, width), BF16),
            jax.ShapeDtypeStruct((parts, tokens, width), F32),
        ],
        scratch_shapes=[pltpu.VMEM((parts * tokens, 2 * width), BF16)],
        compiler_params=pltpu.CompilerParams(vmem_limit_bytes=VMEM_BYTES),
    )(packed, packed, packed)


def attend_back_kernel(q_ref, k_ref, v_ref, o_ref, g_ref, lse_ref, out_ref, dk_ref, dv_ref):
    part, block = pl.program_id(0), pl.program_id(1)
    parts, tokens = k_ref.shape[0], k_ref.shape[2]
    rows, width = q_ref.shape[2], q_ref.shape[3]
    seq = parts * tokens

    @pl.when((part == 0) & (block == 0))
    def _():
        dk_ref[...] = jnp.zeros_like(dk_ref)
        dv_ref[...] = jnp.zeros_like(dv_ref)

    queries = q_ref[0, 0] * SCALE
    grads = g_ref[0]
    keys = k_ref[:, 0].reshape(seq, width)
    values = v_ref[:, 0].reshape(seq, width)
    product = grads.astype(F32) * o_ref[0].astype(F32)
    logs = lse_ref[0]
    query_rows = queries.T
    grad_rows = grads.T
    lane = lane_head(width)
    dquery = jnp.zeros((rows, width), F32)
    for head in range(width // HD):
        own = lane == head
        span = slice(head * HD, (head + 1) * HD)
        scores = times_transposed(jnp.where(own, queries, 0).astype(BF16), keys)
        weight = jnp.exp(scores - logs[:, head * HD : head * HD + 1])
        inner = jnp.sum(jnp.where(own, product, 0.0), axis=1, keepdims=True)
        weight_grad = times_transposed(jnp.where(own, grads, 0).astype(BF16), values)
        score_grad = (weight * (weight_grad - inner)).astype(BF16)
        dv_ref[span, :] += matmul(grad_rows[span], weight.astype(BF16))
        dk_ref[span, :] += matmul(query_rows[span], score_grad)
        dquery = jnp.where(own, matmul(score_grad, keys), dquery)
    out_ref[part, 0, pl.ds(pl.multiple_of(block * rows, rows), rows), :] = (dquery * SCALE).astype(BF16)

    @pl.when((part == parts - 1) & (block == pl.num_programs(1) - 1))
    def _():
        out_ref[:, 1] = dk_ref[...].T.astype(BF16).reshape(parts, tokens, width)
        out_ref[:, 2] = dv_ref[...].T.astype(BF16).reshape(parts, tokens, width)


def attend_back(packed, mixed, grads, logs):
    parts, _, tokens, width = packed.shape
    rows = block_rows(tokens)
    own = pl.BlockSpec((1, rows, width), lambda i, j: (i, j, 0))
    return pl.pallas_call(
        attend_back_kernel,
        name="attend_back",
        grid=(parts, tokens // rows),
        in_specs=[
            pl.BlockSpec((1, 1, rows, width), lambda i, j: (i, 0, j, 0)),
            pl.BlockSpec((parts, 1, tokens, width), lambda i, j: (0, 1, 0, 0)),
            pl.BlockSpec((parts, 1, tokens, width), lambda i, j: (0, 2, 0, 0)),
            own,
            own,
            own,
        ],
        out_specs=pl.BlockSpec((parts, 3, tokens, width), lambda i, j: (0, 0, 0, 0)),
        out_shape=jax.ShapeDtypeStruct((parts, 3, tokens, width), BF16),
        scratch_shapes=[
            pltpu.VMEM((width, parts * tokens), F32),
            pltpu.VMEM((width, parts * tokens), F32),
        ],
        compiler_params=pltpu.CompilerParams(vmem_limit_bytes=VMEM_BYTES),
    )(packed, packed, packed, mixed, grads, logs)


def xor_order(pieces, index):
    count = pieces.shape[0]
    bit = 1
    while bit < count:
        split = pieces.reshape((count // (2 * bit), 2, bit) + pieces.shape[1:])
        pieces = jnp.where((index & bit) != 0, split[:, ::-1], split).reshape(pieces.shape)
        bit *= 2
    return pieces


def exchange(pieces):
    count = pieces.shape[0]
    return jnp.stack(
        [pieces[0]]
        + [lax.ppermute(pieces[k], "z", [(i, i ^ k) for i in range(count)]) for k in range(1, count)]
    )


def swap(value):
    return lax.ppermute(value, "c", [(0, 1), (1, 0)])


def with_partner(rows):
    return jnp.concatenate([rows, swap(rows)], axis=0)


def sum_with_partner(partial_rows):
    half = partial_rows.shape[0] // 2
    return partial_rows[:half] + swap(partial_rows[half:])


def add_rounded(left, right):
    return (left.astype(F32) + right.astype(F32)).astype(BF16)


def sum_over_z(values, index):
    count = lax.axis_size("z")
    bit = 1
    while bit < count:
        pairs = [(i, i ^ bit) for i in range(count)]
        upper = ((index & bit) != 0).astype(jnp.int32)
        halves = values.reshape((2, values.shape[0] // 2) + values.shape[1:])
        sent = lax.dynamic_index_in_dim(halves, 1 - upper, 0, keepdims=False)
        kept = lax.dynamic_index_in_dim(halves, upper, 0, keepdims=False)
        values = add_rounded(kept, lax.ppermute(sent, "z", pairs))
        bit *= 2
    while bit > 1:
        bit //= 2
        pairs = [(i, i ^ bit) for i in range(count)]
        upper = (index & bit) != 0
        other = lax.ppermute(values, "z", pairs)
        values = jnp.concatenate([jnp.where(upper, other, values), jnp.where(upper, values, other)], axis=0)
    return values


def gelu_parts(pre_act):
    cdf = 0.5 * (1.0 + lax.erf(pre_act * (0.5**0.5)))
    density = jnp.exp(-0.5 * pre_act * pre_act) * 0.3989422804014327
    return (pre_act * cdf).astype(BF16), (cdf + pre_act * density).astype(BF16)


def body(
    images,
    norm1_scale,
    norm1_shift,
    qkv_weight,
    qv_bias,
    out_weight,
    out_bias,
    norm2_scale,
    norm2_shift,
    up_weight,
    up_bias,
    down_weight,
    down_bias,
    cotangent,
):
    image_count, local_len, width = images.shape
    z_count = lax.axis_size("z")
    shards = lax.axis_size("shard")
    z_index, c_index, s_index = lax.axis_index("z"), lax.axis_index("c"), lax.axis_index("shard")
    layers = norm1_scale.shape[0]
    hidden_units = up_bias.shape[1] * shards
    half_width = width // 2
    group = half_width // z_count
    tokens = 2 * local_len

    def my_half(values, axis):
        return lax.dynamic_index_in_dim(values, c_index, axis, keepdims=False)

    def gather(values):
        return lax.all_gather(values, "shard", axis=0, tiled=True)

    vectors = (norm1_scale, norm1_shift, out_bias, norm2_scale, norm2_shift, down_bias, qv_bias, up_bias)
    sizes = [member.shape[1] for member in vectors]
    offsets = [sum(sizes[:place]) for place in range(len(sizes) + 1)]
    small = lax.all_gather(jnp.concatenate(vectors, axis=1), "shard", axis=0)

    def full_vector(layer, place):
        return small[:, layer, offsets[place] : offsets[place + 1]].reshape(-1).astype(F32)

    weights = []
    for layer in range(layers):
        qkv_part = my_half(qkv_weight[layer].reshape(-1, 3, shards, 2, half_width // shards), 3)
        qkv_part = jnp.swapaxes(qkv_part.reshape(-1, 3, z_count, group), 1, 2)
        up_part = my_half(up_weight[layer].reshape(-1, shards, 2, hidden_units // 2 // shards), 2)
        weights.append(
            (
                gather(qkv_part.reshape(-1, 3 * half_width)),
                gather(my_half(out_weight[layer].reshape(2, -1, width), 0)),
                gather(up_part.reshape(-1, hidden_units // 2)),
                gather(my_half(down_weight[layer].reshape(2, -1, width), 0)),
            )
        )

    stream = images.astype(F32).reshape(-1, width)
    saved = []
    for layer in range(layers):
        qkv_full, out_full, up_full, down_full = weights[layer]
        scale_one, shift_one, out_shift, scale_two, shift_two, down_shift, qv_full, up_all = [
            full_vector(layer, place) for place in range(8)
        ]
        qv_halves = my_half(qv_full.reshape(2, shards, 2, half_width // shards), 2).reshape(2, z_count, group)
        qkv_shift = jnp.stack([qv_halves[0], jnp.zeros_like(qv_halves[0]), qv_halves[1]], axis=1).reshape(-1)
        up_shift = my_half(up_all.reshape(shards, 2, -1), 1).reshape(-1)

        normed_own, average_one, inverse_one = norm_forward(stream, scale_one, shift_one)
        normed_one = with_partner(normed_own)
        projected = (matmul(normed_one, qkv_full) + qkv_shift).astype(BF16)
        pieces = projected.reshape(tokens, z_count, 3, group).transpose(1, 2, 0, 3)
        packed = exchange(xor_order(pieces, z_index))
        mixed, logs = attend(packed)
        attended = xor_order(exchange(mixed), z_index).transpose(1, 0, 2).reshape(tokens, half_width)
        middle = stream + sum_with_partner(matmul(attended, out_full)) + out_shift
        two_own, average_two, inverse_two = norm_forward(middle, scale_two, shift_two)
        normed_two = with_partner(two_own)
        pre_act = matmul(normed_two, up_full) + up_shift
        hidden, slope = gelu_parts(pre_act)
        saved.append(
            (
                stream,
                average_one,
                inverse_one,
                normed_one,
                packed,
                mixed,
                logs,
                attended,
                middle,
                average_two,
                inverse_two,
                normed_two,
                hidden,
                slope,
                scale_one,
                scale_two,
            )
        )
        stream = middle + sum_with_partner(matmul(hidden, down_full)) + down_shift
    results = stream.astype(BF16).reshape(image_count, local_len, width)

    def reduce_weight(gradient):
        piece = lax.psum_scatter(gradient.astype(BF16), "shard", scatter_dimension=0, tiled=True)
        piece = sum_over_z(piece, z_index)
        other = swap(piece)
        first = jnp.where(c_index == 0, piece, other)
        second = jnp.where(c_index == 0, other, piece)
        return first, second

    grad_stream = cotangent.astype(F32).reshape(-1, width)
    weight_grads = [None] * layers
    small_grads = [None] * layers
    for layer in reversed(range(layers)):
        (
            stream_in,
            average_one,
            inverse_one,
            normed_one,
            packed,
            mixed,
            logs,
            attended,
            middle,
            average_two,
            inverse_two,
            normed_two,
            hidden,
            slope,
            scale_one,
            scale_two,
        ) = saved[layer]
        qkv_full, out_full, up_full, down_full = weights[layer]
        branch_own = grad_stream.astype(BF16)
        branch_grad = with_partner(branch_own)
        grad_down_b = jnp.sum(branch_own.astype(F32), axis=0)
        pre_grad = (times_transposed(branch_grad, down_full) * slope.astype(F32)).astype(BF16)
        two_grad = sum_with_partner(times_transposed(pre_grad, up_full))
        grad_down = reduce_weight(outer_sum(hidden, branch_grad))
        grad_up = reduce_weight(outer_sum(normed_two, pre_grad))
        grad_up_b = jnp.sum(pre_grad.astype(F32), axis=0)
        middle_back, grad_scale_two, grad_shift_two = norm_backward(
            middle, average_two, inverse_two, scale_two, two_grad
        )
        middle_grad = grad_stream + middle_back
        out_own = middle_grad.astype(BF16)
        out_grad = with_partner(out_own)
        grad_out_b = jnp.sum(out_own.astype(F32), axis=0)
        attended_grad = times_transposed(out_grad, out_full).astype(BF16)
        grad_pieces = attended_grad.reshape(tokens, z_count, group).transpose(1, 0, 2)
        head_grad = exchange(xor_order(grad_pieces, z_index))
        grad_out = reduce_weight(outer_sum(attended, out_grad))
        heads_back = attend_back(packed, mixed, head_grad, logs)
        projected_grad = xor_order(exchange(heads_back), z_index).transpose(2, 0, 1, 3)
        projected_grad = projected_grad.reshape(tokens, 3 * half_width)
        one_grad = sum_with_partner(times_transposed(projected_grad, qkv_full))
        grad_qkv = reduce_weight(outer_sum(normed_one, projected_grad))
        column_sums = jnp.sum(projected_grad.astype(F32), axis=0).reshape(z_count, 3, group)
        grad_qv_b = jnp.stack([column_sums[:, 0], column_sums[:, 2]])
        stream_back, grad_scale_one, grad_shift_one = norm_backward(
            stream_in, average_one, inverse_one, scale_one, one_grad
        )
        grad_stream = middle_grad + stream_back

        def spread(values, lead):
            values = values.reshape(lead, shards, 1, -1)
            nothing = jnp.zeros_like(values)
            halves = jnp.concatenate(
                [
                    jnp.where(c_index == 0, values, nothing),
                    jnp.where(c_index == 0, nothing, values),
                ],
                axis=2,
            )
            return halves.reshape(shards, -1)

        small_grads[layer] = jnp.concatenate(
            [
                member.reshape(shards, -1)
                for member in (
                    grad_scale_one,
                    grad_shift_one,
                    grad_out_b,
                    grad_scale_two,
                    grad_shift_two,
                    grad_down_b,
                    spread(grad_qv_b, 2),
                    spread(grad_up_b, 1),
                )
            ],
            axis=1,
        )
        weight_grads[layer] = (grad_qkv, grad_out, grad_up, grad_down)

    small_sums = lax.psum(jnp.stack(small_grads, axis=1), ("z", "c", "shard"))
    small_sums = lax.dynamic_index_in_dim(small_sums, s_index, 0, keepdims=False)
    vector_grads = [small_sums[:, offsets[place] : offsets[place + 1]] for place in range(8)]

    def join_qkv(pair):
        halves = jnp.stack([part.reshape(-1, z_count, 3, group) for part in pair], axis=0)
        halves = halves.transpose(1, 3, 0, 2, 4).reshape(-1, 3, 2, shards, half_width // shards)
        return jnp.swapaxes(halves, 2, 3).reshape(-1, 3 * width).astype(F32)

    def join_up(pair):
        halves = jnp.stack([part.reshape(-1, shards, hidden_units // 2 // shards) for part in pair], axis=2)
        return halves.reshape(-1, hidden_units).astype(F32)

    def join_rows(pair):
        return jnp.concatenate(pair, axis=0).astype(F32)

    grad_qkv = jnp.stack([join_qkv(member[0]) for member in weight_grads])
    grad_out = jnp.stack([join_rows(member[1]) for member in weight_grads])
    grad_up = jnp.stack([join_up(member[2]) for member in weight_grads])
    grad_down = jnp.stack([join_rows(member[3]) for member in weight_grads])
    input_grad = grad_stream.reshape(image_count, local_len, width)
    return (
        results,
        input_grad,
        vector_grads[0],
        vector_grads[1],
        grad_qkv,
        vector_grads[6],
        grad_out,
        vector_grads[2],
        vector_grads[3],
        vector_grads[4],
        grad_up,
        vector_grads[7],
        grad_down,
        vector_grads[5],
    )


def solution(mesh):
    seq, shards = mesh.devices.shape
    cores = Mesh(mesh.devices.reshape(seq // 2, 2, shards), ("z", "c", "shard"))
    rows = P("shard", ("z", "c"), None)
    vector = P(None, "shard")
    matrix = P(None, "shard", None)
    parameters = (
        vector,
        vector,
        matrix,
        vector,
        matrix,
        vector,
        vector,
        vector,
        matrix,
        vector,
        matrix,
        vector,
    )
    return jax.shard_map(
        body,
        mesh=cores,
        in_specs=(rows,) + parameters + (rows,),
        out_specs=(rows, rows) + parameters,
        check_vma=False,
    )
```

time: 3250 us -> 1290 us (0.40)
  waiting for transfers between devices: 1990 us -> 739 us
  blocking collectives: 364 us -> 9.62 us
  matrix products: 372 us -> 116 us
  local copies, waits for them, and re-layouts: 266 us -> 131 us
  other arithmetic: 207 us -> 87.6 us
  Pallas kernels: 0 us -> 109 us
  starting transfers between devices: 27.2 us -> 72.9 us
    reduce_scatter x8, waiting for transfers between devices: 1650 us -> 177 us  [reduce_weight(): lax.psum_scatter(gradient.astype(BF16), 'shard', scatter_dimension=0, til...]
    ppermute x0 -> x80, waiting for transfers between devices: none -> 402 us  [the longest x24 182 us: exchange(): lax.ppermute(pieces[k], 'z', [(i, i ^ k) for i in range(count)])]
    dot_general x50 -> x8, matrix products: 283 us -> 36.5 us  [matmul(): return jnp.dot(left, right, preferred_element_type=F32)]
    all_gather x20 -> x1, blocking collectives: 178 us -> 9.62 us  [body(): small = lax.all_gather(jnp.concatenate(vectors, axis=1), 'shard', axis=0)]
    all_to_all x6 -> x0, waiting for transfers between devices: 158 us -> none  [the longest x2 142 us: body(): lax.all_to_all(packed, 'seq', split_axis=3, concat_axis=1, tiled=True)]
    all_to_all x2 -> x0, blocking collectives: 126 us -> none  [body(): lax.all_to_all(heads_back, 'seq', split_axis=1, concat_axis=3, tiled=True)]
    pallas_call x0 -> x4, Pallas kernels: none -> 109 us  [the longest x2 65.4 us: attend_back(): pl.pallas_call(attend_back_kernel, name='attend_back', grid=(parts, token...]
    all_gather x14 -> x8, waiting for transfers between devices: 175 us -> 96.6 us  [gather(): return lax.all_gather(values, 'shard', axis=0, tiled=True)]
  transfers between devices with their start and end apart: 28 -> 97, of which waited for: 18 -> 59; matrix products, arithmetic and copies ran while one was open for 19% -> 20% of each run, Pallas kernels for 0% -> 6%
where the time goes in v1:
time: 1290 us; the launch traced here: 1280 us
  waiting for transfers between devices  739 us (57%)
  local copies, waits for them, and re-layouts  131 us (10%)
  matrix products  116 us (9%)
  Pallas kernels  109 us (8%)
  other arithmetic  87.6 us (7%)
  starting transfers between devices  72.9 us (6%)
  between operations  16.7 us (1%)
    ppermute x24, waiting for transfers between devices, exchange(): lax.ppermute(pieces[k], 'z', [(i, i ^ k) for i in range(count)])  182 us
    reduce_scatter x8, waiting for transfers between devices, reduce_weight(): lax.psum_scatter(gradient.astype(BF16), 'shard', scatter_dimension=0, til...  177 us
    ppermute x16, waiting for transfers between devices, sum_over_z(): other = lax.ppermute(values, 'z', pairs)  108 us
    all_gather x8, waiting for transfers between devices, gather(): return lax.all_gather(values, 'shard', axis=0, tiled=True)  96.6 us
    ppermute x16, waiting for transfers between devices, sum_over_z(): values = add_rounded(kept, lax.ppermute(sent, 'z', pairs))  91.3 us
    pallas_call x2, Pallas kernels, attend_back(): pl.pallas_call(attend_back_kernel, name='attend_back', grid=(parts, token...  65.4 us
    psum x1, waiting for transfers between devices, body(): small_sums = lax.psum(jnp.stack(small_grads, axis=1), ('z', 'c', 'shard'))  62.4 us
    dot_general x8, matrix products, outer_sum(): lax.dot_general(left, right, (((0,), (0,)), ((), ())), preferred_element_...  45.9 us
  transfers between devices with their start and end apart: 97, of which 59 were waited for; matrix products, arithmetic and copies ran while one was open for 20% of the time, Pallas kernels for 6%

profile of v1, /device:TPU:0, one launch (start us, length us, event | category | flops | bytes accessed | tf_op | source)
XLA Modules:
  0.0 1280.5 jit_solution(15835765627928791530)
XLA Ops:
  33.5 9.6 all-gather.5
  47.5 14.8 %all-gather.15.cloned.1.call-done = bf16[1024,1536]{0,1:T(8,128)(2,1)} async-done(((bf16[256,1536]{0,1:T(8,128)(2,1)}), bf16[1024,1536]{0,1:T(8,128)(2,1)}) %all-gather.15.cloned.1.call-update) | async-done | bytes 3145744 | tf_op jit(solution)/shard_map/all_gather | solution.py:271
  76.9 10.6 collective-permute-done.3
  87.5 26.3 %collective-permute-done.2 = bf16[3,576,128]{2,1,0:T(8,128)(2,1)S(1)} collective-permute-done((bf16[3,576,128]{2,1,0:T(8,128)(2,1)S(1)}, bf16[3,576,128]{2,1,0:T(8,128)(2,1)S(1)}, u32[]{:S(2)}, u32[]{:S(2)}) %collective-permute-start.2) | collective-permute-done | bytes 442400 | tf_op jit(solution)/shard_map/ppermute | solution.py:194
  115.2 21.8 %attend.2 = (bf16[4,576,128]{2,1,0:T(8,128)(2,1)}, f32[4,576,128]{2,1,0:T(8,128)}) custom-call(bf16[4,3,576,128]{3,2,1,0:T(8,128)(2,1)} %pad_maximum_fusion.2.q_ref.k_ref.v_ref, bf16[4,3,576,128]{3,2,1,0:T(8,128)(2,1)} %pad_maximum_fusion.2.q_ref.k_ref.v_ref, bf16[4,3,576,128]{3,2,1,0:T(8,128)(2,1)} %pad_maximum_fusion.2.q_ref.k_ref.v_ref), custom_call_target="tpu_custom_call" | custom-call | tf_op jit(solution)/shard_map/attend/pallas_call | solution.py:92
  169.2 7.9 multiply_convert_fusion.3
  177.1 22.5 %all-gather.25.cloned.1.call-done = bf16[1,2048,1024]{2,1,0:T(8,128)(2,1)} async-done(((bf16[1,512,1024]{2,1,0:T(8,128)(2,1)}), bf16[1,2048,1024]{2,1,0:T(8,128)(2,1)}) %all-gather.25.cloned.1.call-update) | async-done | bytes 4194320 | tf_op jit(solution)/shard_map/all_gather | solution.py:271
  211.2 33.9 %all-gather.19.cloned.1.call-done = bf16[1024,1536]{0,1:T(8,128)(2,1)} async-done(((bf16[256,1536]{0,1:T(8,128)(2,1)}), bf16[1024,1536]{0,1:T(8,128)(2,1)}) %all-gather.19.cloned.1.call-update) | async-done | bytes 3145744 | tf_op jit(solution)/shard_map/all_gather | solution.py:271
  266.2 10.6 collective-permute-done.13
  276.8 26.3 %collective-permute-done.12 = bf16[3,576,128]{2,1,0:T(8,128)(2,1)S(1)} collective-permute-done((bf16[3,576,128]{2,1,0:T(8,128)(2,1)S(1)}, bf16[3,576,128]{2,1,0:T(8,128)(2,1)S(1)}, u32[]{:S(2)}, u32[]{:S(2)}) %collective-permute-start.12) | collective-permute-done | bytes 442400 | tf_op jit(solution)/shard_map/ppermute | solution.py:194
  304.5 21.8 %attend.3 = (bf16[4,576,128]{2,1,0:T(8,128)(2,1)}, f32[4,576,128]{2,1,0:T(8,128)}) custom-call(bf16[4,3,576,128]{3,2,1,0:T(8,128)(2,1)} %pad_maximum_fusion.3.q_ref.k_ref.v_ref, bf16[4,3,576,128]{3,2,1,0:T(8,128)(2,1)} %pad_maximum_fusion.3.q_ref.k_ref.v_ref, bf16[4,3,576,128]{3,2,1,0:T(8,128)(2,1)} %pad_maximum_fusion.3.q_ref.k_ref.v_ref), custom_call_target="tpu_custom_call" | custom-call | tf_op jit(solution)/shard_map/attend/pallas_call | solution.py:92
  351.5 6.9 multiply_convert_fusion.2
  358.4 25.3 %all-gather.29.cloned.1.call-done = bf16[1,2048,1024]{2,1,0:T(8,128)(2,1)} async-done(((bf16[1,512,1024]{2,1,0:T(8,128)(2,1)}), bf16[1,2048,1024]{2,1,0:T(8,128)(2,1)}) %all-gather.29.cloned.1.call-update) | async-done | bytes 4194320 | tf_op jit(solution)/shard_map/all_gather | solution.py:271
  383.7 7.8 convert_reduce_fusion
  417.5 7.7 collective-permute-done.24
  426.1 32.8 %attend_back.2 = bf16[4,3,576,128]{3,2,1,0:T(8,128)(2,1)} custom-call(bf16[4,3,576,128]{3,2,1,0:T(8,128)(2,1)} %pad_maximum_fusion.3.q_ref.k_ref.v_ref, bf16[4,3,576,128]{3,2,1,0:T(8,128)(2,1)} %pad_maximum_fusion.3.q_ref.k_ref.v_ref, bf16[4,3,576,128]{3,2,1,0:T(8,128)(2,1)} %pad_maximum_fusion.3.q_ref.k_ref.v_ref, ...), custom_call_target="tpu_custom_call" | custom-call | tf_op jit(solution)/shard_map/attend_back/pallas_call | solution.py:158
  464.9 10.6 collective-permute-done.28
  475.5 23.8 %collective-permute-done.27 = bf16[3,576,128]{2,1,0:T(8,128)(2,1)S(1)} collective-permute-done((bf16[3,576,128]{2,1,0:T(8,128)(2,1)S(1)}, bf16[3,576,128]{2,1,0:T(8,128)(2,1)S(1)}, u32[]{:S(2)}, u32[]{:S(2)}) %collective-permute-start.27) | collective-permute-done | bytes 442400 | tf_op jit(solution)/shard_map/ppermute | solution.py:194
  517.3 7.8 convert_reduce_fusion.1
  559.7 32.6 %attend_back.3 = bf16[4,3,576,128]{3,2,1,0:T(8,128)(2,1)} custom-call(bf16[4,3,576,128]{3,2,1,0:T(8,128)(2,1)} %pad_maximum_fusion.2.q_ref.k_ref.v_ref, bf16[4,3,576,128]{3,2,1,0:T(8,128)(2,1)} %pad_maximum_fusion.2.q_ref.k_ref.v_ref, bf16[4,3,576,128]{3,2,1,0:T(8,128)(2,1)} %pad_maximum_fusion.2.q_ref.k_ref.v_ref, ...), custom_call_target="tpu_custom_call" | custom-call | tf_op jit(solution)/shard_map/attend_back/pallas_call | solution.py:158
  599.2 10.8 collective-permute-done.38
  610.1 24.2 %collective-permute-done.37 = bf16[3,576,128]{2,1,0:T(8,128)(2,1)} collective-permute-done((bf16[3,576,128]{2,1,0:T(8,128)(2,1)}, bf16[3,576,128]{2,1,0:T(8,128)(2,1)}, u32[]{:S(2)}, u32[]{:S(2)}) %collective-permute-start.37) | collective-permute-done | bytes 442400 | tf_op jit(solution)/shard_map/ppermute | solution.py:194
  658.5 7.5 convolution_convert_fusion.4
  666.1 7.5 convolution_convert_fusion.2
  681.1 6.7 convolution_convert_fusion.5
  689.0 6.8 convolution_convert_fusion.3
  697.0 5.9 collective-permute-done.55
  743.7 62.4 %all-reduce.2.cloned.1.call-done = f32[4,2,3072]{2,1,0:T(2,128)} async-done(((f32[4,2,3072]{2,1,0:T(2,128)}), f32[4,2,3072]{2,1,0:T(2,128)}) %all-reduce.2.cloned.1.call-update) | async-done | bytes 98320 | tf_op jit(solution)/shard_map/psum | solution.py:433
  814.5 48.6 %reduce-scatter.19.cloned.1.call-done = bf16[256,2048]{1,0:T(8,128)(2,1)} async-done(((bf16[1024,2048]{1,0:T(8,128)(2,1)}), bf16[256,2048]{1,0:T(8,128)(2,1)}) %reduce-scatter.19.cloned.1.call-update) | async-done | bytes 1048592 | tf_op jit(solution)/shard_map/reduce_scatter | solution.py:342
  866.5 53.2 %reduce-scatter.23.cloned.1.call-done = bf16[512,1024]{1,0:T(8,128)(2,1)} async-done(((bf16[2048,1024]{1,0:T(8,128)(2,1)}), bf16[512,1024]{1,0:T(8,128)(2,1)}) %reduce-scatter.23.cloned.1.call-update) | async-done | bytes 1048592 | tf_op jit(solution)/shard_map/reduce_scatter | solution.py:342
  924.7 41.8 %reduce-scatter.11.cloned.1.call-done = bf16[256,1536]{1,0:T(8,128)(2,1)} async-done(((bf16[1024,1536]{1,0:T(8,128)(2,1)}), bf16[256,1536]{1,0:T(8,128)(2,1)}) %reduce-scatter.11.cloned.1.call-update) | async-done | bytes 786448 | tf_op jit(solution)/shard_map/reduce_scatter | solution.py:342
  974.6 10.8 collective-permute-done.45
  986.0 12.7 collective-permute-done.66
  998.9 12.5 collective-permute-done.46
  1014.5 16.5 %collective-permute-done.47 = bf16[64,1536]{1,0:T(8,128)(2,1)S(1)} collective-permute-done((bf16[64,1536]{1,0:T(8,128)(2,1)S(1)}, bf16[64,1536]{1,0:T(8,128)(2,1)S(1)}, u32[]{:S(2)}, u32[]{:S(2)}) %collective-permute-start.47) | collective-permute-done | bytes 196640 | tf_op jit(solution)/shard_map/ppermute | solution.py:230
  1035.5 8.2 collective-permute-done.48
  1044.0 10.9 collective-permute-done.68
  1056.3 9.8 collective-permute-done.78
  1091.6 33.6 %reduce-scatter.9.cloned.1.call-done = bf16[256,1536]{1,0:T(8,128)(2,1)} async-done(((bf16[1024,1536]{1,0:T(8,128)(2,1)}), bf16[256,1536]{1,0:T(8,128)(2,1)}) %reduce-scatter.9.cloned.1.call-update) | async-done | bytes 786448 | tf_op jit(solution)/shard_map/reduce_scatter | solution.py:342
  1133.4 10.8 collective-permute-done.40
  1144.9 12.7 collective-permute-done.61
  1157.7 12.5 collective-permute-done.41
  1173.4 16.5 %collective-permute-done.42 = bf16[64,1536]{1,0:T(8,128)(2,1)S(1)} collective-permute-done((bf16[64,1536]{1,0:T(8,128)(2,1)S(1)}, bf16[64,1536]{1,0:T(8,128)(2,1)S(1)}, u32[]{:S(2)}, u32[]{:S(2)}) %collective-permute-start.42) | collective-permute-done | bytes 196640 | tf_op jit(solution)/shard_map/ppermute | solution.py:230
  1194.3 8.2 collective-permute-done.43
  1202.9 11.0 collective-permute-done.63
  1215.3 9.6 collective-permute-done.73
  1238.4 6.6 copy.178
  1258.8 8.9 copy.179
  (656 shorter events, 415.2 us)
Async XLA Ops:
  7.2 55.1 %all-gather.15.cloned.1.call-start = ((), (), s32[]{:S(2)}) async-start(), calls=%async_computation.8 | async-start | bytes 3932160 | tf_op jit(solution)/shard_map/all_gather | solution.py:271
  15.5 137.3 %all-gather.23.cloned.1.call-start = ((), (), s32[]{:S(2)}) async-start(), calls=%async_computation.21 | async-start | bytes 1310720 | tf_op jit(solution)/shard_map/all_gather | solution.py:271
  17.7 150.0 %all-gather.17.cloned.1.call-start = ((), (), s32[]{:S(2)}) async-start(), calls=%async_computation.9 | async-start | bytes 5242880 | tf_op jit(solution)/shard_map/all_gather | solution.py:271
  26.5 173.1 %all-gather.25.cloned.1.call-start = ((), (), s32[]{:S(2)}) async-start(), calls=%async_computation.22 | async-start | bytes 5242880 | tf_op jit(solution)/shard_map/all_gather | solution.py:271
  31.9 213.3 %all-gather.19.cloned.1.call-start = ((), (), s32[]{:S(2)}) async-start(), calls=%async_computation.10 | async-start | bytes 3932160 | tf_op jit(solution)/shard_map/all_gather | solution.py:271
  33.2 308.9 %all-gather.27.cloned.1.call-start = ((), (), s32[]{:S(2)}) async-start(), calls=%async_computation.23 | async-start | bytes 1310720 | tf_op jit(solution)/shard_map/all_gather | solution.py:271
  75.9 37.9 %collective-permute-start.2 = (bf16[3,576,128]{2,1,0:T(8,128)(2,1)S(1)}, bf16[3,576,128]{2,1,0:T(8,128)(2,1)S(1)}, u32[]{:S(2)}, u32[]{:S(2)}) collective-permute-start(bf16[3,576,128]{2,1,0:T(8,128)(2,1)S(1)} %get-tuple-element.129), channel_id=1, source_target_pairs={{0,16},{8,24},{16,0},{24,8},{1,17},{9,25},{17,1},{25,9},{2,18},{10... | collective-permute-start | bytes 1327112 | tf_op jit(solution)/shard_map/ppermute | solution.py:194
  75.9 37.9 %collective-permute-start.1 = (bf16[3,576,128]{2,1,0:T(8,128)(2,1)S(1)}, bf16[3,576,128]{2,1,0:T(8,128)(2,1)S(1)}, u32[]{:S(2)}, u32[]{:S(2)}) collective-permute-start(bf16[3,576,128]{2,1,0:T(8,128)(2,1)S(1)} %get-tuple-element.130), channel_id=1, source_target_pairs={{0,8},{8,0},{16,24},{24,16},{1,9},{9,1},{17,25},{25,17},{2,10},{10... | collective-permute-start | bytes 1327112 | tf_op jit(solution)/shard_map/ppermute | solution.py:194
  143.4 207.6 %all-gather.21.cloned.1.call-start = ((), (), s32[]{:S(2)}) async-start(), calls=%async_computation.11 | async-start | bytes 5242880 | tf_op jit(solution)/shard_map/all_gather | solution.py:271
  163.2 220.5 %all-gather.29.cloned.1.call-start = ((), (), s32[]{:S(2)}) async-start(), calls=%async_computation.24 | async-start | bytes 5242880 | tf_op jit(solution)/shard_map/all_gather | solution.py:271
  208.7 36.4 %collective-permute-start.10 = (bf16[288,1024]{1,0:T(8,128)(2,1)S(1)}, bf16[288,1024]{1,0:T(8,128)(2,1)}, u32[]{:S(2)}, u32[]{:S(2)}) collective-permute-start(bf16[288,1024]{1,0:T(8,128)(2,1)S(1)} %add_convert_fusion.3), channel_id=1, source_target_pairs={{0,4},{4,0},{1,5},{5,1},{2,6},{6,2},{3,7},{7,3},{8,12},{12,8},{9,1... | collective-permute-start | bytes 1769480 | tf_op jit(solution)/shard_map/ppermute | solution.py:199
  211.2 484.7 %reduce-scatter.15.cloned.1.call-start = ((), (), s32[]{:S(2)}) async-start(), calls=%async_computation.16 | async-start | bytes 1310720 | tf_op jit(solution)/shard_map/reduce_scatter | solution.py:342
  265.1 38.0 %collective-permute-start.12 = (bf16[3,576,128]{2,1,0:T(8,128)(2,1)S(1)}, bf16[3,576,128]{2,1,0:T(8,128)(2,1)S(1)}, u32[]{:S(2)}, u32[]{:S(2)}) collective-permute-start(bf16[3,576,128]{2,1,0:T(8,128)(2,1)S(1)} %get-tuple-element.125), channel_id=1, source_target_pairs={{0,16},{8,24},{16,0},{24,8},{1,17},{9,25},{17,1},{25,9},{2,18},{10... | collective-permute-start | bytes 1327112 | tf_op jit(solution)/shard_map/ppermute | solution.py:194
  265.1 38.0 %collective-permute-start.11 = (bf16[3,576,128]{2,1,0:T(8,128)(2,1)S(1)}, bf16[3,576,128]{2,1,0:T(8,128)(2,1)S(1)}, u32[]{:S(2)}, u32[]{:S(2)}) collective-permute-start(bf16[3,576,128]{2,1,0:T(8,128)(2,1)S(1)} %get-tuple-element.126), channel_id=1, source_target_pairs={{0,8},{8,0},{16,24},{24,16},{1,9},{9,1},{17,25},{25,17},{2,10},{10... | collective-permute-start | bytes 1327112 | tf_op jit(solution)/shard_map/ppermute | solution.py:194
  462.9 36.4 %collective-permute-start.27 = (bf16[3,576,128]{2,1,0:T(8,128)(2,1)S(1)}, bf16[3,576,128]{2,1,0:T(8,128)(2,1)S(1)}, u32[]{:S(2)}, u32[]{:S(2)}) collective-permute-start(bf16[3,576,128]{2,1,0:T(8,128)(2,1)S(1)} %get-tuple-element.121), channel_id=1, source_target_pairs={{0,16},{8,24},{16,0},{24,8},{1,17},{9,25},{17,1},{25,9},{2,18},{10... | collective-permute-start | bytes 1327112 | tf_op jit(solution)/shard_map/ppermute | solution.py:194
  462.9 36.4 %collective-permute-start.26 = (bf16[3,576,128]{2,1,0:T(8,128)(2,1)S(1)}, bf16[3,576,128]{2,1,0:T(8,128)(2,1)S(1)}, u32[]{:S(2)}, u32[]{:S(2)}) collective-permute-start(bf16[3,576,128]{2,1,0:T(8,128)(2,1)S(1)} %get-tuple-element.122), channel_id=1, source_target_pairs={{0,8},{8,0},{16,24},{24,16},{1,9},{9,1},{17,25},{25,17},{2,10},{10... | collective-permute-start | bytes 1327112 | tf_op jit(solution)/shard_map/ppermute | solution.py:194
  534.2 195.8 %reduce-scatter.13.cloned.1.call-start = ((), (), s32[]{:S(2)}) async-start(), calls=%async_computation.15 | async-start | bytes 1310720 | tf_op jit(solution)/shard_map/reduce_scatter | solution.py:342
  596.5 37.7 %collective-permute-start.37 = (bf16[3,576,128]{2,1,0:T(8,128)(2,1)}, bf16[3,576,128]{2,1,0:T(8,128)(2,1)}, u32[]{:S(2)}, u32[]{:S(2)}) collective-permute-start(bf16[3,576,128]{2,1,0:T(8,128)(2,1)} %get-tuple-element.117), channel_id=1, source_target_pairs={{0,16},{8,24},{16,0},{24,8},{1,17},{9,25},{17,1},{25,9},{2,18},{10... | collective-permute-start | bytes 1327112 | tf_op jit(solution)/shard_map/ppermute | solution.py:194
  596.5 37.7 %collective-permute-start.36 = (bf16[3,576,128]{2,1,0:T(8,128)(2,1)S(1)}, bf16[3,576,128]{2,1,0:T(8,128)(2,1)}, u32[]{:S(2)}, u32[]{:S(2)}) collective-permute-start(bf16[3,576,128]{2,1,0:T(8,128)(2,1)S(1)} %get-tuple-element.118), channel_id=1, source_target_pairs={{0,8},{8,0},{16,24},{24,16},{1,9},{9,1},{17,25},{25,17},{2,10},{10... | collective-permute-start | bytes 1327112 | tf_op jit(solution)/shard_map/ppermute | solution.py:194
  652.1 154.0 %all-reduce.2.cloned.1.call-start = ((), (), s32[]{:S(2)}) async-start(), calls=%async_computation.12 | async-start | bytes 196608 | tf_op jit(solution)/shard_map/psum | solution.py:433
  658.4 204.7 %reduce-scatter.19.cloned.1.call-start = ((), (), s32[]{:S(2)}) async-start(), calls=%async_computation.18 | async-start | bytes 5242880 | tf_op jit(solution)/shard_map/reduce_scatter | solution.py:342
  666.0 253.6 %reduce-scatter.23.cloned.1.call-start = ((), (), s32[]{:S(2)}) async-start(), calls=%async_computation.20 | async-start | bytes 5242880 | tf_op jit(solution)/shard_map/reduce_scatter | solution.py:342
  673.6 292.9 %reduce-scatter.11.cloned.1.call-start = ((), (), s32[]{:S(2)}) async-start(), calls=%async_computation.14 | async-start | bytes 3932160 | tf_op jit(solution)/shard_map/reduce_scatter | solution.py:342
  679.8 402.7 %reduce-scatter.17.cloned.1.call-start = ((), (), s32[]{:S(2)}) async-start(), calls=%async_computation.17 | async-start | bytes 5242880 | tf_op jit(solution)/shard_map/reduce_scatter | solution.py:342
  687.8 399.8 %reduce-scatter.21.cloned.1.call-start = ((), (), s32[]{:S(2)}) async-start(), calls=%async_computation.19 | async-start | bytes 5242880 | tf_op jit(solution)/shard_map/reduce_scatter | solution.py:342
  695.8 429.4 %reduce-scatter.9.cloned.1.call-start = ((), (), s32[]{:S(2)}) async-start(), calls=%async_computation.13 | async-start | bytes 3932160 | tf_op jit(solution)/shard_map/reduce_scatter | solution.py:342
  743.5 64.6 %collective-permute-start.52 = (bf16[32,1024]{1,0:T(8,128)(2,1)S(1)}, bf16[32,1024]{1,0:T(8,128)(2,1)S(1)}, u32[]{:S(2)}, u32[]{:S(2)}) collective-permute-start(bf16[32,1024]{1,0:T(8,128)(2,1)S(1)} %fusion.87), channel_id=1, source_target_pairs={{0,16},{8,24},{16,0},{24,8},{1,17},{9,25},{17,1},{25,9},{2,18},{10... | collective-permute-start | bytes 196616 | tf_op jit(solution)/shard_map/ppermute | solution.py:230
  814.4 108.6 %collective-permute-start.54 = (bf16[128,1024]{1,0:T(8,128)(2,1)S(1)}, bf16[128,1024]{1,0:T(8,128)(2,1)S(1)}, u32[]{:S(2)}, u32[]{:S(2)}) collective-permute-start(bf16[128,1024]{1,0:T(8,128)(2,1)S(1)} %pad_maximum_fusion.46), channel_id=1, source_target_pairs={{0,4},{4,0},{1,5},{5,1},{2,6},{6,2},{3,7},{7,3},{8,12},{12,8},{9,1... | collective-permute-start | bytes 786440 | tf_op jit(solution)/shard_map/ppermute | solution.py:199
  865.0 104.1 %collective-permute-start.65 = (bf16[128,2048]{1,0:T(8,128)(2,1)}, bf16[128,2048]{1,0:T(8,128)(2,1)}, u32[]{:S(2)}, u32[]{:S(2)}) collective-permute-start(bf16[128,2048]{1,0:T(8,128)(2,1)} %dynamic-slice_bitcast_fusion.4), channel_id=1, source_target_pairs={{0,8},{8,0},{16,24},{24,16},{1,9},{9,1},{17,25},{25,17},{2,10},{10... | collective-permute-start | bytes 1572872 | tf_op jit(solution)/shard_map/ppermute | solution.py:224
  921.5 51.3 %collective-permute-start.75 = (bf16[256,1024]{1,0:T(8,128)(2,1)}, bf16[256,1024]{1,0:T(8,128)(2,1)}, u32[]{:S(2)}, u32[]{:S(2)}) collective-permute-start(bf16[256,1024]{1,0:T(8,128)(2,1)} %dynamic-slice_bitcast_fusion.2), channel_id=1, source_target_pairs={{0,8},{8,0},{16,24},{24,16},{1,9},{9,1},{17,25},{25,17},{2,10},{10... | collective-permute-start | bytes 1572872 | tf_op jit(solution)/shard_map/ppermute | solution.py:224
  970.3 28.5 %collective-permute-start.66 = (bf16[64,2048]{1,0:T(8,128)(2,1)S(1)}, bf16[64,2048]{1,0:T(8,128)(2,1)S(1)}, u32[]{:S(2)}, u32[]{:S(2)}) collective-permute-start(bf16[64,2048]{1,0:T(8,128)(2,1)S(1)} %dynamic-slice_bitcast_fusion.10), channel_id=1, source_target_pairs={{0,16},{8,24},{16,0},{24,8},{1,17},{9,25},{17,1},{25,9},{2,18},{10... | collective-permute-start | bytes 786440 | tf_op jit(solution)/shard_map/ppermute | solution.py:224
  974.0 37.5 %collective-permute-start.76 = (bf16[128,1024]{1,0:T(8,128)(2,1)S(1)}, bf16[128,1024]{1,0:T(8,128)(2,1)S(1)}, u32[]{:S(2)}, u32[]{:S(2)}) collective-permute-start(bf16[128,1024]{1,0:T(8,128)(2,1)S(1)} %dynamic-slice_bitcast_fusion.8), channel_id=1, source_target_pairs={{0,16},{8,24},{16,0},{24,8},{1,17},{9,25},{17,1},{25,9},{2,18},{10... | collective-permute-start | bytes 786440 | tf_op jit(solution)/shard_map/ppermute | solution.py:224
  985.5 25.8 %collective-permute-start.46 = (bf16[64,1536]{1,0:T(8,128)(2,1)S(1)}, bf16[64,1536]{1,0:T(8,128)(2,1)S(1)}, u32[]{:S(2)}, u32[]{:S(2)}) collective-permute-start(bf16[64,1536]{1,0:T(8,128)(2,1)S(1)} %dynamic-slice_bitcast_fusion.12), channel_id=1, source_target_pairs={{0,16},{8,24},{16,0},{24,8},{1,17},{9,25},{17,1},{25,9},{2,18},{10... | collective-permute-start | bytes 589832 | tf_op jit(solution)/shard_map/ppermute | solution.py:224
  998.8 32.4 %collective-permute-start.67 = (bf16[64,2048]{1,0:T(8,128)(2,1)S(1)}, bf16[64,2048]{1,0:T(8,128)(2,1)S(1)}, u32[]{:S(2)}, u32[]{:S(2)}) collective-permute-start(bf16[64,2048]{1,0:T(8,128)(2,1)S(1)} %fusion.76), channel_id=1, source_target_pairs={{0,16},{8,24},{16,0},{24,8},{1,17},{9,25},{17,1},{25,9},{2,18},{10... | collective-permute-start | bytes 786440 | tf_op jit(solution)/shard_map/ppermute | solution.py:230
  1011.6 23.7 %collective-permute-start.77 = (bf16[128,1024]{1,0:T(8,128)(2,1)S(1)}, bf16[128,1024]{1,0:T(8,128)(2,1)S(1)}, u32[]{:S(2)}, u32[]{:S(2)}) collective-permute-start(bf16[128,1024]{1,0:T(8,128)(2,1)S(1)} %fusion.74), channel_id=1, source_target_pairs={{0,16},{8,24},{16,0},{24,8},{1,17},{9,25},{17,1},{25,9},{2,18},{10... | collective-permute-start | bytes 786440 | tf_op jit(solution)/shard_map/ppermute | solution.py:230
  1031.3 23.7 %collective-permute-start.68 = (bf16[128,2048]{1,0:T(8,128)(2,1)S(1)}, bf16[128,2048]{1,0:T(8,128)(2,1)S(1)}, u32[]{:S(2)}, u32[]{:S(2)}) collective-permute-start(bf16[128,2048]{1,0:T(8,128)(2,1)S(1)} %pad_maximum_fusion.41), channel_id=1, source_target_pairs={{0,8},{8,0},{16,24},{24,16},{1,9},{9,1},{17,25},{25,17},{2,10},{10... | collective-permute-start | bytes 1572872 | tf_op jit(solution)/shard_map/ppermute | solution.py:230
  1035.4 30.7 %collective-permute-start.78 = (bf16[256,1024]{1,0:T(8,128)(2,1)S(1)}, bf16[256,1024]{1,0:T(8,128)(2,1)S(1)}, u32[]{:S(2)}, u32[]{:S(2)}) collective-permute-start(bf16[256,1024]{1,0:T(8,128)(2,1)S(1)} %pad_maximum_fusion.43), channel_id=1, source_target_pairs={{0,8},{8,0},{16,24},{24,16},{1,9},{9,1},{17,25},{25,17},{2,10},{10... | collective-permute-start | bytes 1572872 | tf_op jit(solution)/shard_map/ppermute | solution.py:230
  1084.4 43.4 %collective-permute-start.60 = (bf16[128,2048]{1,0:T(8,128)(2,1)}, bf16[128,2048]{1,0:T(8,128)(2,1)}, u32[]{:S(2)}, u32[]{:S(2)}) collective-permute-start(bf16[128,2048]{1,0:T(8,128)(2,1)} %dynamic-slice_bitcast_fusion.5), channel_id=1, source_target_pairs={{0,8},{8,0},{16,24},{24,16},{1,9},{9,1},{17,25},{25,17},{2,10},{10... | collective-permute-start | bytes 1572872 | tf_op jit(solution)/shard_map/ppermute | solution.py:224
  1089.6 42.0 %collective-permute-start.70 = (bf16[256,1024]{1,0:T(8,128)(2,1)}, bf16[256,1024]{1,0:T(8,128)(2,1)}, u32[]{:S(2)}, u32[]{:S(2)}) collective-permute-start(bf16[256,1024]{1,0:T(8,128)(2,1)} %dynamic-slice_bitcast_fusion.3), channel_id=1, source_target_pairs={{0,8},{8,0},{16,24},{24,16},{1,9},{9,1},{17,25},{25,17},{2,10},{10... | collective-permute-start | bytes 1572872 | tf_op jit(solution)/shard_map/ppermute | solution.py:224
  1129.1 28.5 %collective-permute-start.61 = (bf16[64,2048]{1,0:T(8,128)(2,1)S(1)}, bf16[64,2048]{1,0:T(8,128)(2,1)S(1)}, u32[]{:S(2)}, u32[]{:S(2)}) collective-permute-start(bf16[64,2048]{1,0:T(8,128)(2,1)S(1)} %dynamic-slice_bitcast_fusion.11), channel_id=1, source_target_pairs={{0,16},{8,24},{16,0},{24,8},{1,17},{9,25},{17,1},{25,9},{2,18},{10... | collective-permute-start | bytes 786440 | tf_op jit(solution)/shard_map/ppermute | solution.py:224
  1132.9 37.5 %collective-permute-start.71 = (bf16[128,1024]{1,0:T(8,128)(2,1)S(1)}, bf16[128,1024]{1,0:T(8,128)(2,1)S(1)}, u32[]{:S(2)}, u32[]{:S(2)}) collective-permute-start(bf16[128,1024]{1,0:T(8,128)(2,1)S(1)} %dynamic-slice_bitcast_fusion.9), channel_id=1, source_target_pairs={{0,16},{8,24},{16,0},{24,8},{1,17},{9,25},{17,1},{25,9},{2,18},{10... | collective-permute-start | bytes 786440 | tf_op jit(solution)/shard_map/ppermute | solution.py:224
  1144.3 25.9 %collective-permute-start.41 = (bf16[64,1536]{1,0:T(8,128)(2,1)S(1)}, bf16[64,1536]{1,0:T(8,128)(2,1)S(1)}, u32[]{:S(2)}, u32[]{:S(2)}) collective-permute-start(bf16[64,1536]{1,0:T(8,128)(2,1)S(1)} %dynamic-slice_bitcast_fusion.13), channel_id=1, source_target_pairs={{0,16},{8,24},{16,0},{24,8},{1,17},{9,25},{17,1},{25,9},{2,18},{10... | collective-permute-start | bytes 589832 | tf_op jit(solution)/shard_map/ppermute | solution.py:224
  1157.6 32.4 %collective-permute-start.62 = (bf16[64,2048]{1,0:T(8,128)(2,1)S(1)}, bf16[64,2048]{1,0:T(8,128)(2,1)S(1)}, u32[]{:S(2)}, u32[]{:S(2)}) collective-permute-start(bf16[64,2048]{1,0:T(8,128)(2,1)S(1)} %fusion.77), channel_id=1, source_target_pairs={{0,16},{8,24},{16,0},{24,8},{1,17},{9,25},{17,1},{25,9},{2,18},{10... | collective-permute-start | bytes 786440 | tf_op jit(solution)/shard_map/ppermute | solution.py:230
  1170.4 23.8 %collective-permute-start.72 = (bf16[128,1024]{1,0:T(8,128)(2,1)S(1)}, bf16[128,1024]{1,0:T(8,128)(2,1)S(1)}, u32[]{:S(2)}, u32[]{:S(2)}) collective-permute-start(bf16[128,1024]{1,0:T(8,128)(2,1)S(1)} %fusion.75), channel_id=1, source_target_pairs={{0,16},{8,24},{16,0},{24,8},{1,17},{9,25},{17,1},{25,9},{2,18},{10... | collective-permute-start | bytes 786440 | tf_op jit(solution)/shard_map/ppermute | solution.py:230
  1190.1 23.7 %collective-permute-start.63 = (bf16[128,2048]{1,0:T(8,128)(2,1)S(1)}, bf16[128,2048]{1,0:T(8,128)(2,1)S(1)}, u32[]{:S(2)}, u32[]{:S(2)}) collective-permute-start(bf16[128,2048]{1,0:T(8,128)(2,1)S(1)} %pad_maximum_fusion.40), channel_id=1, source_target_pairs={{0,8},{8,0},{16,24},{24,16},{1,9},{9,1},{17,25},{25,17},{2,10},{10... | collective-permute-start | bytes 1572872 | tf_op jit(solution)/shard_map/ppermute | solution.py:230
  1194.3 30.7 %collective-permute-start.73 = (bf16[256,1024]{1,0:T(8,128)(2,1)S(1)}, bf16[256,1024]{1,0:T(8,128)(2,1)S(1)}, u32[]{:S(2)}, u32[]{:S(2)}) collective-permute-start(bf16[256,1024]{1,0:T(8,128)(2,1)S(1)} %pad_maximum_fusion.42), channel_id=1, source_target_pairs={{0,8},{8,0},{16,24},{24,16},{1,9},{9,1},{17,25},{25,17},{2,10},{10... | collective-permute-start | bytes 1572872 | tf_op jit(solution)/shard_map/ppermute | solution.py:230
  1215.3 29.7 %collective-permute-start.64 = (bf16[256,2048]{1,0:T(8,128)(2,1)}, bf16[256,2048]{1,0:T(8,128)(2,1)}, u32[]{:S(2)}, u32[]{:S(2)}) collective-permute-start(bf16[256,2048]{1,0:T(8,128)(2,1)} %pad_maximum_fusion.14), channel_id=1, source_target_pairs={{0,4},{4,0},{1,5},{5,1},{2,6},{6,2},{3,7},{7,3},{8,12},{12,8},{9,1... | collective-permute-start | bytes 3145736 | tf_op jit(solution)/shard_map/ppermute | solution.py:199
  1226.3 41.4 %collective-permute-start.74 = (bf16[512,1024]{1,0:T(8,128)(2,1)}, bf16[512,1024]{1,0:T(8,128)(2,1)}, u32[]{:S(2)}, u32[]{:S(2)}) collective-permute-start(bf16[512,1024]{1,0:T(8,128)(2,1)} %pad_maximum_fusion.16), channel_id=1, source_target_pairs={{0,4},{4,0},{1,5},{5,1},{2,6},{6,2},{3,7},{7,3},{8,12},{12,8},{9,1... | collective-permute-start | bytes 3145736 | tf_op jit(solution)/shard_map/ppermute | solution.py:199
  (145 other events, 1221.0 us)
Sparse Core Ops, SparseCore 0:
  15.7 46.5 all-gather.14
  64.1 26.6 all-gather.22
  92.6 52.5 all-gather.16
  146.9 52.6 all-gather.24
  201.3 43.8 all-gather.18
  247.4 26.6 all-gather.26
  275.9 52.5 all-gather.20
  330.9 52.6 all-gather.28
  534.3 25.8 reduce-scatter.14
  652.2 27.1 reduce-scatter.12
  685.0 121.0 all-reduce.1
  809.5 53.5 reduce-scatter.18
  866.9 52.6 reduce-scatter.22
  922.5 43.9 reduce-scatter.10
  969.9 52.6 reduce-scatter.16
  1025.7 52.6 reduce-scatter.20
  1081.2 43.9 reduce-scatter.8

commit v2 on v1

--- a/solution.py
+++ b/solution.py
@@ -107,6 +107,11 @@
             jax.ShapeDtypeStruct((parts, tokens, width), F32),
         ],
         scratch_shapes=[pltpu.VMEM((parts * tokens, 2 * width), BF16)],
+        cost_estimate=pl.CostEstimate(
+            flops=2 * 512 * width // HD * (parts * tokens) ** 2,
+            transcendentals=width // HD * (parts * tokens) ** 2,
+            bytes_accessed=12 * parts * tokens * width,
+        ),
         compiler_params=pltpu.CompilerParams(vmem_limit_bytes=VMEM_BYTES),
     )(packed, packed, packed)
 
@@ -173,6 +178,11 @@
             pltpu.VMEM((width, parts * tokens), F32),
             pltpu.VMEM((width, parts * tokens), F32),
         ],
+        cost_estimate=pl.CostEstimate(
+            flops=5 * 512 * width // HD * (parts * tokens) ** 2,
+            transcendentals=width // HD * (parts * tokens) ** 2,
+            bytes_accessed=20 * parts * tokens * width,
+        ),
         compiler_params=pltpu.CompilerParams(vmem_limit_bytes=VMEM_BYTES),
     )(packed, packed, packed, mixed, grads, logs)
 
@@ -209,27 +219,199 @@
 
 
 def add_rounded(left, right):
-    return (left.astype(F32) + right.astype(F32)).astype(BF16)
-
-
-def sum_over_z(values, index):
-    count = lax.axis_size("z")
-    bit = 1
-    while bit < count:
-        pairs = [(i, i ^ bit) for i in range(count)]
-        upper = ((index & bit) != 0).astype(jnp.int32)
+    return (left.astype(F32) + right.astype(F32)).astype(left.dtype)
+
+
+def join_columns_kernel(core_ref, *refs, moves):
+    out_ref = refs[-1]
+    core = core_ref[0]
+    for layer in range(out_ref.shape[0]):
+        own_ref, other_ref = refs[2 * layer], refs[2 * layer + 1]
+        for half in range(2):
+            mine = core == half
+            for source, target, size in moves:
+                span = slice(source, source + size)
+                part = jnp.where(mine, own_ref[:, span], other_ref[:, span])
+                out_ref[layer, :, target[half] : target[half] + size] = part.astype(F32)
+
+
+def join_columns(pairs, core, moves):
+    rows, columns = pairs[0][0].shape
+    block = 64 if rows % 64 == 0 else rows
+    spec = pl.BlockSpec((block, columns), lambda i, core: (i, 0))
+    return pl.pallas_call(
+        partial(join_columns_kernel, moves=moves),
+        name="join_columns",
+        grid_spec=pltpu.PrefetchScalarGridSpec(
+            num_scalar_prefetch=1,
+            grid=(rows // block,),
+            in_specs=[spec] * (2 * len(pairs)),
+            out_specs=pl.BlockSpec((len(pairs), block, 2 * columns), lambda i, core: (0, i, 0)),
+        ),
+        out_shape=jax.ShapeDtypeStruct((len(pairs), rows, 2 * columns), F32),
+        compiler_params=pltpu.CompilerParams(vmem_limit_bytes=VMEM_BYTES),
+    )(core, *[part for pair in pairs for part in pair])
+
+
+def join_rows_kernel(core_ref, *refs):
+    out_ref = refs[-1]
+    mine = core_ref[0] == pl.program_id(0)
+    for layer in range(out_ref.shape[0]):
+        out_ref[layer] = jnp.where(mine, refs[2 * layer][...], refs[2 * layer + 1][...]).astype(F32)
+
+
+def join_rows(pairs, core):
+    rows, columns = pairs[0][0].shape
+    block = 128 if rows % 128 == 0 else rows
+    count = rows // block
+    spec = pl.BlockSpec((block, columns), lambda h, i, core: (i, 0))
+    return pl.pallas_call(
+        join_rows_kernel,
+        name="join_rows",
+        grid_spec=pltpu.PrefetchScalarGridSpec(
+            num_scalar_prefetch=1,
+            grid=(2, count),
+            in_specs=[spec] * (2 * len(pairs)),
+            out_specs=pl.BlockSpec((len(pairs), block, columns), lambda h, i, core: (0, h * count + i, 0)),
+        ),
+        out_shape=jax.ShapeDtypeStruct((len(pairs), 2 * rows, columns), F32),
+        compiler_params=pltpu.CompilerParams(vmem_limit_bytes=VMEM_BYTES),
+    )(core, *[part for pair in pairs for part in pair])
+
+
+class Pipeline:
+    def __init__(self):
+        self.running = []
+        self.finished = {}
+        self.fresh = {}
+
+    def add(self, flow, finish):
+        self.running.append([flow, finish, None, None])
+
+    def advance(self, main):
+        due = []
+        for item in self.running:
+            if item[2] is not None:
+                item[3] -= 1
+            if item[2] is None or item[3] <= 0:
+                due.append(item)
+        flights = [item[2] for item in due]
+        main, flights, fresh = lax.optimization_barrier((main, flights, self.fresh))
+        self.finished.update(fresh)
+        self.fresh = {}
+        steps = []
+        for item, flight in zip(due, flights):
+            try:
+                steps.append((item,) + item[0].send(flight))
+            except StopIteration as stop:
+                item[1](stop.value)
+                self.running.remove(item)
+        sends = [step[1] for step in steps]
+        main, sends = lax.optimization_barrier((main, sends))
+        for (item, _, start, hold), values in zip(steps, sends):
+            item[2], item[3] = start(values), hold
+        return main
+
+    def drain(self):
+        while self.running:
+            self.advance(())
+        self.finished.update(self.fresh)
+
+
+def bit_count(number):
+    return number.bit_length() - 1
+
+
+def swap_pairs(count, bit):
+    return [(i, i ^ (1 << bit)) for i in range(count)]
+
+
+def pick(values, place, axis):
+    return lax.dynamic_index_in_dim(values, place, axis, keepdims=False)
+
+
+def scatter_flow(gradient, index, count):
+    bits = bit_count(count)
+    half = gradient.shape[1] // 2
+    lead = (2,) * bits + (gradient.shape[0] // count,)
+    halves = [gradient[:, :half].reshape(lead + (half,)), gradient[:, half:].reshape(lead + (half,))]
+    for step in range(bits):
+        places = [(bits - 1 - step, 0), (step, bits - 1 - step)]
+        mine = [(index >> bit) & 1 for bit, _ in places]
+        sends = [pick(value, 1 - own, axis) for value, own, (_, axis) in zip(halves, mine, places)]
+        kept = [pick(value, own, axis) for value, own, (_, axis) in zip(halves, mine, places)]
+
+        def start(values, places=places):
+            return [
+                lax.ppermute(value, "shard", swap_pairs(count, bit)) for value, (bit, _) in zip(values, places)
+            ]
+
+        arrived = yield sends, start, 1
+        halves = [add_rounded(own, other) for own, other in zip(kept, arrived)]
+    return jnp.concatenate(halves, axis=1)
+
+
+def offload_flow(gradient, hold):
+    def start(values):
+        return [lax.psum_scatter(values[0], "shard", scatter_dimension=0, tiled=True)]
+
+    (piece,) = yield [gradient], start, hold
+    return piece
+
+
+def line_flow(piece, count):
+    total, carry = piece.astype(F32), None
+    for step in range(1, count):
+        pairs = [(step - 1, step), (count - step, count - step - 1)]
+        send = piece if carry is None else add_rounded(piece, carry)
+
+        def start(values, pairs=pairs):
+            return [lax.ppermute(values[0], "z", pairs)]
+
+        (carry,) = yield [send], start, 1
+        total = total + carry.astype(F32)
+    return total.astype(piece.dtype)
+
+
+def halving_flow(values, index, count):
+    bits = bit_count(count)
+    for bit in range(bits):
+        upper = (index >> bit) & 1
         halves = values.reshape((2, values.shape[0] // 2) + values.shape[1:])
-        sent = lax.dynamic_index_in_dim(halves, 1 - upper, 0, keepdims=False)
-        kept = lax.dynamic_index_in_dim(halves, upper, 0, keepdims=False)
-        values = add_rounded(kept, lax.ppermute(sent, "z", pairs))
-        bit *= 2
-    while bit > 1:
-        bit //= 2
-        pairs = [(i, i ^ bit) for i in range(count)]
-        upper = (index & bit) != 0
-        other = lax.ppermute(values, "z", pairs)
+
+        def start(sent, bit=bit):
+            return [lax.ppermute(sent[0], "z", swap_pairs(count, bit))]
+
+        (other,) = yield [pick(halves, 1 - upper, 0)], start, 1
+        values = add_rounded(pick(halves, upper, 0), other)
+    for bit in reversed(range(bits)):
+        upper = ((index >> bit) & 1) == 1
+
+        def start(sent, bit=bit):
+            return [lax.ppermute(sent[0], "z", swap_pairs(count, bit))]
+
+        (other,) = yield [values], start, 1
         values = jnp.concatenate([jnp.where(upper, other, values), jnp.where(upper, values, other)], axis=0)
     return values
+
+
+def gather_flow(part, index, count):
+    bits = bit_count(count)
+    half = part.shape[1] // 2
+    halves = [part[:, :half], part[:, half:]]
+    for step in range(bits):
+        places = [(step, 0), (bits - 1 - step, step)]
+
+        def start(values, places=places):
+            return [
+                lax.ppermute(value, "shard", swap_pairs(count, bit)) for value, (bit, _) in zip(values, places)
+            ]
+
+        arrived = yield halves, start, 1
+        for place, (bit, axis) in enumerate(places):
+            upper, own, other = ((index >> bit) & 1) == 1, halves[place], arrived[place]
+            halves[place] = jnp.stack([jnp.where(upper, other, own), jnp.where(upper, own, other)], axis=axis)
+    return jnp.concatenate([value.reshape(-1, half) for value in halves], axis=1)
 
 
 def gelu_parts(pre_act):
@@ -273,29 +455,38 @@
     vectors = (norm1_scale, norm1_shift, out_bias, norm2_scale, norm2_shift, down_bias, qv_bias, up_bias)
     sizes = [member.shape[1] for member in vectors]
     offsets = [sum(sizes[:place]) for place in range(len(sizes) + 1)]
-    small = lax.all_gather(jnp.concatenate(vectors, axis=1), "shard", axis=0)
+    vectors_full = lax.all_gather(jnp.concatenate(vectors, axis=1), "shard", axis=0)
 
     def full_vector(layer, place):
-        return small[:, layer, offsets[place] : offsets[place + 1]].reshape(-1).astype(F32)
-
+        return vectors_full[:, layer, offsets[place] : offsets[place + 1]].reshape(-1).astype(F32)
+
+    pipeline = Pipeline()
     weights = []
     for layer in range(layers):
         qkv_part = my_half(qkv_weight[layer].reshape(-1, 3, shards, 2, half_width // shards), 3)
-        qkv_part = jnp.swapaxes(qkv_part.reshape(-1, 3, z_count, group), 1, 2)
+        qkv_part = jnp.swapaxes(qkv_part.reshape(-1, 3, z_count, group), 1, 2).reshape(-1, 3 * half_width)
         up_part = my_half(up_weight[layer].reshape(-1, shards, 2, hidden_units // 2 // shards), 2)
-        weights.append(
-            (
-                gather(qkv_part.reshape(-1, 3 * half_width)),
-                gather(my_half(out_weight[layer].reshape(2, -1, width), 0)),
-                gather(up_part.reshape(-1, hidden_units // 2)),
-                gather(my_half(down_weight[layer].reshape(2, -1, width), 0)),
-            )
-        )
+        held = {
+            "out_part": my_half(out_weight[layer].reshape(2, -1, width), 0),
+            "up": gather(up_part.reshape(-1, hidden_units // 2)),
+            "down": gather(my_half(down_weight[layer].reshape(2, -1, width), 0)),
+        }
+        if layer == 0:
+            held["qkv"] = gather(qkv_part)
+        else:
+            held["qkv_part"] = qkv_part
+        weights.append(held)
+
+    def fetch(layer, name):
+        def finish(full):
+            weights[layer][name] = full
+
+        pipeline.add(gather_flow(weights[layer][name + "_part"], s_index, shards), finish)
 
     stream = images.astype(F32).reshape(-1, width)
     saved = []
     for layer in range(layers):
-        qkv_full, out_full, up_full, down_full = weights[layer]
+        held = weights[layer]
         scale_one, shift_one, out_shift, scale_two, shift_two, down_shift, qv_full, up_all = [
             full_vector(layer, place) for place in range(8)
         ]
@@ -303,17 +494,28 @@
         qkv_shift = jnp.stack([qv_halves[0], jnp.zeros_like(qv_halves[0]), qv_halves[1]], axis=1).reshape(-1)
         up_shift = my_half(up_all.reshape(shards, 2, -1), 1).reshape(-1)
 
+        if layer == 0:
+            fetch(layer, "out")
         normed_own, average_one, inverse_one = norm_forward(stream, scale_one, shift_one)
+        normed_own = pipeline.advance(normed_own)
         normed_one = with_partner(normed_own)
-        projected = (matmul(normed_one, qkv_full) + qkv_shift).astype(BF16)
+        projected = (matmul(normed_one, held["qkv"]) + qkv_shift).astype(BF16)
         pieces = projected.reshape(tokens, z_count, 3, group).transpose(1, 2, 0, 3)
-        packed = exchange(xor_order(pieces, z_index))
+        if layer + 1 < layers:
+            fetch(layer + 1, "qkv")
+        pieces = pipeline.advance(xor_order(pieces, z_index))
+        packed = pipeline.advance(exchange(pieces))
         mixed, logs = attend(packed)
+        while "out" not in held:
+            mixed = pipeline.advance(mixed)
         attended = xor_order(exchange(mixed), z_index).transpose(1, 0, 2).reshape(tokens, half_width)
-        middle = stream + sum_with_partner(matmul(attended, out_full)) + out_shift
+        middle = stream + sum_with_partner(matmul(attended, held["out"])) + out_shift
+        if layer + 1 < layers:
+            fetch(layer + 1, "out")
+        middle = pipeline.advance(middle)
         two_own, average_two, inverse_two = norm_forward(middle, scale_two, shift_two)
         normed_two = with_partner(two_own)
-        pre_act = matmul(normed_two, up_full) + up_shift
+        pre_act = matmul(normed_two, held["up"]) + up_shift
         hidden, slope = gelu_parts(pre_act)
         saved.append(
             (
@@ -335,20 +537,58 @@
                 scale_two,
             )
         )
-        stream = middle + sum_with_partner(matmul(hidden, down_full)) + down_shift
+        stream = middle + sum_with_partner(matmul(hidden, held["down"])) + down_shift
+        stream = pipeline.advance(stream)
+        while layer + 1 < layers and "qkv" not in weights[layer + 1]:
+            stream = pipeline.advance(stream)
     results = stream.astype(BF16).reshape(image_count, local_len, width)
 
-    def reduce_weight(gradient):
-        piece = lax.psum_scatter(gradient.astype(BF16), "shard", scatter_dimension=0, tiled=True)
-        piece = sum_over_z(piece, z_index)
-        other = swap(piece)
-        first = jnp.where(c_index == 0, piece, other)
-        second = jnp.where(c_index == 0, other, piece)
-        return first, second
+    core = c_index.astype(jnp.int32).reshape(1)
+    block = half_width // shards
+    cut = min(block, group)
+    qkv_moves = []
+    for part in range(3):
+        for start in range(0, half_width, cut):
+            source = start // group * 3 * group + part * group + start % group
+            target = part * width + start // block * 2 * block + start % block
+            qkv_moves.append((source, (target, target + block), cut))
+    block_up = hidden_units // 2 // shards
+    up_moves = [
+        (place * block_up, (2 * place * block_up, (2 * place + 1) * block_up), block_up) for place in range(shards)
+    ]
+
+    joins = {
+        "qkv": lambda pairs: join_columns(pairs, core, qkv_moves),
+        "up": lambda pairs: join_columns(pairs, core, up_moves),
+        "out": lambda pairs: join_rows(pairs, core),
+        "down": lambda pairs: join_rows(pairs, core),
+        "small": lambda pairs: jnp.stack([(own + other).reshape(-1) for own, other in pairs]),
+    }
+    weight_grads = [{} for _ in range(layers)]
+
+    def reduce_flow(gradient, offloaded, hold, halving):
+        if offloaded:
+            piece = yield from offload_flow(gradient, hold)
+        else:
+            piece = yield from scatter_flow(gradient, s_index, shards)
+        if halving:
+            piece = yield from halving_flow(piece, z_index, z_count)
+        else:
+            piece = yield from line_flow(piece, z_count)
+        (other,) = yield [piece], lambda values: [swap(values[0])], 1
+        return piece, other
+
+    def reduce_weight(layer, name, gradient, offloaded, hold=1, halving=False):
+        def finish(pair):
+            weight_grads[layer][name] = pair
+            if all(name in done for done in weight_grads):
+                pipeline.fresh[name] = joins[name]([done[name] for done in weight_grads])
+
+        if name != "small":
+            gradient = gradient.astype(BF16)
+        pipeline.add(reduce_flow(gradient, offloaded, hold, halving), finish)
 
     grad_stream = cotangent.astype(F32).reshape(-1, width)
-    weight_grads = [None] * layers
-    small_grads = [None] * layers
     for layer in reversed(range(layers)):
         (
             stream_in,
@@ -368,14 +608,15 @@
             scale_one,
             scale_two,
         ) = saved[layer]
-        qkv_full, out_full, up_full, down_full = weights[layer]
+        held = weights[layer]
+        offloaded = layer > 0
         branch_own = grad_stream.astype(BF16)
         branch_grad = with_partner(branch_own)
         grad_down_b = jnp.sum(branch_own.astype(F32), axis=0)
-        pre_grad = (times_transposed(branch_grad, down_full) * slope.astype(F32)).astype(BF16)
-        two_grad = sum_with_partner(times_transposed(pre_grad, up_full))
-        grad_down = reduce_weight(outer_sum(hidden, branch_grad))
-        grad_up = reduce_weight(outer_sum(normed_two, pre_grad))
+        reduce_weight(layer, "down", outer_sum(hidden, branch_grad), offloaded, 3, not offloaded)
+        pre_grad = (times_transposed(branch_grad, held["down"]) * slope.astype(F32)).astype(BF16)
+        pre_grad = pipeline.advance(pre_grad)
+        two_grad = sum_with_partner(times_transposed(pre_grad, held["up"]))
         grad_up_b = jnp.sum(pre_grad.astype(F32), axis=0)
         middle_back, grad_scale_two, grad_shift_two = norm_backward(
             middle, average_two, inverse_two, scale_two, two_grad
@@ -384,15 +625,19 @@
         out_own = middle_grad.astype(BF16)
         out_grad = with_partner(out_own)
         grad_out_b = jnp.sum(out_own.astype(F32), axis=0)
-        attended_grad = times_transposed(out_grad, out_full).astype(BF16)
+        attended_grad = times_transposed(out_grad, held["out"]).astype(BF16)
         grad_pieces = attended_grad.reshape(tokens, z_count, group).transpose(1, 0, 2)
-        head_grad = exchange(xor_order(grad_pieces, z_index))
-        grad_out = reduce_weight(outer_sum(attended, out_grad))
-        heads_back = attend_back(packed, mixed, head_grad, logs)
-        projected_grad = xor_order(exchange(heads_back), z_index).transpose(2, 0, 1, 3)
+        grad_pieces = pipeline.advance(xor_order(grad_pieces, z_index))
+        head_grad = exchange(grad_pieces)
+        reduce_weight(layer, "up", outer_sum(normed_two, pre_grad), offloaded, 3, not offloaded)
+        head_grad = pipeline.advance(head_grad)
+        heads_back = pipeline.advance(attend_back(packed, mixed, head_grad, logs))
+        reduce_weight(layer, "out", outer_sum(attended, out_grad), offloaded, 3, not offloaded)
+        arrived = pipeline.advance(exchange(heads_back))
+        projected_grad = xor_order(arrived, z_index).transpose(2, 0, 1, 3)
         projected_grad = projected_grad.reshape(tokens, 3 * half_width)
-        one_grad = sum_with_partner(times_transposed(projected_grad, qkv_full))
-        grad_qkv = reduce_weight(outer_sum(normed_one, projected_grad))
+        one_grad = sum_with_partner(times_transposed(projected_grad, held["qkv"]))
+        reduce_weight(layer, "qkv", outer_sum(normed_one, projected_grad), offloaded, 4, not offloaded)
         column_sums = jnp.sum(projected_grad.astype(F32), axis=0).reshape(z_count, 3, group)
         grad_qv_b = jnp.stack([column_sums[:, 0], column_sums[:, 2]])
         stream_back, grad_scale_one, grad_shift_one = norm_backward(
@@ -412,7 +657,7 @@
             )
             return halves.reshape(shards, -1)
 
-        small_grads[layer] = jnp.concatenate(
+        small = jnp.concatenate(
             [
                 member.reshape(shards, -1)
                 for member in (
@@ -428,28 +673,13 @@
             ],
             axis=1,
         )
-        weight_grads[layer] = (grad_qkv, grad_out, grad_up, grad_down)
-
-    small_sums = lax.psum(jnp.stack(small_grads, axis=1), ("z", "c", "shard"))
-    small_sums = lax.dynamic_index_in_dim(small_sums, s_index, 0, keepdims=False)
-    vector_grads = [small_sums[:, offsets[place] : offsets[place + 1]] for place in range(8)]
-
-    def join_qkv(pair):
-        halves = jnp.stack([part.reshape(-1, z_count, 3, group) for part in pair], axis=0)
-        halves = halves.transpose(1, 3, 0, 2, 4).reshape(-1, 3, 2, shards, half_width // shards)
-        return jnp.swapaxes(halves, 2, 3).reshape(-1, 3 * width).astype(F32)
-
-    def join_up(pair):
-        halves = jnp.stack([part.reshape(-1, shards, hidden_units // 2 // shards) for part in pair], axis=2)
-        return halves.reshape(-1, hidden_units).astype(F32)
-
-    def join_rows(pair):
-        return jnp.concatenate(pair, axis=0).astype(F32)
-
-    grad_qkv = jnp.stack([join_qkv(member[0]) for member in weight_grads])
-    grad_out = jnp.stack([join_rows(member[1]) for member in weight_grads])
-    grad_up = jnp.stack([join_up(member[2]) for member in weight_grads])
-    grad_down = jnp.stack([join_rows(member[3]) for member in weight_grads])
+        reduce_weight(layer, "small", small.reshape(4 * shards, -1), False)
+        grad_stream = pipeline.advance(grad_stream)
+
+    pipeline.drain()
+    sums = pipeline.finished
+    vector_grads = [sums["small"][:, offsets[place] : offsets[place + 1]] for place in range(8)]
+    grad_qkv, grad_out, grad_up, grad_down = sums["qkv"], sums["out"], sums["up"], sums["down"]
     input_grad = grad_stream.reshape(image_count, local_len, width)
     return (
         results,

time: 1290 us -> 1020 us (0.79)
  waiting for transfers between devices: 739 us -> 349 us
  starting transfers between devices: 72.9 us -> 174 us
  Pallas kernels: 109 us -> 132 us
  local copies, waits for them, and re-layouts: 131 us -> 116 us
  other arithmetic: 87.6 us -> 102 us
    reduce_scatter x8 -> x4, waiting for transfers between devices: 177 us -> 0.03 us  [start(): lax.psum_scatter(values[0], 'shard', scatter_dimension=0, tiled=True)]
    ppermute x32 -> x70, starting transfers between devices: 32.8 us -> 127 us  [the longest x18 46.5 us: start(): return [lax.ppermute(values[0], 'z', pairs)]]
    all_gather x8 -> x5, waiting for transfers between devices: 96.6 us -> 10.4 us  [gather(): return lax.all_gather(values, 'shard', axis=0, tiled=True)]
    psum x1 -> x0, waiting for transfers between devices: 62.4 us -> none  [body(): small_sums = lax.psum(jnp.stack(small_grads, axis=1), ('z', 'c', 'shard'))]
    ppermute x32 -> x70, waiting for transfers between devices: 199 us -> 156 us  [the longest x36 91 us: start(): lax.ppermute(value, 'shard', swap_pairs(count, bit))]
    convert_element_type x21 -> x39, other arithmetic: 10.8 us -> 33.8 us  [the longest x32 24.9 us: add_rounded(): return (left.astype(F32) + right.astype(F32)).astype(left.dtype)]
    pallas_call x0 -> x4, Pallas kernels: none -> 22.9 us  [the longest x2 11.5 us: join_rows(): pl.pallas_call(join_rows_kernel, name='join_rows', grid_spec=pltpu.Prefet...]
    select_n x8 -> x0, local copies, waits for them, and re-layouts: 15.9 us -> none  [the longest x4 8.45 us: reduce_weight(): first = jnp.where(c_index == 0, piece, other)]
  transfers between devices with their start and end apart: 97 -> 129, of which waited for: 59 -> 49; matrix products, arithmetic and copies ran while one was open for 20% -> 23% of each run, Pallas kernels for 6% -> 13%
where the time goes in v2:
time: 1020 us; the launch traced here: 1010 us
  waiting for transfers between devices  349 us (34%)
  starting transfers between devices  174 us (17%)
  Pallas kernels  132 us (13%)
  local copies, waits for them, and re-layouts  116 us (11%)
  matrix products  105 us (10%)
  other arithmetic  102 us (10%)
  between operations  18.1 us (2%)
    ppermute x24, waiting for transfers between devices, exchange(): lax.ppermute(pieces[k], 'z', [(i, i ^ k) for i in range(count)])  168 us
    ppermute x36, waiting for transfers between devices, start(): lax.ppermute(value, 'shard', swap_pairs(count, bit))  91 us
    pallas_call x2, Pallas kernels, attend_back(): pl.pallas_call(attend_back_kernel, name='attend_back', grid=(parts, token...  65.5 us
    ppermute x16, waiting for transfers between devices, start(): return [lax.ppermute(sent[0], 'z', swap_pairs(count, bit))]  47.7 us
    ppermute x18, starting transfers between devices, start(): return [lax.ppermute(values[0], 'z', pairs)]  46.5 us
    pallas_call x2, Pallas kernels, attend(): pl.pallas_call(attend_kernel, name='attend', grid=(parts, tokens // rows)...  43.9 us
    ppermute x24, starting transfers between devices, exchange(): lax.ppermute(pieces[k], 'z', [(i, i ^ k) for i in range(count)])  42.2 us
    ppermute x16, starting transfers between devices, start(): return [lax.ppermute(sent[0], 'z', swap_pairs(count, bit))]  41.5 us
  transfers between devices with their start and end apart: 129, of which 49 were waited for; matrix products, arithmetic and copies ran while one was open for 23% of the time, Pallas kernels for 13%

profile of v2, /device:TPU:0, one launch (start us, length us, event | category | flops | bytes accessed | tf_op | source)
XLA Modules:
  0.0 1006.7 jit_solution(15786631246450379443)
XLA Ops:
  31.6 9.9 all-gather.3
  54.8 10.3 %all-gather.10.cloned.1.call-done = bf16[1024,1536]{0,1:T(8,128)(2,1)} async-done(((bf16[256,1536]{0,1:T(8,128)(2,1)}), bf16[1024,1536]{0,1:T(8,128)(2,1)}) %all-gather.10.cloned.1.call-update) | async-done | bytes 3145744 | tf_op jit(solution)/shard_map/all_gather | solution.py:453
  65.1 5.5 add_convert_fusion.1
  94.9 6.3 collective-permute-done.5
  102.7 24.9 %collective-permute-done.4 = bf16[3,576,128]{2,1,0:T(8,128)(2,1)} collective-permute-done((bf16[3,576,128]{2,1,0:T(8,128)(2,1)}, bf16[3,576,128]{2,1,0:T(8,128)(2,1)}, u32[]{:S(2)}, u32[]{:S(2)}) %collective-permute-start.4) | collective-permute-done | bytes 442400 | tf_op jit(solution)/shard_map/ppermute | solution.py:204
  136.7 22.1 %attend.2 = (bf16[4,576,128]{2,1,0:T(8,128)(2,1)}, f32[4,576,128]{2,1,0:T(8,128)}) custom-call(bf16[4,3,576,128]{3,2,1,0:T(8,128)(2,1)} %pad_maximum_fusion.3.q_ref.k_ref.v_ref, bf16[4,3,576,128]{3,2,1,0:T(8,128)(2,1)} %pad_maximum_fusion.3.q_ref.k_ref.v_ref, bf16[4,3,576,128]{3,2,1,0:T(8,128)(2,1)} %pad_maximum_fusion.3.q_ref.k_ref.v_ref), custom_call_target="tpu_custom_call" | custom-call | flops 10871635968 | bytes 3538944 | tf_op jit(solution)/shard_map/attend/pallas_call | solution.py:92
  168.8 4.8 collective-permute-done.11
  178.8 22.4 %collective-permute-done.14 = bf16[2,256,768]{1,2,0:T(8,128)(2,1)S(1)} collective-permute-done((bf16[2,256,768]{1,2,0:T(8,128)(2,1)S(1)}, bf16[2,256,768]{1,2,0:T(8,128)(2,1)S(1)}, u32[]{:S(2)}, u32[]{:S(2)}) %collective-permute-start.14) | collective-permute-done | bytes 786464 | tf_op jit(solution)/shard_map/ppermute | solution.py:407
  205.0 7.9 multiply_convert_fusion.3
  212.9 5.1 fusion.16
  227.7 4.8 collective-permute-done.18
  237.6 11.0 %collective-permute-done.20 = bf16[2,128,512]{2,1,0:T(8,128)(2,1)S(1)} collective-permute-done((bf16[2,128,512]{2,1,0:T(8,128)(2,1)S(1)}, bf16[2,128,512]{2,1,0:T(8,128)(2,1)S(1)}, u32[]{:S(2)}, u32[]{:S(2)}) %collective-permute-start.20) | collective-permute-done | bytes 262176 | tf_op jit(solution)/shard_map/ppermute | solution.py:407
  255.2 5.5 add_convert_fusion
  273.7 10.5 %collective-permute-done.25 = bf16[3,576,128]{2,1,0:T(8,128)(2,1)S(1)} collective-permute-done((bf16[3,576,128]{2,1,0:T(8,128)(2,1)S(1)}, bf16[3,576,128]{2,1,0:T(8,128)(2,1)S(1)}, u32[]{:S(2)}, u32[]{:S(2)}) %collective-permute-start.25) | collective-permute-done | bytes 442400 | tf_op jit(solution)/shard_map/ppermute | solution.py:204
  284.1 26.4 %collective-permute-done.24 = bf16[3,576,128]{2,1,0:T(8,128)(2,1)S(1)} collective-permute-done((bf16[3,576,128]{2,1,0:T(8,128)(2,1)S(1)}, bf16[3,576,128]{2,1,0:T(8,128)(2,1)S(1)}, u32[]{:S(2)}, u32[]{:S(2)}) %collective-permute-start.24) | collective-permute-done | bytes 442400 | tf_op jit(solution)/shard_map/ppermute | solution.py:204
  312.0 21.8 %attend.3 = (bf16[4,576,128]{2,1,0:T(8,128)(2,1)}, f32[4,576,128]{2,1,0:T(8,128)}) custom-call(bf16[4,3,576,128]{3,2,1,0:T(8,128)(2,1)} %pad_maximum_fusion.4.q_ref.k_ref.v_ref, bf16[4,3,576,128]{3,2,1,0:T(8,128)(2,1)} %pad_maximum_fusion.4.q_ref.k_ref.v_ref, bf16[4,3,576,128]{3,2,1,0:T(8,128)(2,1)} %pad_maximum_fusion.4.q_ref.k_ref.v_ref), custom_call_target="tpu_custom_call" | custom-call | flops 10871635968 | bytes 3538944 | tf_op jit(solution)/shard_map/attend/pallas_call | solution.py:92
  343.6 5.0 collective-permute-done.27
  358.0 7.0 multiply_convert_fusion.2
  365.0 8.1 multiply_convert_fusion.1
  373.0 6.3 convolution_convert_fusion.5
  379.4 5.1 fusion.185
  399.6 6.3 convolution_convert_fusion.4
  410.9 32.9 %attend_back.2 = bf16[4,3,576,128]{3,2,1,0:T(8,128)(2,1)} custom-call(bf16[4,3,576,128]{3,2,1,0:T(8,128)(2,1)} %pad_maximum_fusion.4.q_ref.k_ref.v_ref, bf16[4,3,576,128]{3,2,1,0:T(8,128)(2,1)} %pad_maximum_fusion.4.q_ref.k_ref.v_ref, bf16[4,3,576,128]{3,2,1,0:T(8,128)(2,1)} %pad_maximum_fusion.4.q_ref.k_ref.v_ref, ...), custom_call_target="tpu_custom_call" | custom-call | flops 27179089920 | bytes 5898240 | tf_op jit(solution)/shard_map/attend_back/pallas_call | solution.py:163
  455.0 26.1 %collective-permute-done.40 = bf16[3,576,128]{2,1,0:T(8,128)(2,1)} collective-permute-done((bf16[3,576,128]{2,1,0:T(8,128)(2,1)}, bf16[3,576,128]{2,1,0:T(8,128)(2,1)}, u32[]{:S(2)}, u32[]{:S(2)}) %collective-permute-start.40) | collective-permute-done | bytes 442400 | tf_op jit(solution)/shard_map/ppermute | solution.py:204
  481.1 7.0 collective-permute-done.39
  488.1 8.2 collective-permute-done.38
  505.4 4.9 fusion.32
  515.6 6.2 convolution_convert_fusion.1
  534.8 19.2 %collective-permute-start.46 = (bf16[256,2048]{1,0:T(8,128)(2,1)S(1)}, bf16[256,2048]{1,0:T(8,128)(2,1)S(1)}, u32[]{:S(2)}, u32[]{:S(2)}) collective-permute-start(bf16[256,2048]{1,0:T(8,128)(2,1)S(1)} %copy-done.6), channel_id=1, source_target_pairs={{0,8},{24,16},{1,9},{25,17},{2,10},{26,18},{3,11},{27,19},{4,12},{... | collective-permute-start | bytes 3145736 | tf_op jit(solution)/shard_map/ppermute | solution.py:369
  553.9 5.4 convolution_convert_fusion.3
  563.4 6.3 multiply_convert_fusion
  602.9 23.6 %collective-permute-done.53 = f32[4,384]{1,0:T(4,128)S(1)} collective-permute-done((f32[4,384]{1,0:T(4,128)S(1)}, f32[4,384]{1,0:T(4,128)S(1)}, u32[]{:S(2)}, u32[]{:S(2)}) %collective-permute-start.53) | collective-permute-done | bytes 6176 | tf_op jit(solution)/shard_map/ppermute | solution.py:346
  649.1 5.6 collective-permute-start.57
  659.6 11.6 %collective-permute-done.57 = bf16[576,128]{1,0:T(8,128)(2,1)S(1)} collective-permute-done((bf16[576,128]{1,0:T(8,128)(2,1)S(1)}, bf16[576,128]{1,0:T(8,128)(2,1)S(1)}, u32[]{:S(2)}, u32[]{:S(2)}) %collective-permute-start.57) | collective-permute-done | bytes 147488 | tf_op jit(solution)/shard_map/ppermute | solution.py:204
  679.9 6.9 collective-permute-start.68
  688.4 32.6 %attend_back.3 = bf16[4,3,576,128]{3,2,1,0:T(8,128)(2,1)} custom-call(bf16[4,3,576,128]{3,2,1,0:T(8,128)(2,1)} %pad_maximum_fusion.3.q_ref.k_ref.v_ref, bf16[4,3,576,128]{3,2,1,0:T(8,128)(2,1)} %pad_maximum_fusion.3.q_ref.k_ref.v_ref, bf16[4,3,576,128]{3,2,1,0:T(8,128)(2,1)} %pad_maximum_fusion.3.q_ref.k_ref.v_ref, ...), custom_call_target="tpu_custom_call" | custom-call | flops 27179089920 | bytes 5898240 | tf_op jit(solution)/shard_map/attend_back/pallas_call | solution.py:163
  749.8 22.6 %collective-permute-done.72 = bf16[3,576,128]{2,1,0:T(8,128)(2,1)S(1)} collective-permute-done((bf16[3,576,128]{2,1,0:T(8,128)(2,1)}, bf16[3,576,128]{2,1,0:T(8,128)(2,1)S(1)}, u32[]{:S(2)}, u32[]{:S(2)}) %collective-permute-start.72) | collective-permute-done | bytes 442400 | tf_op jit(solution)/shard_map/ppermute | solution.py:204
  779.9 6.3 collective-permute-done.74
  841.4 15.4 %collective-permute-done.95 = f32[2,4,384]{2,1,0:T(4,128)} collective-permute-done((f32[2,4,384]{2,1,0:T(4,128)S(1)}, f32[2,4,384]{2,1,0:T(4,128)}, u32[]{:S(2)}, u32[]{:S(2)}) %collective-permute-start.95) | collective-permute-done | bytes 12320 | tf_op jit(solution)/shard_map/ppermute | solution.py:346
  857.9 12.4 %collective-permute-start.89 = (bf16[256,1024]{1,0:T(8,128)(2,1)}, bf16[256,1024]{1,0:T(8,128)(2,1)}, u32[]{:S(2)}, u32[]{:S(2)}) collective-permute-start(bf16[256,1024]{1,0:T(8,128)(2,1)} %pad_maximum_fusion.52), channel_id=1, source_target_pairs={{0,8},{8,0},{16,24},{24,16},{1,9},{9,1},{17,25},{25,17},{2,10},{10... | collective-permute-start | bytes 1572872 | tf_op jit(solution)/shard_map/ppermute | solution.py:391
  880.3 9.4 collective-permute-done.90
  909.8 11.8 %collective-permute-done.99 = bf16[64,2048]{1,0:T(8,128)(2,1)S(1)} collective-permute-done((bf16[64,2048]{1,0:T(8,128)(2,1)S(1)}, bf16[64,2048]{1,0:T(8,128)(2,1)S(1)}, u32[]{:S(2)}, u32[]{:S(2)}) %collective-permute-start.99) | collective-permute-done | bytes 262176 | tf_op jit(solution)/shard_map/ppermute | solution.py:391
  930.0 8.9 join_rows.2
  938.9 5.6 collective-permute-done.108
  950.8 11.7 %collective-permute-done.110 = bf16[32,1024]{1,0:T(8,128)(2,1)S(1)} collective-permute-done((bf16[32,1024]{1,0:T(8,128)(2,1)S(1)}, bf16[32,1024]{1,0:T(8,128)(2,1)S(1)}, u32[]{:S(2)}, u32[]{:S(2)}) %collective-permute-start.110) | collective-permute-done | bytes 65568 | tf_op jit(solution)/shard_map/ppermute | solution.py:391
  970.6 6.0 join_columns.2
  980.5 8.0 collective-permute-done.117
  994.2 5.5 join_columns.3
  (956 shorter events, 431.9 us)
Async XLA Ops:
  7.2 58.0 %all-gather.10.cloned.1.call-start = ((), (), s32[]{:S(2)}) async-start(), calls=%async_computation.4 | async-start | bytes 3932160 | tf_op jit(solution)/shard_map/all_gather | solution.py:453
  15.5 187.7 %all-gather.12.cloned.1.call-start = ((), (), s32[]{:S(2)}) async-start(), calls=%async_computation.5 | async-start | bytes 5242880 | tf_op jit(solution)/shard_map/all_gather | solution.py:453
  25.9 187.0 %all-gather.16.cloned.1.call-start = ((), (), s32[]{:S(2)}) async-start(), calls=%async_computation.11 | async-start | bytes 5242880 | tf_op jit(solution)/shard_map/all_gather | solution.py:453
  31.4 324.8 %all-gather.14.cloned.1.call-start = ((), (), s32[]{:S(2)}) async-start(), calls=%async_computation.6 | async-start | bytes 5242880 | tf_op jit(solution)/shard_map/all_gather | solution.py:453
  46.0 35.4 %collective-permute-start.1 = (bf16[128,512]{1,0:T(8,128)(2,1)}, bf16[128,512]{1,0:T(8,128)(2,1)}, u32[]{:S(2)}, u32[]{:S(2)}) collective-permute-start(bf16[128,512]{1,0:T(8,128)(2,1)} %get-tuple-element.219), channel_id=1, source_target_pairs={{0,1},{1,0},{2,3},{3,2},{4,5},{5,4},{6,7},{7,6},{8,9},{9,8},{10,11... | collective-permute-start | bytes 393224 | tf_op jit(solution)/shard_map/ppermute | solution.py:407
  47.5 34.0 %collective-permute-start.2 = (bf16[128,512]{1,0:T(8,128)(2,1)}, bf16[128,512]{1,0:T(8,128)(2,1)}, u32[]{:S(2)}, u32[]{:S(2)}) collective-permute-start(bf16[128,512]{1,0:T(8,128)(2,1)} %get-tuple-element.220), channel_id=1, source_target_pairs={{0,2},{1,3},{2,0},{3,1},{4,6},{5,7},{6,4},{7,5},{8,10},{9,11},{10,... | collective-permute-start | bytes 393224 | tf_op jit(solution)/shard_map/ppermute | solution.py:407
  89.3 38.3 %collective-permute-start.4 = (bf16[3,576,128]{2,1,0:T(8,128)(2,1)}, bf16[3,576,128]{2,1,0:T(8,128)(2,1)}, u32[]{:S(2)}, u32[]{:S(2)}) collective-permute-start(bf16[3,576,128]{2,1,0:T(8,128)(2,1)} %get-tuple-element.478), channel_id=1, source_target_pairs={{0,16},{8,24},{16,0},{24,8},{1,17},{9,25},{17,1},{25,9},{2,18},{10... | collective-permute-start | bytes 1327112 | tf_op jit(solution)/shard_map/ppermute | solution.py:204
  89.3 42.4 %collective-permute-start.3 = (bf16[3,576,128]{2,1,0:T(8,128)(2,1)}, bf16[3,576,128]{2,1,0:T(8,128)(2,1)}, u32[]{:S(2)}, u32[]{:S(2)}) collective-permute-start(bf16[3,576,128]{2,1,0:T(8,128)(2,1)} %get-tuple-element.479), channel_id=1, source_target_pairs={{0,8},{8,0},{16,24},{24,16},{1,9},{9,1},{17,25},{25,17},{2,10},{10... | collective-permute-start | bytes 1327112 | tf_op jit(solution)/shard_map/ppermute | solution.py:204
  90.3 44.8 %collective-permute-start.8 = (bf16[256,768]{0,1:T(8,128)(2,1)}, bf16[256,768]{0,1:T(8,128)(2,1)}, u32[]{:S(2)}, u32[]{:S(2)}) collective-permute-start(bf16[256,768]{0,1:T(8,128)(2,1)} %get-tuple-element.227), channel_id=1, source_target_pairs={{0,1},{1,0},{2,3},{3,2},{4,5},{5,4},{6,7},{7,6},{8,9},{9,8},{10,11... | collective-permute-start | bytes 1179656 | tf_op jit(solution)/shard_map/ppermute | solution.py:407
  91.8 43.4 %collective-permute-start.9 = (bf16[256,768]{0,1:T(8,128)(2,1)}, bf16[256,768]{0,1:T(8,128)(2,1)}, u32[]{:S(2)}, u32[]{:S(2)}) collective-permute-start(bf16[256,768]{0,1:T(8,128)(2,1)} %get-tuple-element.228), channel_id=1, source_target_pairs={{0,2},{1,3},{2,0},{3,1},{4,6},{5,7},{6,4},{7,5},{8,10},{9,11},{10,... | collective-permute-start | bytes 1179656 | tf_op jit(solution)/shard_map/ppermute | solution.py:407
  101.2 33.3 %collective-permute-start.6 = (bf16[2,128,512]{2,1,0:T(8,128)(2,1)}, bf16[2,128,512]{2,1,0:T(8,128)(2,1)S(1)}, u32[]{:S(2)}, u32[]{:S(2)}) collective-permute-start(bf16[2,128,512]{2,1,0:T(8,128)(2,1)} %pad_maximum_fusion.55), channel_id=1, source_target_pairs={{0,2},{1,3},{2,0},{3,1},{4,6},{5,7},{6,4},{7,5},{8,10},{9,11},{10,... | collective-permute-start | bytes 786440 | tf_op jit(solution)/shard_map/ppermute | solution.py:407
  131.4 233.6 %all-gather.18.cloned.1.call-start = ((), (), s32[]{:S(2)}) async-start(), calls=%async_computation.12 | async-start | bytes 5242880 | tf_op jit(solution)/shard_map/all_gather | solution.py:453
  222.1 221.7 %reduce-scatter.5.cloned.1.call-start = ((), (), s32[]{:S(2)}) async-start(), calls=%async_computation.7 | async-start | bytes 5242880 | tf_op jit(solution)/shard_map/reduce_scatter | solution.py:356
  272.5 38.0 %collective-permute-start.24 = (bf16[3,576,128]{2,1,0:T(8,128)(2,1)S(1)}, bf16[3,576,128]{2,1,0:T(8,128)(2,1)S(1)}, u32[]{:S(2)}, u32[]{:S(2)}) collective-permute-start(bf16[3,576,128]{2,1,0:T(8,128)(2,1)S(1)} %get-tuple-element.474), channel_id=1, source_target_pairs={{0,16},{8,24},{16,0},{24,8},{1,17},{9,25},{17,1},{25,9},{2,18},{10... | collective-permute-start | bytes 1327112 | tf_op jit(solution)/shard_map/ppermute | solution.py:204
  272.5 38.0 %collective-permute-start.23 = (bf16[3,576,128]{2,1,0:T(8,128)(2,1)S(1)}, bf16[3,576,128]{2,1,0:T(8,128)(2,1)S(1)}, u32[]{:S(2)}, u32[]{:S(2)}) collective-permute-start(bf16[3,576,128]{2,1,0:T(8,128)(2,1)S(1)} %get-tuple-element.475), channel_id=1, source_target_pairs={{0,8},{8,0},{16,24},{24,16},{1,9},{9,1},{17,25},{25,17},{2,10},{10... | collective-permute-start | bytes 1327112 | tf_op jit(solution)/shard_map/ppermute | solution.py:204
  379.4 147.7 %reduce-scatter.7.cloned.1.call-start = ((), (), s32[]{:S(2)}) async-start(), calls=%async_computation.8 | async-start | bytes 5242880 | tf_op jit(solution)/shard_map/reduce_scatter | solution.py:356
  410.9 217.2 %reduce-scatter.9.cloned.1.call-start = ((), (), s32[]{:S(2)}) async-start(), calls=%async_computation.9 | async-start | bytes 1310720 | tf_op jit(solution)/shard_map/reduce_scatter | solution.py:356
  443.8 54.2 %collective-permute-start.41 = (bf16[512,1024]{1,0:T(8,128)(2,1)}, bf16[512,1024]{1,0:T(8,128)(2,1)S(1)}, u32[]{:S(2)}, u32[]{:S(2)}) collective-permute-start(bf16[512,1024]{1,0:T(8,128)(2,1)} %reduce-scatter.5.cloned.1.call-done), channel_id=1, source_target_pairs={{0,8},{24,16},{1,9},{25,17},{2,10},{26,18},{3,11},{27,19},{4,12},{... | collective-permute-start | bytes 3145736 | tf_op jit(solution)/shard_map/ppermute | solution.py:369
  448.6 32.5 %collective-permute-start.40 = (bf16[3,576,128]{2,1,0:T(8,128)(2,1)}, bf16[3,576,128]{2,1,0:T(8,128)(2,1)}, u32[]{:S(2)}, u32[]{:S(2)}) collective-permute-start(bf16[3,576,128]{2,1,0:T(8,128)(2,1)} %get-tuple-element.469), channel_id=1, source_target_pairs={{0,24},{8,16},{16,8},{24,0},{1,25},{9,17},{17,9},{25,1},{2,26},{10... | collective-permute-start | bytes 1327112 | tf_op jit(solution)/shard_map/ppermute | solution.py:204
  450.6 37.5 %collective-permute-start.39 = (bf16[3,576,128]{2,1,0:T(8,128)(2,1)}, bf16[3,576,128]{2,1,0:T(8,128)(2,1)}, u32[]{:S(2)}, u32[]{:S(2)}) collective-permute-start(bf16[3,576,128]{2,1,0:T(8,128)(2,1)} %get-tuple-element.470), channel_id=1, source_target_pairs={{0,16},{8,24},{16,0},{24,8},{1,17},{9,25},{17,1},{25,9},{2,18},{10... | collective-permute-start | bytes 1327112 | tf_op jit(solution)/shard_map/ppermute | solution.py:204
  450.6 45.7 %collective-permute-start.38 = (bf16[3,576,128]{2,1,0:T(8,128)(2,1)S(1)}, bf16[3,576,128]{2,1,0:T(8,128)(2,1)}, u32[]{:S(2)}, u32[]{:S(2)}) collective-permute-start(bf16[3,576,128]{2,1,0:T(8,128)(2,1)S(1)} %get-tuple-element.471), channel_id=1, source_target_pairs={{0,8},{8,0},{16,24},{24,16},{1,9},{9,1},{17,25},{25,17},{2,10},{10... | collective-permute-start | bytes 1327112 | tf_op jit(solution)/shard_map/ppermute | solution.py:204
  531.4 39.5 %collective-permute-start.47 = (f32[2,4,384]{2,1,0:T(4,128)S(1)}, f32[2,4,384]{2,1,0:T(4,128)S(1)}, u32[]{:S(2)}, u32[]{:S(2)}) collective-permute-start(f32[2,4,384]{2,1,0:T(4,128)S(1)} %fusion.108), channel_id=1, source_target_pairs={{0,2},{1,3},{2,0},{3,1},{4,6},{5,7},{6,4},{7,5},{8,10},{9,11},{10,... | collective-permute-start | bytes 36872 | tf_op jit(solution)/shard_map/ppermute | solution.py:346
  532.6 38.3 %collective-permute-start.48 = (f32[2,4,384]{2,1,0:T(4,128)S(1)}, f32[2,4,384]{2,1,0:T(4,128)S(1)}, u32[]{:S(2)}, u32[]{:S(2)}) collective-permute-start(f32[2,4,384]{2,1,0:T(4,128)S(1)} %fusion.109), channel_id=1, source_target_pairs={{0,1},{1,0},{2,3},{3,2},{4,5},{5,4},{6,7},{7,6},{8,9},{9,8},{10,11... | collective-permute-start | bytes 36872 | tf_op jit(solution)/shard_map/ppermute | solution.py:346
  533.5 41.5 %collective-permute-start.45 = (bf16[512,1024]{1,0:T(8,128)(2,1)}, bf16[512,1024]{1,0:T(8,128)(2,1)S(1)}, u32[]{:S(2)}, u32[]{:S(2)}) collective-permute-start(bf16[512,1024]{1,0:T(8,128)(2,1)} %fusion.22), channel_id=1, source_target_pairs={{16,24},{8,0},{17,25},{9,1},{18,26},{10,2},{19,27},{11,3},{20,28},... | collective-permute-start | bytes 3145736 | tf_op jit(solution)/shard_map/ppermute | solution.py:369
  534.8 41.2 %collective-permute-start.46 = (bf16[256,2048]{1,0:T(8,128)(2,1)S(1)}, bf16[256,2048]{1,0:T(8,128)(2,1)S(1)}, u32[]{:S(2)}, u32[]{:S(2)}) collective-permute-start(bf16[256,2048]{1,0:T(8,128)(2,1)S(1)} %copy-done.6), channel_id=1, source_target_pairs={{0,8},{24,16},{1,9},{25,17},{2,10},{26,18},{3,11},{27,19},{4,12},{... | collective-permute-start | bytes 3145736 | tf_op jit(solution)/shard_map/ppermute | solution.py:369
  586.3 137.0 %reduce-scatter.11.cloned.1.call-start = ((), (), s32[]{:S(2)}) async-start(), calls=%async_computation.10 | async-start | bytes 3932160 | tf_op jit(solution)/shard_map/reduce_scatter | solution.py:356
  593.6 36.6 %collective-permute-start.51 = (bf16[512,1024]{1,0:T(8,128)(2,1)}, bf16[512,1024]{1,0:T(8,128)(2,1)}, u32[]{:S(2)}, u32[]{:S(2)}) collective-permute-start(bf16[512,1024]{1,0:T(8,128)(2,1)} %fusion.24.refs_2_), channel_id=1, source_target_pairs={{0,4},{4,0},{1,5},{5,1},{2,6},{6,2},{3,7},{7,3},{8,12},{12,8},{9,1... | collective-permute-start | bytes 3145736 | tf_op jit(solution)/shard_map/ppermute | solution.py:209
  593.9 36.2 %collective-permute-start.52 = (bf16[256,2048]{1,0:T(8,128)(2,1)}, bf16[256,2048]{1,0:T(8,128)(2,1)}, u32[]{:S(2)}, u32[]{:S(2)}) collective-permute-start(bf16[256,2048]{1,0:T(8,128)(2,1)} %fusion.34), channel_id=1, source_target_pairs={{8,16},{16,8},{9,17},{17,9},{10,18},{18,10},{11,19},{19,11},{12,20... | collective-permute-start | bytes 3145736 | tf_op jit(solution)/shard_map/ppermute | solution.py:369
  595.8 34.4 %collective-permute-start.55 = (bf16[2,512,512]{2,1,0:T(8,128)(2,1)}, bf16[2,512,512]{2,1,0:T(8,128)(2,1)}, u32[]{:S(2)}, u32[]{:S(2)}) collective-permute-start(bf16[2,512,512]{2,1,0:T(8,128)(2,1)} %dynamic-slice_bitcast_fusion.3), channel_id=1, source_target_pairs={{0,2},{1,3},{2,0},{3,1},{4,6},{5,7},{6,4},{7,5},{8,10},{9,11},{10,... | collective-permute-start | bytes 3145736 | tf_op jit(solution)/shard_map/ppermute | solution.py:346
  597.0 33.1 %collective-permute-start.56 = (bf16[2,512,512]{2,1,0:T(8,128)(2,1)}, bf16[2,512,512]{2,1,0:T(8,128)(2,1)}, u32[]{:S(2)}, u32[]{:S(2)}) collective-permute-start(bf16[2,512,512]{2,1,0:T(8,128)(2,1)} %dynamic-slice_bitcast_fusion.2), channel_id=1, source_target_pairs={{0,1},{1,0},{2,3},{3,2},{4,5},{5,4},{6,7},{7,6},{8,9},{9,8},{10,11... | collective-permute-start | bytes 3145736 | tf_op jit(solution)/shard_map/ppermute | solution.py:346
  599.3 27.2 %collective-permute-start.53 = (f32[4,384]{1,0:T(4,128)S(1)}, f32[4,384]{1,0:T(4,128)S(1)}, u32[]{:S(2)}, u32[]{:S(2)}) collective-permute-start(f32[4,384]{1,0:T(4,128)S(1)} %fusion.120), channel_id=1, source_target_pairs={{0,1},{1,0},{2,3},{3,2},{4,5},{5,4},{6,7},{7,6},{8,9},{9,8},{10,11... | collective-permute-start | bytes 18440 | tf_op jit(solution)/shard_map/ppermute | solution.py:346
  635.5 38.5 %collective-permute-start.60 = (bf16[256,2048]{1,0:T(8,128)(2,1)S(1)}, bf16[256,2048]{1,0:T(8,128)(2,1)S(1)}, u32[]{:S(2)}, u32[]{:S(2)}) collective-permute-start(bf16[256,2048]{1,0:T(8,128)(2,1)S(1)} %fusion.25), channel_id=1, source_target_pairs={{16,24},{8,0},{17,25},{9,1},{18,26},{10,2},{19,27},{11,3},{20,28},... | collective-permute-start | bytes 3145736 | tf_op jit(solution)/shard_map/ppermute | solution.py:369
  645.1 28.9 %collective-permute-start.63 = (bf16[512,512]{1,0:T(8,128)(2,1)S(1)}, bf16[512,512]{1,0:T(8,128)(2,1)S(1)}, u32[]{:S(2)}, u32[]{:S(2)}) collective-permute-start(bf16[512,512]{1,0:T(8,128)(2,1)S(1)} %dynamic-slice_bitcast_fusion.13), channel_id=1, source_target_pairs={{0,1},{1,0},{2,3},{3,2},{4,5},{5,4},{6,7},{7,6},{8,9},{9,8},{10,11... | collective-permute-start | bytes 1572872 | tf_op jit(solution)/shard_map/ppermute | solution.py:346
  646.3 27.7 %collective-permute-start.64 = (bf16[512,512]{1,0:T(8,128)(2,1)S(1)}, bf16[512,512]{1,0:T(8,128)(2,1)S(1)}, u32[]{:S(2)}, u32[]{:S(2)}) collective-permute-start(bf16[512,512]{1,0:T(8,128)(2,1)S(1)} %dynamic-slice_bitcast_fusion.12), channel_id=1, source_target_pairs={{0,2},{1,3},{2,0},{3,1},{4,6},{5,7},{6,4},{7,5},{8,10},{9,11},{10,... | collective-permute-start | bytes 1572872 | tf_op jit(solution)/shard_map/ppermute | solution.py:346
  679.0 42.0 %collective-permute-start.66 = (bf16[128,1024]{1,0:T(8,128)(2,1)S(1)}, bf16[128,1024]{1,0:T(8,128)(2,1)S(1)}, u32[]{:S(2)}, u32[]{:S(2)}) collective-permute-start(bf16[128,1024]{1,0:T(8,128)(2,1)S(1)} %fusion.100), channel_id=1, source_target_pairs={{8,16},{16,8},{9,17},{17,9},{10,18},{18,10},{11,19},{19,11},{12,20... | collective-permute-start | bytes 786440 | tf_op jit(solution)/shard_map/ppermute | solution.py:369
  679.9 41.2 %collective-permute-start.68 = (bf16[256,1024]{1,0:T(8,128)(2,1)}, bf16[256,1024]{1,0:T(8,128)(2,1)S(1)}, u32[]{:S(2)}, u32[]{:S(2)}) collective-permute-start(bf16[256,1024]{1,0:T(8,128)(2,1)} %dynamic-slice_bitcast_fusion.11), channel_id=1, source_target_pairs={{0,8},{8,0},{16,24},{24,16},{1,9},{9,1},{17,25},{25,17},{2,10},{10... | collective-permute-start | bytes 1572872 | tf_op jit(solution)/shard_map/ppermute | solution.py:383
  686.7 34.3 %collective-permute-start.65 = (bf16[256,2048]{1,0:T(8,128)(2,1)S(1)}, bf16[256,2048]{1,0:T(8,128)(2,1)S(1)}, u32[]{:S(2)}, u32[]{:S(2)}) collective-permute-start(bf16[256,2048]{1,0:T(8,128)(2,1)S(1)} %fusion.27.refs_2_), channel_id=1, source_target_pairs={{0,4},{4,0},{1,5},{5,1},{2,6},{6,2},{3,7},{7,3},{8,12},{12,8},{9,1... | collective-permute-start | bytes 3145736 | tf_op jit(solution)/shard_map/ppermute | solution.py:209
  686.7 35.4 %collective-permute-start.69 = (bf16[2,256,1024]{2,1,0:T(8,128)(2,1)}, bf16[2,256,1024]{2,1,0:T(8,128)(2,1)S(1)}, u32[]{:S(2)}, u32[]{:S(2)}) collective-permute-start(bf16[2,256,1024]{2,1,0:T(8,128)(2,1)} %dynamic-slice_bitcast_fusion.1), channel_id=1, source_target_pairs={{0,2},{1,3},{2,0},{3,1},{4,6},{5,7},{6,4},{7,5},{8,10},{9,11},{10,... | collective-permute-start | bytes 3145736 | tf_op jit(solution)/shard_map/ppermute | solution.py:346
  687.5 35.8 %collective-permute-start.70 = (bf16[2,256,1024]{2,1,0:T(8,128)(2,1)}, bf16[2,256,1024]{2,1,0:T(8,128)(2,1)}, u32[]{:S(2)}, u32[]{:S(2)}) collective-permute-start(bf16[2,256,1024]{2,1,0:T(8,128)(2,1)} %dynamic-slice_bitcast_fusion), channel_id=1, source_target_pairs={{0,1},{1,0},{2,3},{3,2},{4,5},{5,4},{6,7},{7,6},{8,9},{9,8},{10,11... | collective-permute-start | bytes 3145736 | tf_op jit(solution)/shard_map/ppermute | solution.py:346
  737.9 34.4 %collective-permute-start.72 = (bf16[3,576,128]{2,1,0:T(8,128)(2,1)}, bf16[3,576,128]{2,1,0:T(8,128)(2,1)S(1)}, u32[]{:S(2)}, u32[]{:S(2)}) collective-permute-start(bf16[3,576,128]{2,1,0:T(8,128)(2,1)} %get-tuple-element.466), channel_id=1, source_target_pairs={{0,16},{8,24},{16,0},{24,8},{1,17},{9,25},{17,1},{25,9},{2,18},{10... | collective-permute-start | bytes 1327112 | tf_op jit(solution)/shard_map/ppermute | solution.py:204
  740.1 33.7 %collective-permute-start.71 = (bf16[3,576,128]{2,1,0:T(8,128)(2,1)}, bf16[3,576,128]{2,1,0:T(8,128)(2,1)S(1)}, u32[]{:S(2)}, u32[]{:S(2)}) collective-permute-start(bf16[3,576,128]{2,1,0:T(8,128)(2,1)} %get-tuple-element.467), channel_id=1, source_target_pairs={{0,8},{8,0},{16,24},{24,16},{1,9},{9,1},{17,25},{25,17},{2,10},{10... | collective-permute-start | bytes 1327112 | tf_op jit(solution)/shard_map/ppermute | solution.py:204
  740.7 48.0 %collective-permute-start.75 = (bf16[256,1536]{1,0:T(8,128)(2,1)S(1)}, bf16[256,1536]{1,0:T(8,128)(2,1)S(1)}, u32[]{:S(2)}, u32[]{:S(2)}) collective-permute-start(bf16[256,1536]{1,0:T(8,128)(2,1)S(1)} %copy-done.12), channel_id=1, source_target_pairs={{0,8},{24,16},{1,9},{25,17},{2,10},{26,18},{3,11},{27,19},{4,12},{... | collective-permute-start | bytes 2359304 | tf_op jit(solution)/shard_map/ppermute | solution.py:369
  746.4 42.3 %collective-permute-start.78 = (bf16[256,1024]{1,0:T(8,128)(2,1)S(1)}, bf16[256,1024]{1,0:T(8,128)(2,1)S(1)}, u32[]{:S(2)}, u32[]{:S(2)}) collective-permute-start(bf16[256,1024]{1,0:T(8,128)(2,1)S(1)} %copy-done.120), channel_id=1, source_target_pairs={{0,1},{1,0},{2,3},{3,2},{4,5},{5,4},{6,7},{7,6},{8,9},{9,8},{10,11... | collective-permute-start | bytes 1572872 | tf_op jit(solution)/shard_map/ppermute | solution.py:346
  747.6 41.1 %collective-permute-start.79 = (bf16[256,1024]{1,0:T(8,128)(2,1)S(1)}, bf16[256,1024]{1,0:T(8,128)(2,1)S(1)}, u32[]{:S(2)}, u32[]{:S(2)}) collective-permute-start(bf16[256,1024]{1,0:T(8,128)(2,1)S(1)} %copy-done.119), channel_id=1, source_target_pairs={{0,2},{1,3},{2,0},{3,1},{4,6},{5,7},{6,4},{7,5},{8,10},{9,11},{10,... | collective-permute-start | bytes 1572872 | tf_op jit(solution)/shard_map/ppermute | solution.py:346
  835.7 54.1 %collective-permute-start.88 = (bf16[256,1536]{1,0:T(8,128)(2,1)}, bf16[256,1536]{1,0:T(8,128)(2,1)}, u32[]{:S(2)}, u32[]{:S(2)}) collective-permute-start(bf16[256,1536]{1,0:T(8,128)(2,1)} %fusion.39), channel_id=1, source_target_pairs={{16,24},{8,0},{17,25},{9,1},{18,26},{10,2},{19,27},{11,3},{20,28},... | collective-permute-start | bytes 2359304 | tf_op jit(solution)/shard_map/ppermute | solution.py:369
  837.3 52.5 %collective-permute-start.93 = (bf16[2,256,768]{2,1,0:T(8,128)(2,1)}, bf16[2,256,768]{2,1,0:T(8,128)(2,1)}, u32[]{:S(2)}, u32[]{:S(2)}) collective-permute-start(bf16[2,256,768]{2,1,0:T(8,128)(2,1)} %dynamic-slice_bitcast_fusion.5), channel_id=1, source_target_pairs={{0,2},{1,3},{2,0},{3,1},{4,6},{5,7},{6,4},{7,5},{8,10},{9,11},{10,... | collective-permute-start | bytes 2359304 | tf_op jit(solution)/shard_map/ppermute | solution.py:346
  838.5 51.3 %collective-permute-start.94 = (bf16[2,256,768]{2,1,0:T(8,128)(2,1)}, bf16[2,256,768]{2,1,0:T(8,128)(2,1)}, u32[]{:S(2)}, u32[]{:S(2)}) collective-permute-start(bf16[2,256,768]{2,1,0:T(8,128)(2,1)} %dynamic-slice_bitcast_fusion.4), channel_id=1, source_target_pairs={{0,1},{1,0},{2,3},{3,2},{4,5},{5,4},{6,7},{7,6},{8,9},{9,8},{10,11... | collective-permute-start | bytes 2359304 | tf_op jit(solution)/shard_map/ppermute | solution.py:346
  857.9 31.9 %collective-permute-start.89 = (bf16[256,1024]{1,0:T(8,128)(2,1)}, bf16[256,1024]{1,0:T(8,128)(2,1)}, u32[]{:S(2)}, u32[]{:S(2)}) collective-permute-start(bf16[256,1024]{1,0:T(8,128)(2,1)} %pad_maximum_fusion.52), channel_id=1, source_target_pairs={{0,8},{8,0},{16,24},{24,16},{1,9},{9,1},{17,25},{25,17},{2,10},{10... | collective-permute-start | bytes 1572872 | tf_op jit(solution)/shard_map/ppermute | solution.py:391
  (268 other events, 2413.2 us)
Sparse Core Ops, SparseCore 0:
  15.7 49.4 all-gather.9
  67.5 62.5 all-gather.11
  131.9 58.4 all-gather.15
  192.1 62.9 all-gather.13
  257.4 52.6 all-gather.17
  379.5 51.2 reduce-scatter.4
  434.5 52.6 reduce-scatter.6
  586.4 32.6 reduce-scatter.8
  623.0 46.6 reduce-scatter.10

commit v3 on v2

--- a/solution.py
+++ b/solution.py
@@ -12,6 +12,7 @@
 SCALE = HD ** (-0.5)
 F32 = jnp.float32
 BF16 = jnp.bfloat16
+LANES = 512
 VMEM_BYTES = 56 * 1024 * 1024
 
 
@@ -222,61 +223,50 @@
     return (left.astype(F32) + right.astype(F32)).astype(left.dtype)
 
 
-def join_columns_kernel(core_ref, *refs, moves):
+def merge(pieces):
+    blocks = [piece[:, start : start + LANES] for piece in pieces for start in range(0, piece.shape[1], LANES)]
+    return jnp.concatenate([block.astype(BF16) for block in blocks], axis=0)
+
+
+def join_kernel(core_ref, *refs, moves, count):
     out_ref = refs[-1]
-    core = core_ref[0]
     for layer in range(out_ref.shape[0]):
-        own_ref, other_ref = refs[2 * layer], refs[2 * layer + 1]
-        for half in range(2):
-            mine = core == half
-            for source, target, size in moves:
-                span = slice(source, source + size)
-                part = jnp.where(mine, own_ref[:, span], other_ref[:, span])
-                out_ref[layer, :, target[half] : target[half] + size] = part.astype(F32)
-
-
-def join_columns(pairs, core, moves):
-    rows, columns = pairs[0][0].shape
-    block = 64 if rows % 64 == 0 else rows
-    spec = pl.BlockSpec((block, columns), lambda i, core: (i, 0))
+        blocks = refs[2 * count * layer : 2 * count * (layer + 1)]
+        for half, source, target, size in moves:
+            mine = core_ref[0] == (pl.program_id(0) if half is None else half)
+            place, start = source // LANES, source % LANES
+            span = slice(start, start + size)
+            part = jnp.where(mine, blocks[place][:, span], blocks[count + place][:, span])
+            out_ref[layer, :, target : target + size] = part.astype(F32)
+
+
+def join(pairs, core, rows, columns, offsets, moves, by_rows):
+    count = columns // LANES
+    block = next(size for size in (64, 32, 16, 8) if rows % size == 0)
+    steps = rows // block
+    specs, operands = [], []
+    for pair, offset in zip(pairs, offsets):
+        for member in pair:
+            for place in range(count):
+                first = offset // block + place * steps
+                specs.append(pl.BlockSpec((block, LANES), lambda h, i, core, first=first: (first + i, 0)))
+                operands.append(member)
+    if by_rows:
+        grid, shape = (2, steps), (len(pairs), 2 * rows, columns)
+    else:
+        grid, shape = (1, steps), (len(pairs), rows, 2 * columns)
     return pl.pallas_call(
-        partial(join_columns_kernel, moves=moves),
-        name="join_columns",
+        partial(join_kernel, moves=moves, count=count),
+        name="join",
         grid_spec=pltpu.PrefetchScalarGridSpec(
             num_scalar_prefetch=1,
-            grid=(rows // block,),
-            in_specs=[spec] * (2 * len(pairs)),
-            out_specs=pl.BlockSpec((len(pairs), block, 2 * columns), lambda i, core: (0, i, 0)),
+            grid=grid,
+            in_specs=specs,
+            out_specs=pl.BlockSpec((len(pairs), block, shape[2]), lambda h, i, core: (0, h * steps + i, 0)),
         ),
-        out_shape=jax.ShapeDtypeStruct((len(pairs), rows, 2 * columns), F32),
+        out_shape=jax.ShapeDtypeStruct(shape, F32),
         compiler_params=pltpu.CompilerParams(vmem_limit_bytes=VMEM_BYTES),
-    )(core, *[part for pair in pairs for part in pair])
-
-
-def join_rows_kernel(core_ref, *refs):
-    out_ref = refs[-1]
-    mine = core_ref[0] == pl.program_id(0)
-    for layer in range(out_ref.shape[0]):
-        out_ref[layer] = jnp.where(mine, refs[2 * layer][...], refs[2 * layer + 1][...]).astype(F32)
-
-
-def join_rows(pairs, core):
-    rows, columns = pairs[0][0].shape
-    block = 128 if rows % 128 == 0 else rows
-    count = rows // block
-    spec = pl.BlockSpec((block, columns), lambda h, i, core: (i, 0))
-    return pl.pallas_call(
-        join_rows_kernel,
-        name="join_rows",
-        grid_spec=pltpu.PrefetchScalarGridSpec(
-            num_scalar_prefetch=1,
-            grid=(2, count),
-            in_specs=[spec] * (2 * len(pairs)),
-            out_specs=pl.BlockSpec((len(pairs), block, columns), lambda h, i, core: (0, h * count + i, 0)),
-        ),
-        out_shape=jax.ShapeDtypeStruct((len(pairs), 2 * rows, columns), F32),
-        compiler_params=pltpu.CompilerParams(vmem_limit_bytes=VMEM_BYTES),
-    )(core, *[part for pair in pairs for part in pair])
+    )(core, *operands)
 
 
 class Pipeline:
@@ -286,26 +276,30 @@
         self.fresh = {}
 
     def add(self, flow, finish):
-        self.running.append([flow, finish, None, None])
-
-    def advance(self, main):
+        self.running.append([flow, finish, None, ""])
+
+    def advance(self, main, point=None, last=False):
         due = []
         for item in self.running:
-            if item[2] is not None:
+            if isinstance(item[3], int):
                 item[3] -= 1
-            if item[2] is None or item[3] <= 0:
+            if item[2] is None or last or item[3] == 0 or item[3] == point:
                 due.append(item)
         flights = [item[2] for item in due]
         main, flights, fresh = lax.optimization_barrier((main, flights, self.fresh))
         self.finished.update(fresh)
         self.fresh = {}
         steps = []
-        for item, flight in zip(due, flights):
+        waiting = list(zip(due, flights))
+        while waiting:
+            item, flight = waiting.pop(0)
             try:
                 steps.append((item,) + item[0].send(flight))
             except StopIteration as stop:
+                self.running.remove(item)
+                known = len(self.running)
                 item[1](stop.value)
-                self.running.remove(item)
+                waiting += [(added, None) for added in self.running[known:]]
         sends = [step[1] for step in steps]
         main, sends = lax.optimization_barrier((main, sends))
         for (item, _, start, hold), values in zip(steps, sends):
@@ -314,7 +308,7 @@
 
     def drain(self):
         while self.running:
-            self.advance(())
+            self.advance((), last=True)
         self.finished.update(self.fresh)
 
 
@@ -330,7 +324,11 @@
     return lax.dynamic_index_in_dim(values, place, axis, keepdims=False)
 
 
-def scatter_flow(gradient, index, count):
+def pause(point):
+    yield [], lambda values: [], point
+
+
+def scatter_flow(gradient, index, count, points):
     bits = bit_count(count)
     half = gradient.shape[1] // 2
     lead = (2,) * bits + (gradient.shape[0] // count,)
@@ -346,56 +344,37 @@
                 lax.ppermute(value, "shard", swap_pairs(count, bit)) for value, (bit, _) in zip(values, places)
             ]
 
-        arrived = yield sends, start, 1
+        arrived = yield sends, start, points[min(step, len(points) - 1)]
         halves = [add_rounded(own, other) for own, other in zip(kept, arrived)]
     return jnp.concatenate(halves, axis=1)
 
 
-def offload_flow(gradient, hold):
+def offload_flow(gradient, point):
     def start(values):
         return [lax.psum_scatter(values[0], "shard", scatter_dimension=0, tiled=True)]
 
-    (piece,) = yield [gradient], start, hold
+    (piece,) = yield [gradient], start, point
     return piece
 
 
-def line_flow(piece, count):
+def line_flow(piece, count, points):
     total, carry = piece.astype(F32), None
     for step in range(1, count):
+        begin, point = points[step - 1] if step <= len(points) else ("", 1)
+        if begin:
+            yield from pause(begin)
         pairs = [(step - 1, step), (count - step, count - step - 1)]
         send = piece if carry is None else add_rounded(piece, carry)
 
         def start(values, pairs=pairs):
             return [lax.ppermute(values[0], "z", pairs)]
 
-        (carry,) = yield [send], start, 1
+        (carry,) = yield [send], start, point
         total = total + carry.astype(F32)
     return total.astype(piece.dtype)
 
 
-def halving_flow(values, index, count):
-    bits = bit_count(count)
-    for bit in range(bits):
-        upper = (index >> bit) & 1
-        halves = values.reshape((2, values.shape[0] // 2) + values.shape[1:])
-
-        def start(sent, bit=bit):
-            return [lax.ppermute(sent[0], "z", swap_pairs(count, bit))]
-
-        (other,) = yield [pick(halves, 1 - upper, 0)], start, 1
-        values = add_rounded(pick(halves, upper, 0), other)
-    for bit in reversed(range(bits)):
-        upper = ((index >> bit) & 1) == 1
-
-        def start(sent, bit=bit):
-            return [lax.ppermute(sent[0], "z", swap_pairs(count, bit))]
-
-        (other,) = yield [values], start, 1
-        values = jnp.concatenate([jnp.where(upper, other, values), jnp.where(upper, values, other)], axis=0)
-    return values
-
-
-def gather_flow(part, index, count):
+def gather_flow(part, index, count, holds):
     bits = bit_count(count)
     half = part.shape[1] // 2
     halves = [part[:, :half], part[:, half:]]
@@ -407,7 +386,7 @@
                 lax.ppermute(value, "shard", swap_pairs(count, bit)) for value, (bit, _) in zip(values, places)
             ]
 
-        arrived = yield halves, start, 1
+        arrived = yield halves, start, holds[min(step, len(holds) - 1)]
         for place, (bit, axis) in enumerate(places):
             upper, own, other = ((index >> bit) & 1) == 1, halves[place], arrived[place]
             halves[place] = jnp.stack([jnp.where(upper, other, own), jnp.where(upper, own, other)], axis=axis)
@@ -477,11 +456,11 @@
             held["qkv_part"] = qkv_part
         weights.append(held)
 
-    def fetch(layer, name):
+    def fetch(layer, name, holds=(1,)):
         def finish(full):
             weights[layer][name] = full
 
-        pipeline.add(gather_flow(weights[layer][name + "_part"], s_index, shards), finish)
+        pipeline.add(gather_flow(weights[layer][name + "_part"], s_index, shards, holds), finish)
 
     stream = images.astype(F32).reshape(-1, width)
     saved = []
@@ -506,12 +485,13 @@
         pieces = pipeline.advance(xor_order(pieces, z_index))
         packed = pipeline.advance(exchange(pieces))
         mixed, logs = attend(packed)
+        mixed = pipeline.advance(mixed)
         while "out" not in held:
             mixed = pipeline.advance(mixed)
         attended = xor_order(exchange(mixed), z_index).transpose(1, 0, 2).reshape(tokens, half_width)
         middle = stream + sum_with_partner(matmul(attended, held["out"])) + out_shift
         if layer + 1 < layers:
-            fetch(layer + 1, "out")
+            fetch(layer + 1, "out", (1, 3))
         middle = pipeline.advance(middle)
         two_own, average_two, inverse_two = norm_forward(middle, scale_two, shift_two)
         normed_two = with_partner(two_own)
@@ -551,42 +531,82 @@
         for start in range(0, half_width, cut):
             source = start // group * 3 * group + part * group + start % group
             target = part * width + start // block * 2 * block + start % block
-            qkv_moves.append((source, (target, target + block), cut))
+            qkv_moves += [(core_of, source, target + core_of * block, cut) for core_of in range(2)]
     block_up = hidden_units // 2 // shards
     up_moves = [
-        (place * block_up, (2 * place * block_up, (2 * place + 1) * block_up), block_up) for place in range(shards)
+        (core_of, place * block_up, (2 * place + core_of) * block_up, block_up)
+        for place in range(shards)
+        for core_of in range(2)
     ]
-
-    joins = {
-        "qkv": lambda pairs: join_columns(pairs, core, qkv_moves),
-        "up": lambda pairs: join_columns(pairs, core, up_moves),
-        "out": lambda pairs: join_rows(pairs, core),
-        "down": lambda pairs: join_rows(pairs, core),
-        "small": lambda pairs: jnp.stack([(own + other).reshape(-1) for own, other in pairs]),
+    row_moves = [(None, start, start, LANES) for start in range(0, width, LANES)]
+    local = width // shards
+    forms = {
+        "down": (hidden_units // 2 // shards, width, row_moves, True),
+        "up": (local, hidden_units // 2, up_moves, False),
+        "out": (half_width // shards, width, row_moves, True),
+        "qkv": (local, 3 * half_width, qkv_moves, False),
     }
-    weight_grads = [{} for _ in range(layers)]
-
-    def reduce_flow(gradient, offloaded, hold, halving):
-        if offloaded:
-            piece = yield from offload_flow(gradient, hold)
-        else:
-            piece = yield from scatter_flow(gradient, s_index, shards)
-        if halving:
-            piece = yield from halving_flow(piece, z_index, z_count)
-        else:
-            piece = yield from line_flow(piece, z_count)
-        (other,) = yield [piece], lambda values: [swap(values[0])], 1
-        return piece, other
-
-    def reduce_weight(layer, name, gradient, offloaded, hold=1, halving=False):
-        def finish(pair):
-            weight_grads[layer][name] = pair
-            if all(name in done for done in weight_grads):
-                pipeline.fresh[name] = joins[name]([done[name] for done in weight_grads])
-
+    small_rows = 64
+    groups = [
+        [("down",), ("up",)] + ([("out", "qkv"), ("small",)] if layer == 0 else [("out", "qkv", "small")])
+        for layer in range(layers)
+    ]
+
+    def line_points(layer, name):
+        if layer == 0:
+            return [("", "end0")] if name == "down" else []
+        end, later = f"end{layer}", f"end{layer - 1}"
+        b, c, d, e = [f"{kind}{layer - 1}" for kind in "bcde"]
+        return {
+            "down": [("", end), ("", b), (c, d)],
+            "up": [("", b), (c, d), (e, later)],
+            "out": [("", d), (e, later)],
+        }[name]
+
+    pieces_of = [{} for _ in range(layers)]
+    sums_of = [{} for _ in range(layers)]
+
+    def total_flow(merged, points):
+        merged = yield from line_flow(merged, z_count, points)
+        (other,) = yield [merged], lambda values: [swap(values[0])], 1
+        return merged, other
+
+    def arrived_in(layer, name, piece):
+        pieces_of[layer][name] = piece
+        for names in groups[layer]:
+            if name in names and all(member in pieces_of[layer] for member in names):
+                members = [pieces_of[layer][member] for member in names]
+                flow = total_flow(merge(members), line_points(layer, names[0]))
+                pipeline.add(flow, partial(summed, layer, names, [member.size // LANES for member in members]))
+
+    def summed(layer, names, extents, pair):
+        offset = 0
+        for name, extent in zip(names, extents):
+            sums_of[layer][name] = (pair, offset)
+            offset += extent
+            if all(name in sums for sums in sums_of):
+                pairs = [sums[name][0] for sums in sums_of]
+                starts = [sums[name][1] for sums in sums_of]
+                if name == "small":
+                    count = offsets[-1] // LANES
+                    pipeline.fresh[name] = jnp.stack(
+                        [
+                            sum(member[start : start + count].astype(F32) for member in pair).reshape(-1)
+                            for pair, start in zip(pairs, starts)
+                        ]
+                    )
+                else:
+                    rows, columns, moves, by_rows = forms[name]
+                    pipeline.fresh[name] = join(pairs, core, rows, columns, starts, moves, by_rows)
+
+    def reduce_weight(layer, name, gradient, points):
         if name != "small":
             gradient = gradient.astype(BF16)
-        pipeline.add(reduce_flow(gradient, offloaded, hold, halving), finish)
+        if isinstance(points, tuple):
+            flow = scatter_flow(gradient, s_index, shards, points)
+        else:
+            flow = offload_flow(gradient, points)
+        pipeline.add(flow, partial(arrived_in, layer, name))
 
     grad_stream = cotangent.astype(F32).reshape(-1, width)
     for layer in reversed(range(layers)):
@@ -609,13 +629,13 @@
             scale_two,
         ) = saved[layer]
         held = weights[layer]
-        offloaded = layer > 0
+        late = layer == 0
         branch_own = grad_stream.astype(BF16)
         branch_grad = with_partner(branch_own)
         grad_down_b = jnp.sum(branch_own.astype(F32), axis=0)
-        reduce_weight(layer, "down", outer_sum(hidden, branch_grad), offloaded, 3, not offloaded)
+        if not late:
+            reduce_weight(layer, "down", outer_sum(hidden, branch_grad), f"e{layer}")
         pre_grad = (times_transposed(branch_grad, held["down"]) * slope.astype(F32)).astype(BF16)
-        pre_grad = pipeline.advance(pre_grad)
         two_grad = sum_with_partner(times_transposed(pre_grad, held["up"]))
         grad_up_b = jnp.sum(pre_grad.astype(F32), axis=0)
         middle_back, grad_scale_two, grad_shift_two = norm_backward(
@@ -627,17 +647,24 @@
         grad_out_b = jnp.sum(out_own.astype(F32), axis=0)
         attended_grad = times_transposed(out_grad, held["out"]).astype(BF16)
         grad_pieces = attended_grad.reshape(tokens, z_count, group).transpose(1, 0, 2)
-        grad_pieces = pipeline.advance(xor_order(grad_pieces, z_index))
+        grad_pieces = pipeline.advance(xor_order(grad_pieces, z_index), f"b{layer}")
         head_grad = exchange(grad_pieces)
-        reduce_weight(layer, "up", outer_sum(normed_two, pre_grad), offloaded, 3, not offloaded)
-        head_grad = pipeline.advance(head_grad)
-        heads_back = pipeline.advance(attend_back(packed, mixed, head_grad, logs))
-        reduce_weight(layer, "out", outer_sum(attended, out_grad), offloaded, 3, not offloaded)
-        arrived = pipeline.advance(exchange(heads_back))
+        reduce_weight(layer, "up", outer_sum(normed_two, pre_grad), f"end{layer}")
+        if late:
+            reduce_weight(layer, "down", outer_sum(hidden, branch_grad), (f"d{layer}", f"e{layer}"))
+            reduce_weight(layer, "out", outer_sum(attended, out_grad), f"end{layer}")
+        head_grad = pipeline.advance(head_grad, f"c{layer}")
+        heads_back = pipeline.advance(attend_back(packed, mixed, head_grad, logs), f"d{layer}")
+        if not late:
+            reduce_weight(layer, "out", outer_sum(attended, out_grad), f"c{layer - 1}")
+        arrived = pipeline.advance(exchange(heads_back), f"e{layer}")
         projected_grad = xor_order(arrived, z_index).transpose(2, 0, 1, 3)
         projected_grad = projected_grad.reshape(tokens, 3 * half_width)
+        qkv_points = (f"end{layer}", 1) if late else f"c{layer - 1}"
+        reduce_weight(layer, "qkv", outer_sum(normed_one, projected_grad), qkv_points)
+        if late:
+            projected_grad = pipeline.advance(projected_grad, f"q{layer}")
         one_grad = sum_with_partner(times_transposed(projected_grad, held["qkv"]))
-        reduce_weight(layer, "qkv", outer_sum(normed_one, projected_grad), offloaded, 4, not offloaded)
         column_sums = jnp.sum(projected_grad.astype(F32), axis=0).reshape(z_count, 3, group)
         grad_qv_b = jnp.stack([column_sums[:, 0], column_sums[:, 2]])
         stream_back, grad_scale_one, grad_shift_one = norm_backward(
@@ -673,8 +700,9 @@
             ],
             axis=1,
         )
-        reduce_weight(layer, "small", small.reshape(4 * shards, -1), False)
-        grad_stream = pipeline.advance(grad_stream)
+        small = jnp.pad(small.reshape(shards, -1, LANES), ((0, 0), (0, small_rows - offsets[-1] // LANES), (0, 0)))
+        reduce_weight(layer, "small", small.reshape(-1, LANES), 1 if late else f"c{layer - 1}")
+        grad_stream = pipeline.advance(grad_stream, f"end{layer}")
 
     pipeline.drain()
     sums = pipeline.finished

time: 1020 us -> 922 us (0.904)
  starting transfers between devices: 174 us -> 121 us
  waiting for transfers between devices: 349 us -> 298 us
  other arithmetic: 102 us -> 120 us
  local copies, waits for them, and re-layouts: 116 us -> 99.4 us
    ppermute x18 -> x21, waiting for transfers between devices: 17.6 us -> 71.4 us  [start(): return [lax.ppermute(values[0], 'z', pairs)]]
    ppermute x16 -> x0, waiting for transfers between devices: 47.7 us -> none  [start(): return [lax.ppermute(sent[0], 'z', swap_pairs(count, bit))]]
    ppermute x36 -> x20, waiting for transfers between devices: 91 us -> 44.7 us  [start(): lax.ppermute(value, 'shard', swap_pairs(count, bit))]
    ppermute x16 -> x0, starting transfers between devices: 41.5 us -> none  [start(): return [lax.ppermute(sent[0], 'z', swap_pairs(count, bit))]]
    ppermute x24, waiting for transfers between devices: 168 us -> 139 us  [exchange(): lax.ppermute(pieces[k], 'z', [(i, i ^ k) for i in range(count)])]
    ppermute x36 -> x20, starting transfers between devices: 39.1 us -> 21.8 us  [start(): lax.ppermute(value, 'shard', swap_pairs(count, bit))]
    reduce_scatter x4 -> x8, waiting for transfers between devices: 0.03 us -> 14.3 us  [start(): lax.psum_scatter(values[0], 'shard', scatter_dimension=0, tiled=True)]
    ppermute x18 -> x21, starting transfers between devices: 46.5 us -> 58.9 us  [start(): return [lax.ppermute(values[0], 'z', pairs)]]
  transfers between devices with their start and end apart: 129 -> 101, of which waited for: 49 -> 33; matrix products, arithmetic and copies ran while one was open for 23% -> 27% of each run, Pallas kernels for 13% -> 14%
where the time goes in v3:
time: 922 us; the launch traced here: 912 us
  waiting for transfers between devices  298 us (32%)
  Pallas kernels  136 us (15%)
  starting transfers between devices  121 us (13%)
  other arithmetic  120 us (13%)
  matrix products  109 us (12%)
  local copies, waits for them, and re-layouts  99.4 us (11%)
  between operations  17.3 us (2%)
  blocking collectives  10.3 us (1%)
    ppermute x24, waiting for transfers between devices, exchange(): lax.ppermute(pieces[k], 'z', [(i, i ^ k) for i in range(count)])  139 us
    ppermute x21, waiting for transfers between devices, start(): return [lax.ppermute(values[0], 'z', pairs)]  71.4 us
    pallas_call x2, Pallas kernels, attend_back(): pl.pallas_call(attend_back_kernel, name='attend_back', grid=(parts, token...  65.8 us
    ppermute x21, starting transfers between devices, start(): return [lax.ppermute(values[0], 'z', pairs)]  58.9 us
    ppermute x20, waiting for transfers between devices, start(): lax.ppermute(value, 'shard', swap_pairs(count, bit))  44.7 us
    pallas_call x2, Pallas kernels, attend(): pl.pallas_call(attend_kernel, name='attend', grid=(parts, tokens // rows)...  43.8 us
    dot_general x8, matrix products, outer_sum(): lax.dot_general(left, right, (((0,), (0,)), ((), ())), preferred_element_...  41.9 us
    ppermute x24, starting transfers between devices, exchange(): lax.ppermute(pieces[k], 'z', [(i, i ^ k) for i in range(count)])  35.5 us
  transfers between devices with their start and end apart: 101, of which 33 were waited for; matrix products, arithmetic and copies ran while one was open for 27% of the time, Pallas kernels for 14%

profile of v3, /device:TPU:0, one launch (start us, length us, event | category | flops | bytes accessed | tf_op | source)
XLA Modules:
  0.0 911.6 jit_solution(4644440005157154048)
XLA Ops:
  15.6 3.9 fusion.137
  24.6 10.3 %all-gather.3 = bf16[4,2,3072]{2,1,0:T(2,128)(2,1)S(1)} all-gather(bf16[1,2,3072]{2,1,0:T(2,128)(2,1)S(1)} %bitcast.535), channel_id=2, replica_groups=mesh['z'=4,'c'=2,'shard'=4] {'shard'}, dimensions={0}, use_global_device_ids=true | all-gather | bytes 61440 | tf_op jit(solution)/shard_map/all_gather | solution.py:437
  43.6 19.0 %all-gather.10.cloned.1.call-done = bf16[1024,1536]{0,1:T(8,128)(2,1)} async-done(((bf16[256,1536]{0,1:T(8,128)(2,1)}), bf16[1024,1536]{0,1:T(8,128)(2,1)}) %all-gather.10.cloned.1.call-update) | async-done | bytes 3145744 | tf_op jit(solution)/shard_map/all_gather | solution.py:432
  62.6 5.5 add_convert_fusion.1
  87.9 6.5 collective-permute-done.5
  96.0 25.0 %collective-permute-done.4 = bf16[3,576,128]{2,1,0:T(8,128)(2,1)} collective-permute-done((bf16[3,576,128]{2,1,0:T(8,128)(2,1)S(1)}, bf16[3,576,128]{2,1,0:T(8,128)(2,1)}, u32[]{:S(2)}, u32[]{:S(2)}) %collective-permute-start.4) | collective-permute-done | bytes 442400 | tf_op jit(solution)/shard_map/ppermute | solution.py:205
  134.4 21.9 %attend.2 = (bf16[4,576,128]{2,1,0:T(8,128)(2,1)}, f32[4,576,128]{2,1,0:T(8,128)}) custom-call(bf16[4,3,576,128]{3,2,1,0:T(8,128)(2,1)} %pad_maximum_fusion.3.q_ref.k_ref.v_ref, bf16[4,3,576,128]{3,2,1,0:T(8,128)(2,1)} %pad_maximum_fusion.3.q_ref.k_ref.v_ref, bf16[4,3,576,128]{3,2,1,0:T(8,128)(2,1)} %pad_maximum_fusion.3.q_ref.k_ref.v_ref), custom_call_target="tpu_custom_call" | custom-call | flops 10871635968 | bytes 3538944 | tf_op jit(solution)/shard_map/attend/pallas_call | solution.py:93
  178.0 4.1 copy.139
  185.0 7.9 multiply_convert_fusion.3
  192.9 5.1 fusion.16
  204.7 5.0 collective-permute-done.18
  218.6 5.5 add_convert_fusion
  240.8 7.2 collective-permute-done.23
  248.0 25.9 %collective-permute-done.22 = bf16[3,576,128]{2,1,0:T(8,128)(2,1)S(1)} collective-permute-done((bf16[3,576,128]{2,1,0:T(8,128)(2,1)S(1)}, bf16[3,576,128]{2,1,0:T(8,128)(2,1)S(1)}, u32[]{:S(2)}, u32[]{:S(2)}) %collective-permute-start.22) | collective-permute-done | bytes 442400 | tf_op jit(solution)/shard_map/ppermute | solution.py:205
  276.4 21.9 %attend.3 = (bf16[4,576,128]{2,1,0:T(8,128)(2,1)}, f32[4,576,128]{2,1,0:T(8,128)}) custom-call(bf16[4,3,576,128]{3,2,1,0:T(8,128)(2,1)} %pad_maximum_fusion.4.q_ref.k_ref.v_ref, bf16[4,3,576,128]{3,2,1,0:T(8,128)(2,1)} %pad_maximum_fusion.4.q_ref.k_ref.v_ref, bf16[4,3,576,128]{3,2,1,0:T(8,128)(2,1)} %pad_maximum_fusion.4.q_ref.k_ref.v_ref), custom_call_target="tpu_custom_call" | custom-call | flops 10871635968 | bytes 3538944 | tf_op jit(solution)/shard_map/attend/pallas_call | solution.py:93
  308.2 4.9 collective-permute-done.27
  322.4 7.0 multiply_convert_fusion.2
  329.4 7.2 convert_reduce_fusion.1
  346.3 6.3 convolution_convert_fusion.5
  359.7 7.9 convolution_convert_fusion.4
  371.2 33.1 %attend_back.2 = bf16[4,3,576,128]{3,2,1,0:T(8,128)(2,1)} custom-call(bf16[4,3,576,128]{3,2,1,0:T(8,128)(2,1)} %pad_maximum_fusion.4.q_ref.k_ref.v_ref, bf16[4,3,576,128]{3,2,1,0:T(8,128)(2,1)} %pad_maximum_fusion.4.q_ref.k_ref.v_ref, bf16[4,3,576,128]{3,2,1,0:T(8,128)(2,1)} %pad_maximum_fusion.4.q_ref.k_ref.v_ref, ...), custom_call_target="tpu_custom_call" | custom-call | flops 27179089920 | bytes 5898240 | tf_op jit(solution)/shard_map/attend_back/pallas_call | solution.py:164
  414.4 7.5 collective-permute-done.40
  422.0 24.0 %collective-permute-done.39 = bf16[3,576,128]{2,1,0:T(8,128)(2,1)} collective-permute-done((bf16[3,576,128]{2,1,0:T(8,128)(2,1)}, bf16[3,576,128]{2,1,0:T(8,128)(2,1)}, u32[]{:S(2)}, u32[]{:S(2)}) %collective-permute-start.39) | collective-permute-done | bytes 442400 | tf_op jit(solution)/shard_map/ppermute | solution.py:205
  457.0 4.9 fusion.43
  467.9 6.2 convolution_convert_fusion.1
  479.4 11.0 %collective-permute-done.42 = bf16[1024,512]{1,0:T(8,128)(2,1)} collective-permute-done((bf16[1024,512]{1,0:T(8,128)(2,1)}, bf16[1024,512]{1,0:T(8,128)(2,1)}, u32[]{:S(2)}, u32[]{:S(2)}) %collective-permute-start.42) | collective-permute-done | bytes 1048608 | tf_op jit(solution)/shard_map/ppermute | solution.py:370
  499.2 7.3 collective-permute-start.47
  507.0 7.8 convert_reduce_fusion
  519.1 5.0 convolution_convert_fusion.2
  530.6 5.1 convolution_convert_fusion.3
  555.6 14.3 %reduce-scatter.15.cloned.1.call-done = bf16[256,1536]{1,0:T(8,128)(2,1)} async-done(((bf16[1024,1536]{1,0:T(8,128)(2,1)}), bf16[256,1536]{1,0:T(8,128)(2,1)}) %reduce-scatter.15.cloned.1.call-update) | async-done | bytes 786448 | tf_op jit(solution)/shard_map/reduce_scatter | solution.py:354
  579.8 8.3 collective-permute-start.55
  588.1 32.7 %attend_back.3 = bf16[4,3,576,128]{3,2,1,0:T(8,128)(2,1)} custom-call(bf16[4,3,576,128]{3,2,1,0:T(8,128)(2,1)} %pad_maximum_fusion.3.q_ref.k_ref.v_ref, bf16[4,3,576,128]{3,2,1,0:T(8,128)(2,1)} %pad_maximum_fusion.3.q_ref.k_ref.v_ref, bf16[4,3,576,128]{3,2,1,0:T(8,128)(2,1)} %pad_maximum_fusion.3.q_ref.k_ref.v_ref, ...), custom_call_target="tpu_custom_call" | custom-call | flops 27179089920 | bytes 5898240 | tf_op jit(solution)/shard_map/attend_back/pallas_call | solution.py:164
  634.0 9.0 collective-permute-done.58
  648.4 17.5 %collective-permute-done.57 = bf16[3,576,128]{2,1,0:T(8,128)(2,1)S(1)} collective-permute-done((bf16[3,576,128]{2,1,0:T(8,128)(2,1)S(1)}, bf16[3,576,128]{2,1,0:T(8,128)(2,1)S(1)}, u32[]{:S(2)}, u32[]{:S(2)}) %collective-permute-start.57) | collective-permute-done | bytes 442400 | tf_op jit(solution)/shard_map/ppermute | solution.py:205
  672.5 4.9 convolution_convert_fusion
  686.6 6.5 collective-permute-start.65
  705.9 10.8 %collective-permute-done.66 = bf16[2,256,768]{2,1,0:T(8,128)(2,1)} collective-permute-done((bf16[2,256,768]{2,1,0:T(8,128)(2,1)}, bf16[2,256,768]{2,1,0:T(8,128)(2,1)}, u32[]{:S(2)}, u32[]{:S(2)}) %collective-permute-start.66) | collective-permute-done | bytes 786464 | tf_op jit(solution)/shard_map/ppermute | solution.py:344
  736.5 7.4 collective-permute-start.73
  744.4 12.1 %collective-permute-done.71 = bf16[256,768]{1,0:T(8,128)(2,1)} collective-permute-done((bf16[256,768]{1,0:T(8,128)(2,1)}, bf16[256,768]{1,0:T(8,128)(2,1)}, u32[]{:S(2)}, u32[]{:S(2)}) %collective-permute-start.71) | collective-permute-done | bytes 393248 | tf_op jit(solution)/shard_map/ppermute | solution.py:344
  760.2 7.7 collective-permute-done.72
  780.4 7.8 collective-permute-start.77
  789.7 22.5 %collective-permute-done.78 = bf16[64,512]{1,0:T(8,128)(2,1)S(1)} collective-permute-done((bf16[64,512]{1,0:T(8,128)(2,1)S(1)}, bf16[64,512]{1,0:T(8,128)(2,1)S(1)}, u32[]{:S(2)}, u32[]{:S(2)}) %collective-permute-start.78) | collective-permute-done | bytes 65568 | tf_op jit(solution)/shard_map/ppermute | solution.py:370
  819.5 24.8 %collective-permute-done.80 = bf16[1024,512]{1,0:T(8,128)(2,1)S(1)} collective-permute-done((bf16[1024,512]{1,0:T(8,128)(2,1)S(1)}, bf16[1024,512]{1,0:T(8,128)(2,1)S(1)}, u32[]{:S(2)}, u32[]{:S(2)}) %collective-permute-start.80) | collective-permute-done | bytes 1048608 | tf_op jit(solution)/shard_map/ppermute | solution.py:370
  856.8 11.5 %join.4 = f32[2,1024,1024]{2,1,0:T(8,128)} custom-call(s32[1]{0:T(128)} %bitcast.202.core_ref, bf16[1024,512]{1,0:T(8,128)(2,1)} %copy-done.18, bf16[1024,512]{1,0:T(8,128)(2,1)} %copy-done.18, bf16[1024,512]{1,0:T(8,128)(2,1)} %copy-done.48, bf16[1024,512]{1,0:T(8,128)(2,1)} %copy-done.48, bf16[1024,512]{1,0:T(8,128)(2,1)} %copy-done.17, ...), custom_call_target="tpu_custom_call" | custom-call | tf_op jit(solution)/shard_map/join/pallas_call | solution.py:258
  868.4 13.0 %collective-permute-done.85 = bf16[64,512]{1,0:T(8,128)(2,1)S(1)} collective-permute-done((bf16[64,512]{1,0:T(8,128)(2,1)S(1)}, bf16[64,512]{1,0:T(8,128)(2,1)S(1)}, u32[]{:S(2)}, u32[]{:S(2)}) %collective-permute-start.85) | collective-permute-done | bytes 65568 | tf_op jit(solution)/shard_map/ppermute | solution.py:370
  887.8 6.0 join.5
  899.5 5.1 join.6
  (770 shorter events, 352.5 us)
Async XLA Ops:
  7.2 55.4 %all-gather.10.cloned.1.call-start = ((), (), s32[]{:S(2)}) async-start(), calls=%async_computation.8 | async-start | bytes 3932160 | tf_op jit(solution)/shard_map/all_gather | solution.py:432
  15.5 169.4 %all-gather.12.cloned.1.call-start = ((), (), s32[]{:S(2)}) async-start(), calls=%async_computation.9 | async-start | bytes 5242880 | tf_op jit(solution)/shard_map/all_gather | solution.py:432
  24.4 168.5 %all-gather.16.cloned.1.call-start = ((), (), s32[]{:S(2)}) async-start(), calls=%async_computation.19 | async-start | bytes 5242880 | tf_op jit(solution)/shard_map/all_gather | solution.py:432
  38.0 38.1 %collective-permute-start.1 = (bf16[128,512]{1,0:T(8,128)(2,1)}, bf16[128,512]{1,0:T(8,128)(2,1)S(1)}, u32[]{:S(2)}, u32[]{:S(2)}) collective-permute-start(bf16[128,512]{1,0:T(8,128)(2,1)} %get-tuple-element.159), channel_id=1, source_target_pairs={{0,1},{1,0},{2,3},{3,2},{4,5},{5,4},{6,7},{7,6},{8,9},{9,8},{10,11... | collective-permute-start | bytes 393224 | tf_op jit(solution)/shard_map/ppermute | solution.py:386
  39.5 36.6 %collective-permute-start.2 = (bf16[128,512]{1,0:T(8,128)(2,1)}, bf16[128,512]{1,0:T(8,128)(2,1)}, u32[]{:S(2)}, u32[]{:S(2)}) collective-permute-start(bf16[128,512]{1,0:T(8,128)(2,1)} %get-tuple-element.160), channel_id=1, source_target_pairs={{0,2},{1,3},{2,0},{3,1},{4,6},{5,7},{6,4},{7,5},{8,10},{9,11},{10,... | collective-permute-start | bytes 393224 | tf_op jit(solution)/shard_map/ppermute | solution.py:386
  82.9 38.1 %collective-permute-start.4 = (bf16[3,576,128]{2,1,0:T(8,128)(2,1)S(1)}, bf16[3,576,128]{2,1,0:T(8,128)(2,1)}, u32[]{:S(2)}, u32[]{:S(2)}) collective-permute-start(bf16[3,576,128]{2,1,0:T(8,128)(2,1)S(1)} %get-tuple-element.356), channel_id=1, source_target_pairs={{0,16},{8,24},{16,0},{24,8},{1,17},{9,25},{17,1},{25,9},{2,18},{10... | collective-permute-start | bytes 1327112 | tf_op jit(solution)/shard_map/ppermute | solution.py:205
  82.9 45.8 %collective-permute-start.8 = (bf16[256,768]{0,1:T(8,128)(2,1)}, bf16[256,768]{0,1:T(8,128)(2,1)}, u32[]{:S(2)}, u32[]{:S(2)}) collective-permute-start(bf16[256,768]{0,1:T(8,128)(2,1)} %get-tuple-element.167), channel_id=1, source_target_pairs={{0,1},{1,0},{2,3},{3,2},{4,5},{5,4},{6,7},{7,6},{8,9},{9,8},{10,11... | collective-permute-start | bytes 1179656 | tf_op jit(solution)/shard_map/ppermute | solution.py:386
  84.3 44.4 %collective-permute-start.9 = (bf16[256,768]{0,1:T(8,128)(2,1)}, bf16[256,768]{0,1:T(8,128)(2,1)}, u32[]{:S(2)}, u32[]{:S(2)}) collective-permute-start(bf16[256,768]{0,1:T(8,128)(2,1)} %get-tuple-element.168), channel_id=1, source_target_pairs={{0,2},{1,3},{2,0},{3,1},{4,6},{5,7},{6,4},{7,5},{8,10},{9,11},{10,... | collective-permute-start | bytes 1179656 | tf_op jit(solution)/shard_map/ppermute | solution.py:386
  85.1 38.7 %collective-permute-start.3 = (bf16[3,576,128]{2,1,0:T(8,128)(2,1)S(1)}, bf16[3,576,128]{2,1,0:T(8,128)(2,1)}, u32[]{:S(2)}, u32[]{:S(2)}) collective-permute-start(bf16[3,576,128]{2,1,0:T(8,128)(2,1)S(1)} %get-tuple-element.357), channel_id=1, source_target_pairs={{0,8},{8,0},{16,24},{24,16},{1,9},{9,1},{17,25},{25,17},{2,10},{10... | collective-permute-start | bytes 1327112 | tf_op jit(solution)/shard_map/ppermute | solution.py:205
  94.5 31.9 %collective-permute-start.6 = (bf16[2,128,512]{2,1,0:T(8,128)(2,1)}, bf16[2,128,512]{2,1,0:T(8,128)(2,1)}, u32[]{:S(2)}, u32[]{:S(2)}) collective-permute-start(bf16[2,128,512]{2,1,0:T(8,128)(2,1)} %pad_maximum_fusion.51), channel_id=1, source_target_pairs={{0,2},{1,3},{2,0},{3,1},{4,6},{5,7},{6,4},{7,5},{8,10},{9,11},{10,... | collective-permute-start | bytes 786440 | tf_op jit(solution)/shard_map/ppermute | solution.py:386
  123.5 197.2 %all-gather.14.cloned.1.call-start = ((), (), s32[]{:S(2)}) async-start(), calls=%async_computation.10 | async-start | bytes 5242880 | tf_op jit(solution)/shard_map/all_gather | solution.py:432
  184.4 145.0 %all-gather.18.cloned.1.call-start = ((), (), s32[]{:S(2)}) async-start(), calls=%async_computation.20 | async-start | bytes 5242880 | tf_op jit(solution)/shard_map/all_gather | solution.py:432
  235.0 38.9 %collective-permute-start.22 = (bf16[3,576,128]{2,1,0:T(8,128)(2,1)S(1)}, bf16[3,576,128]{2,1,0:T(8,128)(2,1)S(1)}, u32[]{:S(2)}, u32[]{:S(2)}) collective-permute-start(bf16[3,576,128]{2,1,0:T(8,128)(2,1)S(1)} %get-tuple-element.352), channel_id=1, source_target_pairs={{0,16},{8,24},{16,0},{24,8},{1,17},{9,25},{17,1},{25,9},{2,18},{10... | collective-permute-start | bytes 1327112 | tf_op jit(solution)/shard_map/ppermute | solution.py:205
  235.0 38.9 %collective-permute-start.21 = (bf16[3,576,128]{2,1,0:T(8,128)(2,1)S(1)}, bf16[3,576,128]{2,1,0:T(8,128)(2,1)}, u32[]{:S(2)}, u32[]{:S(2)}) collective-permute-start(bf16[3,576,128]{2,1,0:T(8,128)(2,1)S(1)} %get-tuple-element.353), channel_id=1, source_target_pairs={{0,8},{8,0},{16,24},{24,16},{1,9},{9,1},{17,25},{25,17},{2,10},{10... | collective-permute-start | bytes 1327112 | tf_op jit(solution)/shard_map/ppermute | solution.py:205
  237.2 39.1 %collective-permute-start.24 = (bf16[2,128,512]{2,1,0:T(8,128)(2,1)}, bf16[2,128,512]{2,1,0:T(8,128)(2,1)}, u32[]{:S(2)}, u32[]{:S(2)}) collective-permute-start(bf16[2,128,512]{2,1,0:T(8,128)(2,1)} %pad_maximum_fusion.53), channel_id=1, source_target_pairs={{0,2},{1,3},{2,0},{3,1},{4,6},{5,7},{6,4},{7,5},{8,10},{9,11},{10,... | collective-permute-start | bytes 786440 | tf_op jit(solution)/shard_map/ppermute | solution.py:386
  238.5 37.9 %collective-permute-start.25 = (bf16[2,128,512]{2,1,0:T(8,128)(2,1)}, bf16[2,128,512]{2,1,0:T(8,128)(2,1)}, u32[]{:S(2)}, u32[]{:S(2)}) collective-permute-start(bf16[2,128,512]{2,1,0:T(8,128)(2,1)} %pad_maximum_fusion.54), channel_id=1, source_target_pairs={{0,1},{1,0},{2,3},{3,2},{4,5},{5,4},{6,7},{7,6},{8,9},{9,8},{10,11... | collective-permute-start | bytes 786440 | tf_op jit(solution)/shard_map/ppermute | solution.py:386
  240.3 208.3 %reduce-scatter.9.cloned.1.call-start = ((), (), s32[]{:S(2)}) async-start(), calls=%async_computation.11 | async-start | bytes 5242880 | tf_op jit(solution)/shard_map/reduce_scatter | solution.py:354
  355.2 124.3 %reduce-scatter.11.cloned.1.call-start = ((), (), s32[]{:S(2)}) async-start(), calls=%async_computation.12 | async-start | bytes 5242880 | tf_op jit(solution)/shard_map/reduce_scatter | solution.py:354
  371.1 184.5 %reduce-scatter.13.cloned.1.call-start = ((), (), s32[]{:S(2)}) async-start(), calls=%async_computation.13 | async-start | bytes 1310720 | tf_op jit(solution)/shard_map/reduce_scatter | solution.py:354
  408.9 37.0 %collective-permute-start.39 = (bf16[3,576,128]{2,1,0:T(8,128)(2,1)}, bf16[3,576,128]{2,1,0:T(8,128)(2,1)}, u32[]{:S(2)}, u32[]{:S(2)}) collective-permute-start(bf16[3,576,128]{2,1,0:T(8,128)(2,1)} %get-tuple-element.348), channel_id=1, source_target_pairs={{0,16},{8,24},{16,0},{24,8},{1,17},{9,25},{17,1},{25,9},{2,18},{10... | collective-permute-start | bytes 1327112 | tf_op jit(solution)/shard_map/ppermute | solution.py:205
  408.9 37.0 %collective-permute-start.38 = (bf16[3,576,128]{2,1,0:T(8,128)(2,1)S(1)}, bf16[3,576,128]{2,1,0:T(8,128)(2,1)}, u32[]{:S(2)}, u32[]{:S(2)}) collective-permute-start(bf16[3,576,128]{2,1,0:T(8,128)(2,1)S(1)} %get-tuple-element.349), channel_id=1, source_target_pairs={{0,8},{8,0},{16,24},{24,16},{1,9},{9,1},{17,25},{25,17},{2,10},{10... | collective-permute-start | bytes 1327112 | tf_op jit(solution)/shard_map/ppermute | solution.py:205
  467.8 87.8 %reduce-scatter.17.cloned.1.call-start = ((), (), s32[]{:S(2)}) async-start(), calls=%async_computation.15 | async-start | bytes 655360 | tf_op jit(solution)/shard_map/reduce_scatter | solution.py:354
  496.5 73.4 %reduce-scatter.15.cloned.1.call-start = ((), (), s32[]{:S(2)}) async-start(), calls=%async_computation.14 | async-start | bytes 3932160 | tf_op jit(solution)/shard_map/reduce_scatter | solution.py:354
  497.5 43.3 %collective-permute-start.46 = (bf16[1024,512]{1,0:T(8,128)(2,1)}, bf16[1024,512]{1,0:T(8,128)(2,1)}, u32[]{:S(2)}, u32[]{:S(2)}) collective-permute-start(bf16[1024,512]{1,0:T(8,128)(2,1)} %fusion.44), channel_id=1, source_target_pairs={{8,16},{16,8},{9,17},{17,9},{10,18},{18,10},{11,19},{19,11},{12,20... | collective-permute-start | bytes 3145736 | tf_op jit(solution)/shard_map/ppermute | solution.py:370
  499.2 41.5 %collective-permute-start.47 = (bf16[1024,512]{1,0:T(8,128)(2,1)}, bf16[1024,512]{1,0:T(8,128)(2,1)}, u32[]{:S(2)}, u32[]{:S(2)}) collective-permute-start(bf16[1024,512]{1,0:T(8,128)(2,1)} %pad_maximum_fusion.19), channel_id=1, source_target_pairs={{0,8},{24,16},{1,9},{25,17},{2,10},{26,18},{3,11},{27,19},{4,12},{... | collective-permute-start | bytes 3145736 | tf_op jit(solution)/shard_map/ppermute | solution.py:370
  506.5 199.4 %reduce-scatter.21.cloned.1.call-start = ((), (), s32[]{:S(2)}) async-start(), calls=%async_computation.17 | async-start | bytes 1310720 | tf_op jit(solution)/shard_map/reduce_scatter | solution.py:354
  574.8 144.2 %reduce-scatter.19.cloned.1.call-start = ((), (), s32[]{:S(2)}) async-start(), calls=%async_computation.16 | async-start | bytes 5242880 | tf_op jit(solution)/shard_map/reduce_scatter | solution.py:354
  574.8 46.1 %collective-permute-start.51 = (bf16[1024,512]{1,0:T(8,128)(2,1)}, bf16[1024,512]{1,0:T(8,128)(2,1)}, u32[]{:S(2)}, u32[]{:S(2)}) collective-permute-start(bf16[1024,512]{1,0:T(8,128)(2,1)} %fusion.25), channel_id=1, source_target_pairs={{16,24},{8,0},{17,25},{9,1},{18,26},{10,2},{19,27},{11,3},{20,28},... | collective-permute-start | bytes 3145736 | tf_op jit(solution)/shard_map/ppermute | solution.py:370
  576.1 44.8 %collective-permute-start.52 = (bf16[1024,512]{1,0:T(8,128)(2,1)}, bf16[1024,512]{1,0:T(8,128)(2,1)}, u32[]{:S(2)}, u32[]{:S(2)}) collective-permute-start(bf16[1024,512]{1,0:T(8,128)(2,1)} %fusion.45), channel_id=1, source_target_pairs={{8,16},{16,8},{9,17},{17,9},{10,18},{18,10},{11,19},{19,11},{12,20... | collective-permute-start | bytes 3145736 | tf_op jit(solution)/shard_map/ppermute | solution.py:370
  577.8 43.2 %collective-permute-start.53 = (bf16[2,512,512]{2,1,0:T(8,128)(2,1)}, bf16[2,512,512]{2,1,0:T(8,128)(2,1)}, u32[]{:S(2)}, u32[]{:S(2)}) collective-permute-start(bf16[2,512,512]{2,1,0:T(8,128)(2,1)} %dynamic-slice_bitcast_fusion.1), channel_id=1, source_target_pairs={{0,2},{1,3},{2,0},{3,1},{4,6},{5,7},{6,4},{7,5},{8,10},{9,11},{10,... | collective-permute-start | bytes 3145736 | tf_op jit(solution)/shard_map/ppermute | solution.py:344
  579.2 41.8 %collective-permute-start.54 = (bf16[2,512,512]{2,1,0:T(8,128)(2,1)}, bf16[2,512,512]{2,1,0:T(8,128)(2,1)}, u32[]{:S(2)}, u32[]{:S(2)}) collective-permute-start(bf16[2,512,512]{2,1,0:T(8,128)(2,1)} %dynamic-slice_bitcast_fusion), channel_id=1, source_target_pairs={{0,1},{1,0},{2,3},{3,2},{4,5},{5,4},{6,7},{7,6},{8,9},{9,8},{10,11... | collective-permute-start | bytes 3145736 | tf_op jit(solution)/shard_map/ppermute | solution.py:344
  579.8 41.1 %collective-permute-start.55 = (bf16[1088,512]{1,0:T(8,128)(2,1)S(1)}, bf16[1088,512]{1,0:T(8,128)(2,1)S(1)}, u32[]{:S(2)}, u32[]{:S(2)}) collective-permute-start(bf16[1088,512]{1,0:T(8,128)(2,1)S(1)} %constant_dynamic-update-slice_fusion.18), channel_id=1, source_target_pairs={{0,8},{24,16},{1,9},{25,17},{2,10},{26,18},{3,11},{27,19},{4,12},{... | collective-permute-start | bytes 3342344 | tf_op jit(solution)/shard_map/ppermute | solution.py:370
  620.8 147.1 %reduce-scatter.23.cloned.1.call-start = ((), (), s32[]{:S(2)}) async-start(), calls=%async_computation.18 | async-start | bytes 655360 | tf_op jit(solution)/shard_map/reduce_scatter | solution.py:354
  628.8 37.4 %collective-permute-start.59 = (bf16[1024,512]{1,0:T(8,128)(2,1)S(1)}, bf16[1024,512]{1,0:T(8,128)(2,1)S(1)}, u32[]{:S(2)}, u32[]{:S(2)}) collective-permute-start(bf16[1024,512]{1,0:T(8,128)(2,1)S(1)} %fusion.27.refs_4_.refs_5_), channel_id=1, source_target_pairs={{0,4},{4,0},{1,5},{5,1},{2,6},{6,2},{3,7},{7,3},{8,12},{12,8},{9,1... | collective-permute-start | bytes 3145736 | tf_op jit(solution)/shard_map/ppermute | solution.py:210
  628.8 37.1 %collective-permute-start.57 = (bf16[3,576,128]{2,1,0:T(8,128)(2,1)S(1)}, bf16[3,576,128]{2,1,0:T(8,128)(2,1)S(1)}, u32[]{:S(2)}, u32[]{:S(2)}) collective-permute-start(bf16[3,576,128]{2,1,0:T(8,128)(2,1)S(1)} %get-tuple-element.344), channel_id=1, source_target_pairs={{0,16},{8,24},{16,0},{24,8},{1,17},{9,25},{17,1},{25,9},{2,18},{10... | collective-permute-start | bytes 1327112 | tf_op jit(solution)/shard_map/ppermute | solution.py:205
  628.8 37.1 %collective-permute-start.56 = (bf16[3,576,128]{2,1,0:T(8,128)(2,1)S(1)}, bf16[3,576,128]{2,1,0:T(8,128)(2,1)S(1)}, u32[]{:S(2)}, u32[]{:S(2)}) collective-permute-start(bf16[3,576,128]{2,1,0:T(8,128)(2,1)S(1)} %get-tuple-element.345), channel_id=1, source_target_pairs={{0,8},{8,0},{16,24},{24,16},{1,9},{9,1},{17,25},{25,17},{2,10},{10... | collective-permute-start | bytes 1327112 | tf_op jit(solution)/shard_map/ppermute | solution.py:205
  632.4 33.8 %collective-permute-start.60 = (bf16[512,512]{1,0:T(8,128)(2,1)S(1)}, bf16[512,512]{1,0:T(8,128)(2,1)S(1)}, u32[]{:S(2)}, u32[]{:S(2)}) collective-permute-start(bf16[512,512]{1,0:T(8,128)(2,1)S(1)} %dynamic-slice_bitcast_fusion.7), channel_id=1, source_target_pairs={{0,1},{1,0},{2,3},{3,2},{4,5},{5,4},{6,7},{7,6},{8,9},{9,8},{10,11... | collective-permute-start | bytes 1572872 | tf_op jit(solution)/shard_map/ppermute | solution.py:344
  685.3 33.6 %collective-permute-start.63 = (bf16[1024,512]{1,0:T(8,128)(2,1)}, bf16[1024,512]{1,0:T(8,128)(2,1)}, u32[]{:S(2)}, u32[]{:S(2)}) collective-permute-start(bf16[1024,512]{1,0:T(8,128)(2,1)} %fusion.28), channel_id=1, source_target_pairs={{16,24},{8,0},{17,25},{9,1},{18,26},{10,2},{19,27},{11,3},{20,28},... | collective-permute-start | bytes 3145736 | tf_op jit(solution)/shard_map/ppermute | solution.py:370
  686.6 32.3 %collective-permute-start.65 = (bf16[1024,512]{1,0:T(8,128)(2,1)}, bf16[1024,512]{1,0:T(8,128)(2,1)}, u32[]{:S(2)}, u32[]{:S(2)}) collective-permute-start(bf16[1024,512]{1,0:T(8,128)(2,1)} %pad_maximum_fusion.20), channel_id=1, source_target_pairs={{0,8},{24,16},{1,9},{25,17},{2,10},{26,18},{3,11},{27,19},{4,12},{... | collective-permute-start | bytes 3145736 | tf_op jit(solution)/shard_map/ppermute | solution.py:370
  733.4 34.6 %collective-permute-start.69 = (bf16[1088,512]{1,0:T(8,128)(2,1)}, bf16[1088,512]{1,0:T(8,128)(2,1)}, u32[]{:S(2)}, u32[]{:S(2)}) collective-permute-start(bf16[1088,512]{1,0:T(8,128)(2,1)} %fusion.22), channel_id=1, source_target_pairs={{16,24},{8,0},{17,25},{9,1},{18,26},{10,2},{19,27},{11,3},{20,28},... | collective-permute-start | bytes 3342344 | tf_op jit(solution)/shard_map/ppermute | solution.py:370
  734.8 33.2 %collective-permute-start.68 = (bf16[1024,512]{1,0:T(8,128)(2,1)S(1)}, bf16[1024,512]{1,0:T(8,128)(2,1)S(1)}, u32[]{:S(2)}, u32[]{:S(2)}) collective-permute-start(bf16[1024,512]{1,0:T(8,128)(2,1)S(1)} %fusion.30.refs_8_.refs_9_.refs_10_.refs_11_), channel_id=1, source_target_pairs={{0,4},{4,0},{1,5},{5,1},{2,6},{6,2},{3,7},{7,3},{8,12},{12,8},{9,1... | collective-permute-start | bytes 3145736 | tf_op jit(solution)/shard_map/ppermute | solution.py:210
  734.8 33.1 %collective-permute-start.70 = (bf16[1024,512]{1,0:T(8,128)(2,1)}, bf16[1024,512]{1,0:T(8,128)(2,1)}, u32[]{:S(2)}, u32[]{:S(2)}) collective-permute-start(bf16[1024,512]{1,0:T(8,128)(2,1)} %fusion.46), channel_id=1, source_target_pairs={{8,16},{16,8},{9,17},{17,9},{10,18},{18,10},{11,19},{19,11},{12,20... | collective-permute-start | bytes 3145736 | tf_op jit(solution)/shard_map/ppermute | solution.py:370
  778.3 33.9 %collective-permute-start.74 = (bf16[1088,512]{1,0:T(8,128)(2,1)S(1)}, bf16[1088,512]{1,0:T(8,128)(2,1)S(1)}, u32[]{:S(2)}, u32[]{:S(2)}) collective-permute-start(bf16[1088,512]{1,0:T(8,128)(2,1)S(1)} %fusion.24.refs_6_.refs_7_.refs_8_.refs_4_.refs_5_), channel_id=1, source_target_pairs={{0,4},{4,0},{1,5},{5,1},{2,6},{6,2},{3,7},{7,3},{8,12},{12,8},{9,1... | collective-permute-start | bytes 3342344 | tf_op jit(solution)/shard_map/ppermute | solution.py:210
  778.4 33.8 %collective-permute-start.75 = (bf16[1024,512]{1,0:T(8,128)(2,1)S(1)}, bf16[1024,512]{1,0:T(8,128)(2,1)S(1)}, u32[]{:S(2)}, u32[]{:S(2)}) collective-permute-start(bf16[1024,512]{1,0:T(8,128)(2,1)S(1)} %fusion.31), channel_id=1, source_target_pairs={{16,24},{8,0},{17,25},{9,1},{18,26},{10,2},{19,27},{11,3},{20,28},... | collective-permute-start | bytes 3145736 | tf_op jit(solution)/shard_map/ppermute | solution.py:370
  779.7 32.5 %collective-permute-start.76 = (bf16[1024,512]{1,0:T(8,128)(2,1)S(1)}, bf16[1024,512]{1,0:T(8,128)(2,1)S(1)}, u32[]{:S(2)}, u32[]{:S(2)}) collective-permute-start(bf16[1024,512]{1,0:T(8,128)(2,1)S(1)} %fusion.47), channel_id=1, source_target_pairs={{8,16},{16,8},{9,17},{17,9},{10,18},{18,10},{11,19},{19,11},{12,20... | collective-permute-start | bytes 3145736 | tf_op jit(solution)/shard_map/ppermute | solution.py:370
  780.4 31.8 %collective-permute-start.77 = (bf16[1024,512]{1,0:T(8,128)(2,1)}, bf16[1024,512]{1,0:T(8,128)(2,1)S(1)}, u32[]{:S(2)}, u32[]{:S(2)}) collective-permute-start(bf16[1024,512]{1,0:T(8,128)(2,1)} %slice_dynamic-update-slice_fusion), channel_id=1, source_target_pairs={{0,8},{24,16},{1,9},{25,17},{2,10},{26,18},{3,11},{27,19},{4,12},{... | collective-permute-start | bytes 3145736 | tf_op jit(solution)/shard_map/ppermute | solution.py:370
  849.3 32.1 %collective-permute-start.83 = (bf16[1024,512]{1,0:T(8,128)(2,1)S(1)}, bf16[1024,512]{1,0:T(8,128)(2,1)S(1)}, u32[]{:S(2)}, u32[]{:S(2)}) collective-permute-start(bf16[1024,512]{1,0:T(8,128)(2,1)S(1)} %fusion.36.refs_0_.refs_1_.refs_2_.refs_3_), channel_id=1, source_target_pairs={{0,4},{4,0},{1,5},{5,1},{2,6},{6,2},{3,7},{7,3},{8,12},{12,8},{9,1... | collective-permute-start | bytes 3145736 | tf_op jit(solution)/shard_map/ppermute | solution.py:210
  849.3 32.1 %collective-permute-start.84 = (bf16[1024,512]{1,0:T(8,128)(2,1)}, bf16[1024,512]{1,0:T(8,128)(2,1)S(1)}, u32[]{:S(2)}, u32[]{:S(2)}) collective-permute-start(bf16[1024,512]{1,0:T(8,128)(2,1)} %fusion.37), channel_id=1, source_target_pairs={{16,24},{8,0},{17,25},{9,1},{18,26},{10,2},{19,27},{11,3},{20,28},... | collective-permute-start | bytes 3145736 | tf_op jit(solution)/shard_map/ppermute | solution.py:370
  (201 other events, 2135.1 us)
Sparse Core Ops, SparseCore 0:
  15.7 46.8 all-gather.9
  65.0 59.0 all-gather.11
  125.9 62.5 all-gather.15
  190.2 60.6 all-gather.13
  253.1 53.0 all-gather.17
  355.3 51.0 reduce-scatter.8
  410.1 52.6 reduce-scatter.10
  467.9 26.7 reduce-scatter.12
  497.8 24.7 reduce-scatter.16
  526.0 43.9 reduce-scatter.14
  574.9 35.0 reduce-scatter.20
  620.9 61.3 reduce-scatter.18
  734.9 25.9 reduce-scatter.22

commit v4 on v3

--- a/solution.py
+++ b/solution.py
@@ -372,6 +372,28 @@
         (carry,) = yield [send], start, point
         total = total + carry.astype(F32)
     return total.astype(piece.dtype)
+
+
+def halving_flow(values, index, count):
+    bits = bit_count(count)
+    for bit in range(bits):
+        upper = (index >> bit) & 1
+        halves = values.reshape((2, values.shape[0] // 2) + values.shape[1:])
+
+        def start(sent, bit=bit):
+            return [lax.ppermute(sent[0], "z", swap_pairs(count, bit))]
+
+        (other,) = yield [pick(halves, 1 - upper, 0)], start, 1
+        values = add_rounded(pick(halves, upper, 0), other)
+    for bit in reversed(range(bits)):
+        upper = ((index >> bit) & 1) == 1
+
+        def start(sent, bit=bit):
+            return [lax.ppermute(sent[0], "z", swap_pairs(count, bit))]
+
+        (other,) = yield [values], start, 1
+        values = jnp.concatenate([jnp.where(upper, other, values), jnp.where(upper, values, other)], axis=0)
+    return values
 
 
 def gather_flow(part, index, count, holds):
@@ -554,20 +576,23 @@
 
     def line_points(layer, name):
         if layer == 0:
-            return [("", "end0")] if name == "down" else []
-        end, later = f"end{layer}", f"end{layer - 1}"
+            return {"down": [("", "q0"), ("", "end0")], "up": [("", "end0")]}.get(name, [])
+        end, q, later = f"end{layer}", f"q{layer - 1}", f"end{layer - 1}"
         b, c, d, e = [f"{kind}{layer - 1}" for kind in "bcde"]
         return {
             "down": [("", end), ("", b), (c, d)],
-            "up": [("", b), (c, d), (e, later)],
-            "out": [("", d), (e, later)],
+            "up": [("", b), (c, d), (e, q)],
+            "out": [("", d), (e, q), ("", later)],
         }[name]
 
     pieces_of = [{} for _ in range(layers)]
     sums_of = [{} for _ in range(layers)]
 
-    def total_flow(merged, points):
-        merged = yield from line_flow(merged, z_count, points)
+    def total_flow(merged, points, halving):
+        if halving:
+            merged = yield from halving_flow(merged, z_index, z_count)
+        else:
+            merged = yield from line_flow(merged, z_count, points)
         (other,) = yield [merged], lambda values: [swap(values[0])], 1
         return merged, other
 
@@ -576,7 +601,7 @@
         for names in groups[layer]:
             if name in names and all(member in pieces_of[layer] for member in names):
                 members = [pieces_of[layer][member] for member in names]
-                flow = total_flow(merge(members), line_points(layer, names[0]))
+                flow = total_flow(merge(members), line_points(layer, names[0]), layer == 0 and "qkv" in names)
                 pipeline.add(flow, partial(summed, layer, names, [member.size // LANES for member in members]))
 
     def summed(layer, names, extents, pair):
@@ -649,14 +674,12 @@
         grad_pieces = attended_grad.reshape(tokens, z_count, group).transpose(1, 0, 2)
         grad_pieces = pipeline.advance(xor_order(grad_pieces, z_index), f"b{layer}")
         head_grad = exchange(grad_pieces)
-        reduce_weight(layer, "up", outer_sum(normed_two, pre_grad), f"end{layer}")
+        reduce_weight(layer, "up", outer_sum(normed_two, pre_grad), f"q{layer}" if late else f"end{layer}")
         if late:
             reduce_weight(layer, "down", outer_sum(hidden, branch_grad), (f"d{layer}", f"e{layer}"))
-            reduce_weight(layer, "out", outer_sum(attended, out_grad), f"end{layer}")
         head_grad = pipeline.advance(head_grad, f"c{layer}")
         heads_back = pipeline.advance(attend_back(packed, mixed, head_grad, logs), f"d{layer}")
-        if not late:
-            reduce_weight(layer, "out", outer_sum(attended, out_grad), f"c{layer - 1}")
+        reduce_weight(layer, "out", outer_sum(attended, out_grad), f"end{layer}" if late else f"c{layer - 1}")
         arrived = pipeline.advance(exchange(heads_back), f"e{layer}")
         projected_grad = xor_order(arrived, z_index).transpose(2, 0, 1, 3)
         projected_grad = projected_grad.reshape(tokens, 3 * half_width)

time: 922 us -> 981 us (1.064)
  waiting for transfers between devices: 298 us -> 328 us
  local copies, waits for them, and re-layouts: 99.4 us -> 118 us
    ppermute x0 -> x4, waiting for transfers between devices: none -> 35.4 us  [start(): return [lax.ppermute(sent[0], 'z', swap_pairs(count, bit))]]
    ppermute x21 -> x18, waiting for transfers between devices: 71.4 us -> 49.7 us  [start(): return [lax.ppermute(values[0], 'z', pairs)]]
    ppermute x21 -> x18, starting transfers between devices: 58.9 us -> 53.4 us  [start(): return [lax.ppermute(values[0], 'z', pairs)]]
    unnamed x334 -> x344, local copies, waits for them, and re-layouts: 33.3 us -> 35.3 us
  transfers between devices with their start and end apart: 101 -> 102, of which waited for: 33 -> 41; matrix products, arithmetic and copies ran while one was open for 27% -> 26% of each run, Pallas kernels for 14% -> 13%
where the time goes in v4:
time: 981 us; the launch traced here: 970 us
  waiting for transfers between devices  328 us (33%)
  Pallas kernels  136 us (14%)
  starting transfers between devices  126 us (13%)
  other arithmetic  125 us (13%)
  local copies, waits for them, and re-layouts  118 us (12%)
  matrix products  110 us (11%)
  between operations  16.8 us (2%)
  blocking collectives  10.3 us (1%)
    ppermute x24, waiting for transfers between devices, exchange(): lax.ppermute(pieces[k], 'z', [(i, i ^ k) for i in range(count)])  141 us
    pallas_call x2, Pallas kernels, attend_back(): pl.pallas_call(attend_back_kernel, name='attend_back', grid=(parts, token...  65.8 us
    ppermute x18, starting transfers between devices, start(): return [lax.ppermute(values[0], 'z', pairs)]  53.4 us
    ppermute x20, waiting for transfers between devices, start(): lax.ppermute(value, 'shard', swap_pairs(count, bit))  51.9 us
    ppermute x18, waiting for transfers between devices, start(): return [lax.ppermute(values[0], 'z', pairs)]  49.7 us
    pallas_call x2, Pallas kernels, attend(): pl.pallas_call(attend_kernel, name='attend', grid=(parts, tokens // rows)...  43.7 us
    dot_general x8, matrix products, outer_sum(): lax.dot_general(left, right, (((0,), (0,)), ((), ())), preferred_element_...  43.1 us
    convert_element_type x22, other arithmetic, add_rounded(): return (left.astype(F32) + right.astype(F32)).astype(left.dtype)  37.8 us
  transfers between devices with their start and end apart: 102, of which 41 were waited for; matrix products, arithmetic and copies ran while one was open for 26% of the time, Pallas kernels for 13%

profile of v4, /device:TPU:0, one launch (start us, length us, event | category | flops | bytes accessed | tf_op | source)
XLA Modules:
  0.0 970.1 jit_solution(14765823281476473542)
XLA Ops:
  24.6 10.3 %all-gather.3 = bf16[4,2,3072]{2,1,0:T(2,128)(2,1)S(1)} all-gather(bf16[1,2,3072]{2,1,0:T(2,128)(2,1)S(1)} %bitcast.540), channel_id=2, replica_groups=mesh['z'=4,'c'=2,'shard'=4] {'shard'}, dimensions={0}, use_global_device_ids=true | all-gather | bytes 61440 | tf_op jit(solution)/shard_map/all_gather | solution.py:459
  44.6 18.0 %all-gather.10.cloned.1.call-done = bf16[1024,1536]{0,1:T(8,128)(2,1)} async-done(((bf16[256,1536]{0,1:T(8,128)(2,1)}), bf16[1024,1536]{0,1:T(8,128)(2,1)}) %all-gather.10.cloned.1.call-update) | async-done | bytes 3145744 | tf_op jit(solution)/shard_map/all_gather | solution.py:454
  83.1 6.9 collective-permute-done.5
  91.4 24.9 %collective-permute-done.4 = bf16[3,576,128]{2,1,0:T(8,128)(2,1)} collective-permute-done((bf16[3,576,128]{2,1,0:T(8,128)(2,1)S(1)}, bf16[3,576,128]{2,1,0:T(8,128)(2,1)}, u32[]{:S(2)}, u32[]{:S(2)}) %collective-permute-start.4) | collective-permute-done | bytes 442400 | tf_op jit(solution)/shard_map/ppermute | solution.py:205
  122.1 8.4 collective-permute-done.7
  136.0 21.8 %attend.2 = (bf16[4,576,128]{2,1,0:T(8,128)(2,1)}, f32[4,576,128]{2,1,0:T(8,128)}) custom-call(bf16[4,3,576,128]{3,2,1,0:T(8,128)(2,1)} %pad_maximum_fusion.3.q_ref.k_ref.v_ref, bf16[4,3,576,128]{3,2,1,0:T(8,128)(2,1)} %pad_maximum_fusion.3.q_ref.k_ref.v_ref, bf16[4,3,576,128]{3,2,1,0:T(8,128)(2,1)} %pad_maximum_fusion.3.q_ref.k_ref.v_ref), custom_call_target="tpu_custom_call" | custom-call | flops 10871635968 | bytes 3538944 | tf_op jit(solution)/shard_map/attend/pallas_call | solution.py:93
  185.5 7.0 multiply_convert_fusion.3
  192.5 5.1 fusion.16
  221.5 5.6 add_convert_fusion
  246.5 7.5 collective-permute-done.23
  254.0 25.4 %collective-permute-done.22 = bf16[3,576,128]{2,1,0:T(8,128)(2,1)} collective-permute-done((bf16[3,576,128]{2,1,0:T(8,128)(2,1)}, bf16[3,576,128]{2,1,0:T(8,128)(2,1)}, u32[]{:S(2)}, u32[]{:S(2)}) %collective-permute-start.22) | collective-permute-done | bytes 442400 | tf_op jit(solution)/shard_map/ppermute | solution.py:205
  282.0 21.9 %attend.3 = (bf16[4,576,128]{2,1,0:T(8,128)(2,1)}, f32[4,576,128]{2,1,0:T(8,128)}) custom-call(bf16[4,3,576,128]{3,2,1,0:T(8,128)(2,1)} %pad_maximum_fusion.4.q_ref.k_ref.v_ref, bf16[4,3,576,128]{3,2,1,0:T(8,128)(2,1)} %pad_maximum_fusion.4.q_ref.k_ref.v_ref, bf16[4,3,576,128]{3,2,1,0:T(8,128)(2,1)} %pad_maximum_fusion.4.q_ref.k_ref.v_ref), custom_call_target="tpu_custom_call" | custom-call | flops 10871635968 | bytes 3538944 | tf_op jit(solution)/shard_map/attend/pallas_call | solution.py:93
  313.8 5.3 collective-permute-done.27
  328.4 7.0 multiply_convert_fusion.2
  335.4 7.5 convert_reduce_fusion.1
  352.4 6.3 convolution_convert_fusion.5
  365.9 8.1 convolution_convert_fusion.4
  377.7 33.1 %attend_back.2 = bf16[4,3,576,128]{3,2,1,0:T(8,128)(2,1)} custom-call(bf16[4,3,576,128]{3,2,1,0:T(8,128)(2,1)} %pad_maximum_fusion.4.q_ref.k_ref.v_ref, bf16[4,3,576,128]{3,2,1,0:T(8,128)(2,1)} %pad_maximum_fusion.4.q_ref.k_ref.v_ref, bf16[4,3,576,128]{3,2,1,0:T(8,128)(2,1)} %pad_maximum_fusion.4.q_ref.k_ref.v_ref, ...), custom_call_target="tpu_custom_call" | custom-call | flops 27179089920 | bytes 5898240 | tf_op jit(solution)/shard_map/attend_back/pallas_call | solution.py:164
  420.9 7.6 collective-permute-done.40
  428.5 23.9 %collective-permute-done.39 = bf16[3,576,128]{2,1,0:T(8,128)(2,1)} collective-permute-done((bf16[3,576,128]{2,1,0:T(8,128)(2,1)}, bf16[3,576,128]{2,1,0:T(8,128)(2,1)}, u32[]{:S(2)}, u32[]{:S(2)}) %collective-permute-start.39) | collective-permute-done | bytes 442400 | tf_op jit(solution)/shard_map/ppermute | solution.py:205
  463.4 4.9 fusion.40
  474.3 6.2 convolution_convert_fusion.1
  485.9 11.0 %collective-permute-done.42 = bf16[1024,512]{1,0:T(8,128)(2,1)} collective-permute-done((bf16[1024,512]{1,0:T(8,128)(2,1)}, bf16[1024,512]{1,0:T(8,128)(2,1)}, u32[]{:S(2)}, u32[]{:S(2)}) %collective-permute-start.42) | collective-permute-done | bytes 1048608 | tf_op jit(solution)/shard_map/ppermute | solution.py:370
  505.6 6.8 collective-permute-start.47
  512.7 7.8 convert_reduce_fusion
  524.8 5.0 convolution_convert_fusion.2
  535.8 6.4 convolution_convert_fusion.3
  555.7 5.9 collective-permute-done.49
  562.5 13.5 %reduce-scatter.15.cloned.1.call-done = bf16[256,1536]{1,0:T(8,128)(2,1)} async-done(((bf16[1024,1536]{1,0:T(8,128)(2,1)}), bf16[256,1536]{1,0:T(8,128)(2,1)}) %reduce-scatter.15.cloned.1.call-update) | async-done | bytes 786448 | tf_op jit(solution)/shard_map/reduce_scatter | solution.py:354
  585.5 9.2 collective-permute-start.55
  594.7 32.8 %attend_back.3 = bf16[4,3,576,128]{3,2,1,0:T(8,128)(2,1)} custom-call(bf16[4,3,576,128]{3,2,1,0:T(8,128)(2,1)} %pad_maximum_fusion.3.q_ref.k_ref.v_ref, bf16[4,3,576,128]{3,2,1,0:T(8,128)(2,1)} %pad_maximum_fusion.3.q_ref.k_ref.v_ref, bf16[4,3,576,128]{3,2,1,0:T(8,128)(2,1)} %pad_maximum_fusion.3.q_ref.k_ref.v_ref, ...), custom_call_target="tpu_custom_call" | custom-call | flops 27179089920 | bytes 5898240 | tf_op jit(solution)/shard_map/attend_back/pallas_call | solution.py:164
  657.2 22.9 %collective-permute-done.57 = bf16[3,576,128]{2,1,0:T(8,128)(2,1)S(1)} collective-permute-done((bf16[3,576,128]{2,1,0:T(8,128)(2,1)}, bf16[3,576,128]{2,1,0:T(8,128)(2,1)S(1)}, u32[]{:S(2)}, u32[]{:S(2)}) %collective-permute-start.57) | collective-permute-done | bytes 442400 | tf_op jit(solution)/shard_map/ppermute | solution.py:205
  691.0 10.6 %collective-permute-start.64 = (bf16[1024,512]{1,0:T(8,128)(2,1)}, bf16[1024,512]{1,0:T(8,128)(2,1)}, u32[]{:S(2)}, u32[]{:S(2)}) collective-permute-start(bf16[1024,512]{1,0:T(8,128)(2,1)} %pad_maximum_fusion.20), channel_id=1, source_target_pairs={{0,8},{24,16},{1,9},{25,17},{2,10},{26,18},{3,11},{27,19},{4,12},{... | collective-permute-start | bytes 3145736 | tf_op jit(solution)/shard_map/ppermute | solution.py:370
  701.5 4.6 convolution_convert_fusion
  709.4 11.3 %collective-permute-done.62 = bf16[1024,512]{1,0:T(8,128)(2,1)S(1)} collective-permute-done((bf16[1024,512]{1,0:T(8,128)(2,1)}, bf16[1024,512]{1,0:T(8,128)(2,1)S(1)}, u32[]{:S(2)}, u32[]{:S(2)}) %collective-permute-start.62) | collective-permute-done | bytes 1048608 | tf_op jit(solution)/shard_map/ppermute | solution.py:370
  742.5 20.4 %collective-permute-done.69 = bf16[2,256,768]{2,1,0:T(8,128)(2,1)} collective-permute-done((bf16[2,256,768]{2,1,0:T(8,128)(2,1)}, bf16[2,256,768]{2,1,0:T(8,128)(2,1)}, u32[]{:S(2)}, u32[]{:S(2)}) %collective-permute-start.69) | collective-permute-done | bytes 786464 | tf_op jit(solution)/shard_map/ppermute | solution.py:344
  764.5 6.0 collective-permute-start.71
  776.7 15.0 %collective-permute-done.71 = bf16[1024,512]{1,0:T(8,128)(2,1)} collective-permute-done((bf16[1024,512]{1,0:T(8,128)(2,1)}, bf16[1024,512]{1,0:T(8,128)(2,1)}, u32[]{:S(2)}, u32[]{:S(2)}) %collective-permute-start.71) | collective-permute-done | bytes 1048608 | tf_op jit(solution)/shard_map/ppermute | solution.py:370
  817.0 9.4 collective-permute-done.74
  826.9 8.7 reduce-scatter.23.cloned.1.call-done
  851.1 5.6 collective-permute-start.79
  859.2 11.1 %collective-permute-done.80 = bf16[64,512]{1,0:T(8,128)(2,1)} collective-permute-done((bf16[64,512]{1,0:T(8,128)(2,1)}, bf16[64,512]{1,0:T(8,128)(2,1)}, u32[]{:S(2)}, u32[]{:S(2)}) %collective-permute-start.80) | collective-permute-done | bytes 65568 | tf_op jit(solution)/shard_map/ppermute | solution.py:370
  870.3 20.8 %collective-permute-done.79 = bf16[512,512]{1,0:T(8,128)(2,1)} collective-permute-done((bf16[512,512]{1,0:T(8,128)(2,1)}, bf16[512,512]{1,0:T(8,128)(2,1)}, u32[]{:S(2)}, u32[]{:S(2)}) %collective-permute-start.79) | collective-permute-done | bytes 524320 | tf_op jit(solution)/shard_map/ppermute | solution.py:384
  900.5 11.7 %join.4 = f32[2,1024,1024]{2,1,0:T(8,128)} custom-call(s32[1]{0:T(128)} %bitcast.208.core_ref, bf16[1024,512]{1,0:T(8,128)(2,1)} %fusion.33.refs_0_.refs_1_, bf16[1024,512]{1,0:T(8,128)(2,1)} %fusion.33.refs_0_.refs_1_, bf16[1024,512]{1,0:T(8,128)(2,1)} %copy-done.56, bf16[1024,512]{1,0:T(8,128)(2,1)} %copy-done.56, bf16[1024,512]{1,0:T(8,128)(2,1)} %copy-done.20, ...), custom_call_target="tpu_custom_call" | custom-call | tf_op jit(solution)/shard_map/join/pallas_call | solution.py:258
  920.2 4.4 fusion.12
  927.0 5.9 join.5
  936.3 13.1 %collective-permute-done.86 = bf16[512,512]{1,0:T(8,128)(2,1)S(1)} collective-permute-done((bf16[512,512]{1,0:T(8,128)(2,1)}, bf16[512,512]{1,0:T(8,128)(2,1)S(1)}, u32[]{:S(2)}, u32[]{:S(2)}) %collective-permute-start.86) | collective-permute-done | bytes 524320 | tf_op jit(solution)/shard_map/ppermute | solution.py:392
  958.3 5.1 join.6
  (788 shorter events, 395.9 us)
Async XLA Ops:
  7.2 55.4 %all-gather.10.cloned.1.call-start = ((), (), s32[]{:S(2)}) async-start(), calls=%async_computation.8 | async-start | bytes 3932160 | tf_op jit(solution)/shard_map/all_gather | solution.py:454
  15.5 169.9 %all-gather.12.cloned.1.call-start = ((), (), s32[]{:S(2)}) async-start(), calls=%async_computation.9 | async-start | bytes 5242880 | tf_op jit(solution)/shard_map/all_gather | solution.py:454
  24.4 168.1 %all-gather.16.cloned.1.call-start = ((), (), s32[]{:S(2)}) async-start(), calls=%async_computation.19 | async-start | bytes 5242880 | tf_op jit(solution)/shard_map/all_gather | solution.py:454
  38.0 34.9 %collective-permute-start.1 = (bf16[128,512]{1,0:T(8,128)(2,1)}, bf16[128,512]{1,0:T(8,128)(2,1)}, u32[]{:S(2)}, u32[]{:S(2)}) collective-permute-start(bf16[128,512]{1,0:T(8,128)(2,1)} %get-tuple-element.162), channel_id=1, source_target_pairs={{0,1},{1,0},{2,3},{3,2},{4,5},{5,4},{6,7},{7,6},{8,9},{9,8},{10,11... | collective-permute-start | bytes 393224 | tf_op jit(solution)/shard_map/ppermute | solution.py:408
  39.5 33.4 %collective-permute-start.2 = (bf16[128,512]{1,0:T(8,128)(2,1)}, bf16[128,512]{1,0:T(8,128)(2,1)}, u32[]{:S(2)}, u32[]{:S(2)}) collective-permute-start(bf16[128,512]{1,0:T(8,128)(2,1)} %get-tuple-element.163), channel_id=1, source_target_pairs={{0,2},{1,3},{2,0},{3,1},{4,6},{5,7},{6,4},{7,5},{8,10},{9,11},{10,... | collective-permute-start | bytes 393224 | tf_op jit(solution)/shard_map/ppermute | solution.py:408
  78.2 38.1 %collective-permute-start.4 = (bf16[3,576,128]{2,1,0:T(8,128)(2,1)S(1)}, bf16[3,576,128]{2,1,0:T(8,128)(2,1)}, u32[]{:S(2)}, u32[]{:S(2)}) collective-permute-start(bf16[3,576,128]{2,1,0:T(8,128)(2,1)S(1)} %get-tuple-element.362), channel_id=1, source_target_pairs={{0,16},{8,24},{16,0},{24,8},{1,17},{9,25},{17,1},{25,9},{2,18},{10... | collective-permute-start | bytes 1327112 | tf_op jit(solution)/shard_map/ppermute | solution.py:205
  78.2 52.3 %collective-permute-start.8 = (bf16[256,768]{0,1:T(8,128)(2,1)}, bf16[256,768]{0,1:T(8,128)(2,1)}, u32[]{:S(2)}, u32[]{:S(2)}) collective-permute-start(bf16[256,768]{0,1:T(8,128)(2,1)} %get-tuple-element.170), channel_id=1, source_target_pairs={{0,1},{1,0},{2,3},{3,2},{4,5},{5,4},{6,7},{7,6},{8,9},{9,8},{10,11... | collective-permute-start | bytes 1179656 | tf_op jit(solution)/shard_map/ppermute | solution.py:408
  79.6 50.9 %collective-permute-start.9 = (bf16[256,768]{0,1:T(8,128)(2,1)S(1)}, bf16[256,768]{0,1:T(8,128)(2,1)}, u32[]{:S(2)}, u32[]{:S(2)}) collective-permute-start(bf16[256,768]{0,1:T(8,128)(2,1)S(1)} %copy-done.104), channel_id=1, source_target_pairs={{0,2},{1,3},{2,0},{3,1},{4,6},{5,7},{6,4},{7,5},{8,10},{9,11},{10,... | collective-permute-start | bytes 1179656 | tf_op jit(solution)/shard_map/ppermute | solution.py:408
  80.2 39.1 %collective-permute-start.3 = (bf16[3,576,128]{2,1,0:T(8,128)(2,1)S(1)}, bf16[3,576,128]{2,1,0:T(8,128)(2,1)}, u32[]{:S(2)}, u32[]{:S(2)}) collective-permute-start(bf16[3,576,128]{2,1,0:T(8,128)(2,1)S(1)} %get-tuple-element.363), channel_id=1, source_target_pairs={{0,8},{8,0},{16,24},{24,16},{1,9},{9,1},{17,25},{25,17},{2,10},{10... | collective-permute-start | bytes 1327112 | tf_op jit(solution)/shard_map/ppermute | solution.py:205
  90.0 32.1 %collective-permute-start.6 = (bf16[2,128,512]{2,1,0:T(8,128)(2,1)}, bf16[2,128,512]{2,1,0:T(8,128)(2,1)}, u32[]{:S(2)}, u32[]{:S(2)}) collective-permute-start(bf16[2,128,512]{2,1,0:T(8,128)(2,1)} %pad_maximum_fusion.53), channel_id=1, source_target_pairs={{0,2},{1,3},{2,0},{3,1},{4,6},{5,7},{6,4},{7,5},{8,10},{9,11},{10,... | collective-permute-start | bytes 786440 | tf_op jit(solution)/shard_map/ppermute | solution.py:408
  118.8 207.8 %all-gather.14.cloned.1.call-start = ((), (), s32[]{:S(2)}) async-start(), calls=%async_computation.10 | async-start | bytes 5242880 | tf_op jit(solution)/shard_map/all_gather | solution.py:454
  185.1 150.3 %all-gather.18.cloned.1.call-start = ((), (), s32[]{:S(2)}) async-start(), calls=%async_computation.20 | async-start | bytes 5242880 | tf_op jit(solution)/shard_map/all_gather | solution.py:454
  240.5 38.9 %collective-permute-start.22 = (bf16[3,576,128]{2,1,0:T(8,128)(2,1)}, bf16[3,576,128]{2,1,0:T(8,128)(2,1)}, u32[]{:S(2)}, u32[]{:S(2)}) collective-permute-start(bf16[3,576,128]{2,1,0:T(8,128)(2,1)} %get-tuple-element.358), channel_id=1, source_target_pairs={{0,16},{8,24},{16,0},{24,8},{1,17},{9,25},{17,1},{25,9},{2,18},{10... | collective-permute-start | bytes 1327112 | tf_op jit(solution)/shard_map/ppermute | solution.py:205
  240.5 38.9 %collective-permute-start.21 = (bf16[3,576,128]{2,1,0:T(8,128)(2,1)S(1)}, bf16[3,576,128]{2,1,0:T(8,128)(2,1)}, u32[]{:S(2)}, u32[]{:S(2)}) collective-permute-start(bf16[3,576,128]{2,1,0:T(8,128)(2,1)S(1)} %get-tuple-element.359), channel_id=1, source_target_pairs={{0,8},{8,0},{16,24},{24,16},{1,9},{9,1},{17,25},{25,17},{2,10},{10... | collective-permute-start | bytes 1327112 | tf_op jit(solution)/shard_map/ppermute | solution.py:205
  243.3 38.7 %collective-permute-start.24 = (bf16[2,128,512]{2,1,0:T(8,128)(2,1)}, bf16[2,128,512]{2,1,0:T(8,128)(2,1)}, u32[]{:S(2)}, u32[]{:S(2)}) collective-permute-start(bf16[2,128,512]{2,1,0:T(8,128)(2,1)} %pad_maximum_fusion.55), channel_id=1, source_target_pairs={{0,2},{1,3},{2,0},{3,1},{4,6},{5,7},{6,4},{7,5},{8,10},{9,11},{10,... | collective-permute-start | bytes 786440 | tf_op jit(solution)/shard_map/ppermute | solution.py:408
  243.8 38.2 %collective-permute-start.25 = (bf16[2,128,512]{2,1,0:T(8,128)(2,1)S(1)}, bf16[2,128,512]{2,1,0:T(8,128)(2,1)}, u32[]{:S(2)}, u32[]{:S(2)}) collective-permute-start(bf16[2,128,512]{2,1,0:T(8,128)(2,1)S(1)} %copy-done.105), channel_id=1, source_target_pairs={{0,1},{1,0},{2,3},{3,2},{4,5},{5,4},{6,7},{7,6},{8,9},{9,8},{10,11... | collective-permute-start | bytes 786440 | tf_op jit(solution)/shard_map/ppermute | solution.py:408
  246.2 208.7 %reduce-scatter.9.cloned.1.call-start = ((), (), s32[]{:S(2)}) async-start(), calls=%async_computation.11 | async-start | bytes 5242880 | tf_op jit(solution)/shard_map/reduce_scatter | solution.py:354
  361.3 124.6 %reduce-scatter.11.cloned.1.call-start = ((), (), s32[]{:S(2)}) async-start(), calls=%async_computation.12 | async-start | bytes 5242880 | tf_op jit(solution)/shard_map/reduce_scatter | solution.py:354
  377.7 184.9 %reduce-scatter.13.cloned.1.call-start = ((), (), s32[]{:S(2)}) async-start(), calls=%async_computation.13 | async-start | bytes 1310720 | tf_op jit(solution)/shard_map/reduce_scatter | solution.py:354
  414.9 37.4 %collective-permute-start.39 = (bf16[3,576,128]{2,1,0:T(8,128)(2,1)}, bf16[3,576,128]{2,1,0:T(8,128)(2,1)}, u32[]{:S(2)}, u32[]{:S(2)}) collective-permute-start(bf16[3,576,128]{2,1,0:T(8,128)(2,1)} %get-tuple-element.354), channel_id=1, source_target_pairs={{0,16},{8,24},{16,0},{24,8},{1,17},{9,25},{17,1},{25,9},{2,18},{10... | collective-permute-start | bytes 1327112 | tf_op jit(solution)/shard_map/ppermute | solution.py:205
  414.9 37.4 %collective-permute-start.38 = (bf16[3,576,128]{2,1,0:T(8,128)(2,1)S(1)}, bf16[3,576,128]{2,1,0:T(8,128)(2,1)}, u32[]{:S(2)}, u32[]{:S(2)}) collective-permute-start(bf16[3,576,128]{2,1,0:T(8,128)(2,1)S(1)} %get-tuple-element.355), channel_id=1, source_target_pairs={{0,8},{8,0},{16,24},{24,16},{1,9},{9,1},{17,25},{25,17},{2,10},{10... | collective-permute-start | bytes 1327112 | tf_op jit(solution)/shard_map/ppermute | solution.py:205
  474.3 88.3 %reduce-scatter.17.cloned.1.call-start = ((), (), s32[]{:S(2)}) async-start(), calls=%async_computation.15 | async-start | bytes 655360 | tf_op jit(solution)/shard_map/reduce_scatter | solution.py:354
  502.8 73.2 %reduce-scatter.15.cloned.1.call-start = ((), (), s32[]{:S(2)}) async-start(), calls=%async_computation.14 | async-start | bytes 3932160 | tf_op jit(solution)/shard_map/reduce_scatter | solution.py:354
  503.8 43.2 %collective-permute-start.46 = (bf16[1024,512]{1,0:T(8,128)(2,1)}, bf16[1024,512]{1,0:T(8,128)(2,1)}, u32[]{:S(2)}, u32[]{:S(2)}) collective-permute-start(bf16[1024,512]{1,0:T(8,128)(2,1)} %fusion.41), channel_id=1, source_target_pairs={{8,16},{16,8},{9,17},{17,9},{10,18},{18,10},{11,19},{19,11},{12,20... | collective-permute-start | bytes 3145736 | tf_op jit(solution)/shard_map/ppermute | solution.py:370
  505.6 41.4 %collective-permute-start.47 = (bf16[1024,512]{1,0:T(8,128)(2,1)}, bf16[1024,512]{1,0:T(8,128)(2,1)}, u32[]{:S(2)}, u32[]{:S(2)}) collective-permute-start(bf16[1024,512]{1,0:T(8,128)(2,1)} %pad_maximum_fusion.19), channel_id=1, source_target_pairs={{0,8},{24,16},{1,9},{25,17},{2,10},{26,18},{3,11},{27,19},{4,12},{... | collective-permute-start | bytes 3145736 | tf_op jit(solution)/shard_map/ppermute | solution.py:370
  512.4 210.7 %reduce-scatter.19.cloned.1.call-start = ((), (), s32[]{:S(2)}) async-start(), calls=%async_computation.16 | async-start | bytes 5242880 | tf_op jit(solution)/shard_map/reduce_scatter | solution.py:354
  580.9 195.8 %reduce-scatter.21.cloned.1.call-start = ((), (), s32[]{:S(2)}) async-start(), calls=%async_computation.17 | async-start | bytes 1310720 | tf_op jit(solution)/shard_map/reduce_scatter | solution.py:354
  580.9 46.5 %collective-permute-start.51 = (bf16[1024,512]{1,0:T(8,128)(2,1)}, bf16[1024,512]{1,0:T(8,128)(2,1)}, u32[]{:S(2)}, u32[]{:S(2)}) collective-permute-start(bf16[1024,512]{1,0:T(8,128)(2,1)} %fusion.25), channel_id=1, source_target_pairs={{16,24},{8,0},{17,25},{9,1},{18,26},{10,2},{19,27},{11,3},{20,28},... | collective-permute-start | bytes 3145736 | tf_op jit(solution)/shard_map/ppermute | solution.py:370
  582.2 45.2 %collective-permute-start.52 = (bf16[1024,512]{1,0:T(8,128)(2,1)S(1)}, bf16[1024,512]{1,0:T(8,128)(2,1)S(1)}, u32[]{:S(2)}, u32[]{:S(2)}) collective-permute-start(bf16[1024,512]{1,0:T(8,128)(2,1)S(1)} %fusion.42), channel_id=1, source_target_pairs={{8,16},{16,8},{9,17},{17,9},{10,18},{18,10},{11,19},{19,11},{12,20... | collective-permute-start | bytes 3145736 | tf_op jit(solution)/shard_map/ppermute | solution.py:370
  583.4 45.3 %collective-permute-start.53 = (bf16[2,512,512]{2,1,0:T(8,128)(2,1)}, bf16[2,512,512]{2,1,0:T(8,128)(2,1)}, u32[]{:S(2)}, u32[]{:S(2)}) collective-permute-start(bf16[2,512,512]{2,1,0:T(8,128)(2,1)} %dynamic-slice_bitcast_fusion.1), channel_id=1, source_target_pairs={{0,2},{1,3},{2,0},{3,1},{4,6},{5,7},{6,4},{7,5},{8,10},{9,11},{10,... | collective-permute-start | bytes 3145736 | tf_op jit(solution)/shard_map/ppermute | solution.py:344
  584.8 46.5 %collective-permute-start.54 = (bf16[2,512,512]{2,1,0:T(8,128)(2,1)}, bf16[2,512,512]{2,1,0:T(8,128)(2,1)}, u32[]{:S(2)}, u32[]{:S(2)}) collective-permute-start(bf16[2,512,512]{2,1,0:T(8,128)(2,1)} %dynamic-slice_bitcast_fusion), channel_id=1, source_target_pairs={{0,1},{1,0},{2,3},{3,2},{4,5},{5,4},{6,7},{7,6},{8,9},{9,8},{10,11... | collective-permute-start | bytes 3145736 | tf_op jit(solution)/shard_map/ppermute | solution.py:344
  585.5 45.9 %collective-permute-start.55 = (bf16[1088,512]{1,0:T(8,128)(2,1)S(1)}, bf16[1088,512]{1,0:T(8,128)(2,1)S(1)}, u32[]{:S(2)}, u32[]{:S(2)}) collective-permute-start(bf16[1088,512]{1,0:T(8,128)(2,1)S(1)} %constant_dynamic-update-slice_fusion.18), channel_id=1, source_target_pairs={{0,8},{24,16},{1,9},{25,17},{2,10},{26,18},{3,11},{27,19},{4,12},{... | collective-permute-start | bytes 3342344 | tf_op jit(solution)/shard_map/ppermute | solution.py:370
  644.7 36.8 %collective-permute-start.59 = (bf16[1024,512]{1,0:T(8,128)(2,1)S(1)}, bf16[1024,512]{1,0:T(8,128)(2,1)}, u32[]{:S(2)}, u32[]{:S(2)}) collective-permute-start(bf16[1024,512]{1,0:T(8,128)(2,1)S(1)} %fusion.27.refs_4_.refs_5_), channel_id=1, source_target_pairs={{0,4},{4,0},{1,5},{5,1},{2,6},{6,2},{3,7},{7,3},{8,12},{12,8},{9,1... | collective-permute-start | bytes 3145736 | tf_op jit(solution)/shard_map/ppermute | solution.py:210
  648.0 32.1 %collective-permute-start.57 = (bf16[3,576,128]{2,1,0:T(8,128)(2,1)}, bf16[3,576,128]{2,1,0:T(8,128)(2,1)S(1)}, u32[]{:S(2)}, u32[]{:S(2)}) collective-permute-start(bf16[3,576,128]{2,1,0:T(8,128)(2,1)} %get-tuple-element.350), channel_id=1, source_target_pairs={{0,16},{8,24},{16,0},{24,8},{1,17},{9,25},{17,1},{25,9},{2,18},{10... | collective-permute-start | bytes 1327112 | tf_op jit(solution)/shard_map/ppermute | solution.py:205
  651.0 29.1 %collective-permute-start.56 = (bf16[3,576,128]{2,1,0:T(8,128)(2,1)}, bf16[3,576,128]{2,1,0:T(8,128)(2,1)S(1)}, u32[]{:S(2)}, u32[]{:S(2)}) collective-permute-start(bf16[3,576,128]{2,1,0:T(8,128)(2,1)} %get-tuple-element.351), channel_id=1, source_target_pairs={{0,8},{8,0},{16,24},{24,16},{1,9},{9,1},{17,25},{25,17},{2,10},{10... | collective-permute-start | bytes 1327112 | tf_op jit(solution)/shard_map/ppermute | solution.py:205
  651.1 30.4 %collective-permute-start.60 = (bf16[512,512]{1,0:T(8,128)(2,1)}, bf16[512,512]{1,0:T(8,128)(2,1)S(1)}, u32[]{:S(2)}, u32[]{:S(2)}) collective-permute-start(bf16[512,512]{1,0:T(8,128)(2,1)} %dynamic-slice_bitcast_fusion.8), channel_id=1, source_target_pairs={{0,1},{1,0},{2,3},{3,2},{4,5},{5,4},{6,7},{7,6},{8,9},{9,8},{10,11... | collective-permute-start | bytes 1572872 | tf_op jit(solution)/shard_map/ppermute | solution.py:344
  652.6 28.9 %collective-permute-start.61 = (bf16[512,512]{1,0:T(8,128)(2,1)}, bf16[512,512]{1,0:T(8,128)(2,1)S(1)}, u32[]{:S(2)}, u32[]{:S(2)}) collective-permute-start(bf16[512,512]{1,0:T(8,128)(2,1)} %dynamic-slice_bitcast_fusion.7), channel_id=1, source_target_pairs={{0,2},{1,3},{2,0},{3,1},{4,6},{5,7},{6,4},{7,5},{8,10},{9,11},{10,... | collective-permute-start | bytes 1572872 | tf_op jit(solution)/shard_map/ppermute | solution.py:344
  683.0 39.0 %collective-permute-start.63 = (bf16[1088,512]{1,0:T(8,128)(2,1)}, bf16[1088,512]{1,0:T(8,128)(2,1)S(1)}, u32[]{:S(2)}, u32[]{:S(2)}) collective-permute-start(bf16[1088,512]{1,0:T(8,128)(2,1)} %fusion.39), channel_id=1, source_target_pairs={{8,16},{16,8},{9,17},{17,9},{10,18},{18,10},{11,19},{19,11},{12,20... | collective-permute-start | bytes 3342344 | tf_op jit(solution)/shard_map/ppermute | solution.py:370
  689.7 31.0 %collective-permute-start.62 = (bf16[1024,512]{1,0:T(8,128)(2,1)}, bf16[1024,512]{1,0:T(8,128)(2,1)S(1)}, u32[]{:S(2)}, u32[]{:S(2)}) collective-permute-start(bf16[1024,512]{1,0:T(8,128)(2,1)} %fusion.28), channel_id=1, source_target_pairs={{16,24},{8,0},{17,25},{9,1},{18,26},{10,2},{19,27},{11,3},{20,28},... | collective-permute-start | bytes 3145736 | tf_op jit(solution)/shard_map/ppermute | solution.py:370
  691.0 31.1 %collective-permute-start.64 = (bf16[1024,512]{1,0:T(8,128)(2,1)}, bf16[1024,512]{1,0:T(8,128)(2,1)}, u32[]{:S(2)}, u32[]{:S(2)}) collective-permute-start(bf16[1024,512]{1,0:T(8,128)(2,1)} %pad_maximum_fusion.20), channel_id=1, source_target_pairs={{0,8},{24,16},{1,9},{25,17},{2,10},{26,18},{3,11},{27,19},{4,12},{... | collective-permute-start | bytes 3145736 | tf_op jit(solution)/shard_map/ppermute | solution.py:370
  736.8 98.7 %reduce-scatter.23.cloned.1.call-start = ((), (), s32[]{:S(2)}) async-start(), calls=%async_computation.18 | async-start | bytes 655360 | tf_op jit(solution)/shard_map/reduce_scatter | solution.py:354
  739.5 52.2 %collective-permute-start.67 = (bf16[1088,512]{1,0:T(8,128)(2,1)}, bf16[1088,512]{1,0:T(8,128)(2,1)}, u32[]{:S(2)}, u32[]{:S(2)}) collective-permute-start(bf16[1088,512]{1,0:T(8,128)(2,1)} %fusion.22), channel_id=1, source_target_pairs={{16,24},{8,0},{17,25},{9,1},{18,26},{10,2},{19,27},{11,3},{20,28},... | collective-permute-start | bytes 3342344 | tf_op jit(solution)/shard_map/ppermute | solution.py:370
  740.9 35.8 %collective-permute-start.70 = (bf16[2,256,768]{2,1,0:T(8,128)(2,1)}, bf16[2,256,768]{2,1,0:T(8,128)(2,1)}, u32[]{:S(2)}, u32[]{:S(2)}) collective-permute-start(bf16[2,256,768]{2,1,0:T(8,128)(2,1)} %dynamic-slice_bitcast_fusion.2), channel_id=1, source_target_pairs={{0,1},{1,0},{2,3},{3,2},{4,5},{5,4},{6,7},{7,6},{8,9},{9,8},{10,11... | collective-permute-start | bytes 2359304 | tf_op jit(solution)/shard_map/ppermute | solution.py:344
  742.5 34.2 %collective-permute-start.66 = (bf16[1024,512]{1,0:T(8,128)(2,1)S(1)}, bf16[1024,512]{1,0:T(8,128)(2,1)S(1)}, u32[]{:S(2)}, u32[]{:S(2)}) collective-permute-start(bf16[1024,512]{1,0:T(8,128)(2,1)S(1)} %fusion.30.refs_8_.refs_9_.refs_10_.refs_11_), channel_id=1, source_target_pairs={{0,4},{4,0},{1,5},{5,1},{2,6},{6,2},{3,7},{7,3},{8,12},{12,8},{9,1... | collective-permute-start | bytes 3145736 | tf_op jit(solution)/shard_map/ppermute | solution.py:210
  808.5 27.9 %collective-permute-start.72 = (bf16[1088,512]{1,0:T(8,128)(2,1)S(1)}, bf16[1088,512]{1,0:T(8,128)(2,1)S(1)}, u32[]{:S(2)}, u32[]{:S(2)}) collective-permute-start(bf16[1088,512]{1,0:T(8,128)(2,1)S(1)} %fusion.24.refs_6_.refs_7_.refs_8_.refs_4_.refs_5_), channel_id=1, source_target_pairs={{0,4},{4,0},{1,5},{5,1},{2,6},{6,2},{3,7},{7,3},{8,12},{12,8},{9,1... | collective-permute-start | bytes 3342344 | tf_op jit(solution)/shard_map/ppermute | solution.py:210
  849.8 41.3 %collective-permute-start.77 = (bf16[1024,512]{1,0:T(8,128)(2,1)}, bf16[1024,512]{1,0:T(8,128)(2,1)S(1)}, u32[]{:S(2)}, u32[]{:S(2)}) collective-permute-start(bf16[1024,512]{1,0:T(8,128)(2,1)} %fusion.33.refs_0_.refs_1_), channel_id=1, source_target_pairs={{0,4},{4,0},{1,5},{5,1},{2,6},{6,2},{3,7},{7,3},{8,12},{12,8},{9,1... | collective-permute-start | bytes 3145736 | tf_op jit(solution)/shard_map/ppermute | solution.py:210
  849.8 42.3 %collective-permute-start.78 = (bf16[1024,512]{1,0:T(8,128)(2,1)}, bf16[1024,512]{1,0:T(8,128)(2,1)}, u32[]{:S(2)}, u32[]{:S(2)}) collective-permute-start(bf16[1024,512]{1,0:T(8,128)(2,1)} %fusion.34), channel_id=1, source_target_pairs={{16,24},{8,0},{17,25},{9,1},{18,26},{10,2},{19,27},{11,3},{20,28},... | collective-permute-start | bytes 3145736 | tf_op jit(solution)/shard_map/ppermute | solution.py:370
  851.1 40.0 %collective-permute-start.79 = (bf16[512,512]{1,0:T(8,128)(2,1)}, bf16[512,512]{1,0:T(8,128)(2,1)}, u32[]{:S(2)}, u32[]{:S(2)}) collective-permute-start(bf16[512,512]{1,0:T(8,128)(2,1)} %dynamic-slice_bitcast_fusion.6), channel_id=1, source_target_pairs={{0,8},{8,0},{16,24},{24,16},{1,9},{9,1},{17,25},{25,17},{2,10},{10... | collective-permute-start | bytes 1572872 | tf_op jit(solution)/shard_map/ppermute | solution.py:384
  (207 other events, 2581.0 us)
Sparse Core Ops, SparseCore 0:
  15.7 46.8 all-gather.9
  65.0 66.0 all-gather.11
  132.9 58.4 all-gather.15
  193.1 55.3 all-gather.13
  250.8 55.5 all-gather.17
  361.4 51.4 reduce-scatter.8
  416.7 52.6 reduce-scatter.10
  474.4 26.3 reduce-scatter.12
  503.9 24.7 reduce-scatter.16
  532.1 43.9 reduce-scatter.14
  581.0 73.6 reduce-scatter.18
  737.0 33.3 reduce-scatter.20
  808.7 26.8 reduce-scatter.22

commit v5 on v3

--- a/solution.py
+++ b/solution.py
@@ -50,7 +50,7 @@
 
 
 def block_rows(tokens):
-    for rows in (288, 192, 144, 96, 48, 16):
+    for rows in (576, 288, 192, 144, 96, 48, 16):
         if tokens % rows == 0:
             return rows
     return tokens
@@ -270,7 +270,8 @@
 
 
 class Pipeline:
-    def __init__(self):
+    def __init__(self, tied=True):
+        self.tied = tied
         self.running = []
         self.finished = {}
         self.fresh = {}
@@ -286,7 +287,9 @@
             if item[2] is None or last or item[3] == 0 or item[3] == point:
                 due.append(item)
         flights = [item[2] for item in due]
-        main, flights, fresh = lax.optimization_barrier((main, flights, self.fresh))
+        fresh = self.fresh
+        if self.tied:
+            main, flights, fresh = lax.optimization_barrier((main, flights, fresh))
         self.finished.update(fresh)
         self.fresh = {}
         steps = []
@@ -301,7 +304,8 @@
                 item[1](stop.value)
                 waiting += [(added, None) for added in self.running[known:]]
         sends = [step[1] for step in steps]
-        main, sends = lax.optimization_barrier((main, sends))
+        if self.tied:
+            main, sends = lax.optimization_barrier((main, sends))
         for (item, _, start, hold), values in zip(steps, sends):
             item[2], item[3] = start(values), hold
         return main
@@ -439,7 +443,7 @@
     def full_vector(layer, place):
         return vectors_full[:, layer, offsets[place] : offsets[place + 1]].reshape(-1).astype(F32)
 
-    pipeline = Pipeline()
+    pipeline, free = Pipeline(), Pipeline(tied=False)
     weights = []
     for layer in range(layers):
         qkv_part = my_half(qkv_weight[layer].reshape(-1, 3, shards, 2, half_width // shards), 3)
@@ -577,7 +581,8 @@
             if name in names and all(member in pieces_of[layer] for member in names):
                 members = [pieces_of[layer][member] for member in names]
                 flow = total_flow(merge(members), line_points(layer, names[0]))
-                pipeline.add(flow, partial(summed, layer, names, [member.size // LANES for member in members]))
+                line = free if layer == 0 and "qkv" in names else pipeline
+                line.add(flow, partial(summed, layer, names, [member.size // LANES for member in members]))
 
     def summed(layer, names, extents, pair):
         offset = 0
@@ -606,7 +611,8 @@
             flow = scatter_flow(gradient, s_index, shards, points)
         else:
             flow = offload_flow(gradient, points)
-        pipeline.add(flow, partial(arrived_in, layer, name))
+        line = free if layer == 0 and name == "qkv" else pipeline
+        line.add(flow, partial(arrived_in, layer, name))
 
     grad_stream = cotangent.astype(F32).reshape(-1, width)
     for layer in reversed(range(layers)):
@@ -705,6 +711,8 @@
         grad_stream = pipeline.advance(grad_stream, f"end{layer}")
 
     pipeline.drain()
+    free.drain()
+    pipeline.finished.update(pipeline.fresh)
     sums = pipeline.finished
     vector_grads = [sums["small"][:, offsets[place] : offsets[place + 1]] for place in range(8)]
     grad_qkv, grad_out, grad_up, grad_down = sums["qkv"], sums["out"], sums["up"], sums["down"]

time: 922 us -> 914 us (level)
  waiting for transfers between devices: 298 us -> 278 us
  starting transfers between devices: 121 us -> 131 us
    ppermute x20, waiting for transfers between devices: 44.7 us -> 17.2 us  [start(): lax.ppermute(value, 'shard', swap_pairs(count, bit))]
    unnamed x334 -> x350, local copies, waits for them, and re-layouts: 33.3 us -> 30.6 us
  transfers between devices with their start and end apart: 101 -> 101, of which waited for: 33 -> 34; matrix products, arithmetic and copies ran while one was open for 27% -> 33% of each run, Pallas kernels for 14% -> 14%
where the time goes in v5:
time: 914 us; the launch traced here: 903 us
  waiting for transfers between devices  278 us (30%)
  starting transfers between devices  131 us (14%)
  Pallas kernels  130 us (14%)
  other arithmetic  123 us (13%)
  matrix products  110 us (12%)
  local copies, waits for them, and re-layouts  105 us (11%)
  between operations  17.1 us (2%)
  blocking collectives  10.3 us (1%)
    ppermute x24, waiting for transfers between devices, exchange(): lax.ppermute(pieces[k], 'z', [(i, i ^ k) for i in range(count)])  136 us
    ppermute x21, waiting for transfers between devices, start(): return [lax.ppermute(values[0], 'z', pairs)]  74 us
    ppermute x21, starting transfers between devices, start(): return [lax.ppermute(values[0], 'z', pairs)]  67.3 us
    pallas_call x2, Pallas kernels, attend_back(): pl.pallas_call(attend_back_kernel, name='attend_back', grid=(parts, token...  62.5 us
    dot_general x8, matrix products, outer_sum(): lax.dot_general(left, right, (((0,), (0,)), ((), ())), preferred_element_...  41.5 us
    pallas_call x2, Pallas kernels, attend(): pl.pallas_call(attend_kernel, name='attend', grid=(parts, tokens // rows)...  40.8 us
    ppermute x24, starting transfers between devices, exchange(): lax.ppermute(pieces[k], 'z', [(i, i ^ k) for i in range(count)])  35.5 us
    dot_general x8, matrix products, matmul(): return jnp.dot(left, right, preferred_element_type=F32)  35.1 us
  transfers between devices with their start and end apart: 101, of which 34 were waited for; matrix products, arithmetic and copies ran while one was open for 33% of the time, Pallas kernels for 14%

profile of v5, /device:TPU:0, one launch (start us, length us, event | category | flops | bytes accessed | tf_op | source)
XLA Modules:
  0.0 903.3 jit_solution(11540634310758185081)
XLA Ops:
  15.6 3.9 fusion.137
  24.6 10.3 %all-gather.3 = bf16[4,2,3072]{2,1,0:T(2,128)(2,1)S(1)} all-gather(bf16[1,2,3072]{2,1,0:T(2,128)(2,1)S(1)} %bitcast.534), channel_id=2, replica_groups=mesh['z'=4,'c'=2,'shard'=4] {'shard'}, dimensions={0}, use_global_device_ids=true | all-gather | bytes 61440 | tf_op jit(solution)/shard_map/all_gather | solution.py:441
  43.6 19.0 %all-gather.10.cloned.1.call-done = bf16[1024,1536]{0,1:T(8,128)(2,1)} async-done(((bf16[256,1536]{0,1:T(8,128)(2,1)}), bf16[1024,1536]{0,1:T(8,128)(2,1)}) %all-gather.10.cloned.1.call-update) | async-done | bytes 3145744 | tf_op jit(solution)/shard_map/all_gather | solution.py:436
  62.6 5.5 add_convert_fusion.1
  87.9 6.5 collective-permute-done.5
  95.9 25.0 %collective-permute-done.4 = bf16[3,576,128]{2,1,0:T(8,128)(2,1)} collective-permute-done((bf16[3,576,128]{2,1,0:T(8,128)(2,1)S(1)}, bf16[3,576,128]{2,1,0:T(8,128)(2,1)}, u32[]{:S(2)}, u32[]{:S(2)}) %collective-permute-start.4) | collective-permute-done | bytes 442400 | tf_op jit(solution)/shard_map/ppermute | solution.py:205
  134.4 20.4 %attend.2 = (bf16[4,576,128]{2,1,0:T(8,128)(2,1)}, f32[4,576,128]{2,1,0:T(8,128)}) custom-call(bf16[4,3,576,128]{3,2,1,0:T(8,128)(2,1)} %pad_maximum_fusion.3.q_ref.k_ref.v_ref, bf16[4,3,576,128]{3,2,1,0:T(8,128)(2,1)} %pad_maximum_fusion.3.q_ref.k_ref.v_ref, bf16[4,3,576,128]{3,2,1,0:T(8,128)(2,1)} %pad_maximum_fusion.3.q_ref.k_ref.v_ref), custom_call_target="tpu_custom_call" | custom-call | flops 10871635968 | bytes 3538944 | tf_op jit(solution)/shard_map/attend/pallas_call | solution.py:93
  154.9 4.3 collective-permute-done.10
  178.0 4.1 copy.139
  184.9 7.9 multiply_convert_fusion.3
  192.9 5.1 fusion.16
  204.7 5.0 collective-permute-done.18
  218.5 5.5 add_convert_fusion
  240.7 7.3 collective-permute-done.23
  248.0 25.9 %collective-permute-done.22 = bf16[3,576,128]{2,1,0:T(8,128)(2,1)S(1)} collective-permute-done((bf16[3,576,128]{2,1,0:T(8,128)(2,1)S(1)}, bf16[3,576,128]{2,1,0:T(8,128)(2,1)S(1)}, u32[]{:S(2)}, u32[]{:S(2)}) %collective-permute-start.22) | collective-permute-done | bytes 442400 | tf_op jit(solution)/shard_map/ppermute | solution.py:205
  276.3 20.4 %attend.3 = (bf16[4,576,128]{2,1,0:T(8,128)(2,1)}, f32[4,576,128]{2,1,0:T(8,128)}) custom-call(bf16[4,3,576,128]{3,2,1,0:T(8,128)(2,1)} %pad_maximum_fusion.4.q_ref.k_ref.v_ref, bf16[4,3,576,128]{3,2,1,0:T(8,128)(2,1)} %pad_maximum_fusion.4.q_ref.k_ref.v_ref, bf16[4,3,576,128]{3,2,1,0:T(8,128)(2,1)} %pad_maximum_fusion.4.q_ref.k_ref.v_ref), custom_call_target="tpu_custom_call" | custom-call | flops 10871635968 | bytes 3538944 | tf_op jit(solution)/shard_map/attend/pallas_call | solution.py:93
  306.7 4.9 collective-permute-done.27
  321.0 7.0 multiply_convert_fusion.2
  327.9 7.2 convert_reduce_fusion.1
  344.8 6.3 convolution_convert_fusion.5
  358.2 7.8 convolution_convert_fusion.4
  369.7 31.6 %attend_back.2 = bf16[4,3,576,128]{3,2,1,0:T(8,128)(2,1)} custom-call(bf16[4,3,576,128]{3,2,1,0:T(8,128)(2,1)} %pad_maximum_fusion.4.q_ref.k_ref.v_ref, bf16[4,3,576,128]{3,2,1,0:T(8,128)(2,1)} %pad_maximum_fusion.4.q_ref.k_ref.v_ref, bf16[4,3,576,128]{3,2,1,0:T(8,128)(2,1)} %pad_maximum_fusion.4.q_ref.k_ref.v_ref, ...), custom_call_target="tpu_custom_call" | custom-call | flops 27179089920 | bytes 5898240 | tf_op jit(solution)/shard_map/attend_back/pallas_call | solution.py:164
  411.4 7.6 collective-permute-done.40
  419.0 23.9 %collective-permute-done.39 = bf16[3,576,128]{2,1,0:T(8,128)(2,1)} collective-permute-done((bf16[3,576,128]{2,1,0:T(8,128)(2,1)}, bf16[3,576,128]{2,1,0:T(8,128)(2,1)}, u32[]{:S(2)}, u32[]{:S(2)}) %collective-permute-start.39) | collective-permute-done | bytes 442400 | tf_op jit(solution)/shard_map/ppermute | solution.py:205
  454.3 4.9 fusion.43
  465.5 6.2 convolution_convert_fusion.1
  477.0 10.7 %collective-permute-done.42 = bf16[1024,512]{1,0:T(8,128)(2,1)} collective-permute-done((bf16[1024,512]{1,0:T(8,128)(2,1)}, bf16[1024,512]{1,0:T(8,128)(2,1)}, u32[]{:S(2)}, u32[]{:S(2)}) %collective-permute-start.42) | collective-permute-done | bytes 1048608 | tf_op jit(solution)/shard_map/ppermute | solution.py:374
  496.5 6.5 collective-permute-start.47
  503.1 7.1 convert_reduce_fusion
  514.6 5.0 convolution_convert_fusion.2
  527.4 5.1 convolution_convert_fusion.3
  552.5 14.8 %reduce-scatter.15.cloned.1.call-done = bf16[256,1536]{1,0:T(8,128)(2,1)} async-done(((bf16[1024,1536]{1,0:T(8,128)(2,1)}), bf16[256,1536]{1,0:T(8,128)(2,1)}) %reduce-scatter.15.cloned.1.call-update) | async-done | bytes 786448 | tf_op jit(solution)/shard_map/reduce_scatter | solution.py:358
  576.3 10.1 %collective-permute-start.55 = (bf16[1088,512]{1,0:T(8,128)(2,1)S(1)}, bf16[1088,512]{1,0:T(8,128)(2,1)}, u32[]{:S(2)}, u32[]{:S(2)}) collective-permute-start(bf16[1088,512]{1,0:T(8,128)(2,1)S(1)} %constant_dynamic-update-slice_fusion.18), channel_id=1, source_target_pairs={{0,8},{24,16},{1,9},{25,17},{2,10},{26,18},{3,11},{27,19},{4,12},{... | collective-permute-start | bytes 3342344 | tf_op jit(solution)/shard_map/ppermute | solution.py:374
  586.3 30.9 %attend_back.3 = bf16[4,3,576,128]{3,2,1,0:T(8,128)(2,1)} custom-call(bf16[4,3,576,128]{3,2,1,0:T(8,128)(2,1)} %pad_maximum_fusion.3.q_ref.k_ref.v_ref, bf16[4,3,576,128]{3,2,1,0:T(8,128)(2,1)} %pad_maximum_fusion.3.q_ref.k_ref.v_ref, bf16[4,3,576,128]{3,2,1,0:T(8,128)(2,1)} %pad_maximum_fusion.3.q_ref.k_ref.v_ref, ...), custom_call_target="tpu_custom_call" | custom-call | flops 27179089920 | bytes 5898240 | tf_op jit(solution)/shard_map/attend_back/pallas_call | solution.py:164
  636.5 6.9 collective-permute-done.58
  648.8 16.5 %collective-permute-done.57 = bf16[3,576,128]{2,1,0:T(8,128)(2,1)S(1)} collective-permute-done((bf16[3,576,128]{2,1,0:T(8,128)(2,1)}, bf16[3,576,128]{2,1,0:T(8,128)(2,1)S(1)}, u32[]{:S(2)}, u32[]{:S(2)}) %collective-permute-start.57) | collective-permute-done | bytes 442400 | tf_op jit(solution)/shard_map/ppermute | solution.py:205
  674.0 4.6 convolution_convert_fusion
  692.7 10.4 %collective-permute-start.65 = (bf16[1024,512]{1,0:T(8,128)(2,1)}, bf16[1024,512]{1,0:T(8,128)(2,1)}, u32[]{:S(2)}, u32[]{:S(2)}) collective-permute-start(bf16[1024,512]{1,0:T(8,128)(2,1)} %pad_maximum_fusion.20), channel_id=1, source_target_pairs={{0,8},{24,16},{1,9},{25,17},{2,10},{26,18},{3,11},{27,19},{4,12},{... | collective-permute-start | bytes 3145736 | tf_op jit(solution)/shard_map/ppermute | solution.py:374
  739.7 10.6 %collective-permute-start.69 = (bf16[1024,512]{1,0:T(8,128)(2,1)}, bf16[1024,512]{1,0:T(8,128)(2,1)}, u32[]{:S(2)}, u32[]{:S(2)}) collective-permute-start(bf16[1024,512]{1,0:T(8,128)(2,1)} %pad_maximum_fusion.21), channel_id=1, source_target_pairs={{0,8},{24,16},{1,9},{25,17},{2,10},{26,18},{3,11},{27,19},{4,12},{... | collective-permute-start | bytes 3145736 | tf_op jit(solution)/shard_map/ppermute | solution.py:374
  759.8 7.3 reduce-scatter.23.cloned.1.call-done
  767.1 6.0 collective-permute-done.69
  781.7 13.5 %collective-permute-done.84 = bf16[1024,512]{1,0:T(8,128)(2,1)} collective-permute-done((bf16[1024,512]{1,0:T(8,128)(2,1)}, bf16[1024,512]{1,0:T(8,128)(2,1)}, u32[]{:S(2)}, u32[]{:S(2)}) %collective-permute-start.84) | collective-permute-done | bytes 1048608 | tf_op jit(solution)/shard_map/ppermute | solution.py:374
  797.7 7.3 collective-permute-start.73
  818.4 21.4 %collective-permute-done.75 = bf16[1024,512]{1,0:T(8,128)(2,1)S(1)} collective-permute-done((bf16[1024,512]{1,0:T(8,128)(2,1)S(1)}, bf16[1024,512]{1,0:T(8,128)(2,1)S(1)}, u32[]{:S(2)}, u32[]{:S(2)}) %collective-permute-start.75) | collective-permute-done | bytes 1048608 | tf_op jit(solution)/shard_map/ppermute | solution.py:374
  841.7 20.2 %collective-permute-done.86 = bf16[1024,512]{1,0:T(8,128)(2,1)S(1)} collective-permute-done((bf16[1024,512]{1,0:T(8,128)(2,1)S(1)}, bf16[1024,512]{1,0:T(8,128)(2,1)S(1)}, u32[]{:S(2)}, u32[]{:S(2)}) %collective-permute-start.86) | collective-permute-done | bytes 1048608 | tf_op jit(solution)/shard_map/ppermute | solution.py:374
  866.7 11.5 %join.4 = f32[2,1024,1024]{2,1,0:T(8,128)} custom-call(s32[1]{0:T(128)} %bitcast.190.core_ref, bf16[1024,512]{1,0:T(8,128)(2,1)} %copy-done.16, bf16[1024,512]{1,0:T(8,128)(2,1)} %copy-done.16, bf16[1024,512]{1,0:T(8,128)(2,1)} %copy-done.50, bf16[1024,512]{1,0:T(8,128)(2,1)} %copy-done.50, bf16[1024,512]{1,0:T(8,128)(2,1)} %copy-done.15, ...), custom_call_target="tpu_custom_call" | custom-call | tf_op jit(solution)/shard_map/join/pallas_call | solution.py:258
  883.6 5.1 join.6
  888.7 6.0 join.5
  (786 shorter events, 365.2 us)
Async XLA Ops:
  7.2 55.4 %all-gather.10.cloned.1.call-start = ((), (), s32[]{:S(2)}) async-start(), calls=%async_computation.8 | async-start | bytes 3932160 | tf_op jit(solution)/shard_map/all_gather | solution.py:436
  15.5 169.3 %all-gather.12.cloned.1.call-start = ((), (), s32[]{:S(2)}) async-start(), calls=%async_computation.9 | async-start | bytes 5242880 | tf_op jit(solution)/shard_map/all_gather | solution.py:436
  24.4 168.5 %all-gather.16.cloned.1.call-start = ((), (), s32[]{:S(2)}) async-start(), calls=%async_computation.19 | async-start | bytes 5242880 | tf_op jit(solution)/shard_map/all_gather | solution.py:436
  38.0 38.1 %collective-permute-start.1 = (bf16[128,512]{1,0:T(8,128)(2,1)}, bf16[128,512]{1,0:T(8,128)(2,1)S(1)}, u32[]{:S(2)}, u32[]{:S(2)}) collective-permute-start(bf16[128,512]{1,0:T(8,128)(2,1)} %get-tuple-element.141), channel_id=1, source_target_pairs={{0,1},{1,0},{2,3},{3,2},{4,5},{5,4},{6,7},{7,6},{8,9},{9,8},{10,11... | collective-permute-start | bytes 393224 | tf_op jit(solution)/shard_map/ppermute | solution.py:390
  39.5 36.6 %collective-permute-start.2 = (bf16[128,512]{1,0:T(8,128)(2,1)}, bf16[128,512]{1,0:T(8,128)(2,1)}, u32[]{:S(2)}, u32[]{:S(2)}) collective-permute-start(bf16[128,512]{1,0:T(8,128)(2,1)} %get-tuple-element.142), channel_id=1, source_target_pairs={{0,2},{1,3},{2,0},{3,1},{4,6},{5,7},{6,4},{7,5},{8,10},{9,11},{10,... | collective-permute-start | bytes 393224 | tf_op jit(solution)/shard_map/ppermute | solution.py:390
  82.9 38.1 %collective-permute-start.4 = (bf16[3,576,128]{2,1,0:T(8,128)(2,1)S(1)}, bf16[3,576,128]{2,1,0:T(8,128)(2,1)}, u32[]{:S(2)}, u32[]{:S(2)}) collective-permute-start(bf16[3,576,128]{2,1,0:T(8,128)(2,1)S(1)} %get-tuple-element.320), channel_id=1, source_target_pairs={{0,16},{8,24},{16,0},{24,8},{1,17},{9,25},{17,1},{25,9},{2,18},{10... | collective-permute-start | bytes 1327112 | tf_op jit(solution)/shard_map/ppermute | solution.py:205
  82.9 45.8 %collective-permute-start.8 = (bf16[256,768]{0,1:T(8,128)(2,1)}, bf16[256,768]{0,1:T(8,128)(2,1)}, u32[]{:S(2)}, u32[]{:S(2)}) collective-permute-start(bf16[256,768]{0,1:T(8,128)(2,1)} %get-tuple-element.149), channel_id=1, source_target_pairs={{0,1},{1,0},{2,3},{3,2},{4,5},{5,4},{6,7},{7,6},{8,9},{9,8},{10,11... | collective-permute-start | bytes 1179656 | tf_op jit(solution)/shard_map/ppermute | solution.py:390
  84.3 44.4 %collective-permute-start.9 = (bf16[256,768]{0,1:T(8,128)(2,1)}, bf16[256,768]{0,1:T(8,128)(2,1)}, u32[]{:S(2)}, u32[]{:S(2)}) collective-permute-start(bf16[256,768]{0,1:T(8,128)(2,1)} %get-tuple-element.150), channel_id=1, source_target_pairs={{0,2},{1,3},{2,0},{3,1},{4,6},{5,7},{6,4},{7,5},{8,10},{9,11},{10,... | collective-permute-start | bytes 1179656 | tf_op jit(solution)/shard_map/ppermute | solution.py:390
  85.1 38.6 %collective-permute-start.3 = (bf16[3,576,128]{2,1,0:T(8,128)(2,1)S(1)}, bf16[3,576,128]{2,1,0:T(8,128)(2,1)}, u32[]{:S(2)}, u32[]{:S(2)}) collective-permute-start(bf16[3,576,128]{2,1,0:T(8,128)(2,1)S(1)} %get-tuple-element.321), channel_id=1, source_target_pairs={{0,8},{8,0},{16,24},{24,16},{1,9},{9,1},{17,25},{25,17},{2,10},{10... | collective-permute-start | bytes 1327112 | tf_op jit(solution)/shard_map/ppermute | solution.py:205
  94.4 31.9 %collective-permute-start.6 = (bf16[2,128,512]{2,1,0:T(8,128)(2,1)}, bf16[2,128,512]{2,1,0:T(8,128)(2,1)}, u32[]{:S(2)}, u32[]{:S(2)}) collective-permute-start(bf16[2,128,512]{2,1,0:T(8,128)(2,1)} %pad_maximum_fusion.51), channel_id=1, source_target_pairs={{0,2},{1,3},{2,0},{3,1},{4,6},{5,7},{6,4},{7,5},{8,10},{9,11},{10,... | collective-permute-start | bytes 786440 | tf_op jit(solution)/shard_map/ppermute | solution.py:390
  123.5 195.7 %all-gather.14.cloned.1.call-start = ((), (), s32[]{:S(2)}) async-start(), calls=%async_computation.10 | async-start | bytes 5242880 | tf_op jit(solution)/shard_map/all_gather | solution.py:436
  184.4 143.5 %all-gather.18.cloned.1.call-start = ((), (), s32[]{:S(2)}) async-start(), calls=%async_computation.20 | async-start | bytes 5242880 | tf_op jit(solution)/shard_map/all_gather | solution.py:436
  235.0 38.9 %collective-permute-start.22 = (bf16[3,576,128]{2,1,0:T(8,128)(2,1)S(1)}, bf16[3,576,128]{2,1,0:T(8,128)(2,1)S(1)}, u32[]{:S(2)}, u32[]{:S(2)}) collective-permute-start(bf16[3,576,128]{2,1,0:T(8,128)(2,1)S(1)} %get-tuple-element.316), channel_id=1, source_target_pairs={{0,16},{8,24},{16,0},{24,8},{1,17},{9,25},{17,1},{25,9},{2,18},{10... | collective-permute-start | bytes 1327112 | tf_op jit(solution)/shard_map/ppermute | solution.py:205
  235.0 38.9 %collective-permute-start.21 = (bf16[3,576,128]{2,1,0:T(8,128)(2,1)S(1)}, bf16[3,576,128]{2,1,0:T(8,128)(2,1)}, u32[]{:S(2)}, u32[]{:S(2)}) collective-permute-start(bf16[3,576,128]{2,1,0:T(8,128)(2,1)S(1)} %get-tuple-element.317), channel_id=1, source_target_pairs={{0,8},{8,0},{16,24},{24,16},{1,9},{9,1},{17,25},{25,17},{2,10},{10... | collective-permute-start | bytes 1327112 | tf_op jit(solution)/shard_map/ppermute | solution.py:205
  237.2 39.1 %collective-permute-start.24 = (bf16[2,128,512]{2,1,0:T(8,128)(2,1)}, bf16[2,128,512]{2,1,0:T(8,128)(2,1)}, u32[]{:S(2)}, u32[]{:S(2)}) collective-permute-start(bf16[2,128,512]{2,1,0:T(8,128)(2,1)} %pad_maximum_fusion.53), channel_id=1, source_target_pairs={{0,2},{1,3},{2,0},{3,1},{4,6},{5,7},{6,4},{7,5},{8,10},{9,11},{10,... | collective-permute-start | bytes 786440 | tf_op jit(solution)/shard_map/ppermute | solution.py:390
  238.4 37.9 %collective-permute-start.25 = (bf16[2,128,512]{2,1,0:T(8,128)(2,1)}, bf16[2,128,512]{2,1,0:T(8,128)(2,1)}, u32[]{:S(2)}, u32[]{:S(2)}) collective-permute-start(bf16[2,128,512]{2,1,0:T(8,128)(2,1)} %pad_maximum_fusion.54), channel_id=1, source_target_pairs={{0,1},{1,0},{2,3},{3,2},{4,5},{5,4},{6,7},{7,6},{8,9},{9,8},{10,11... | collective-permute-start | bytes 786440 | tf_op jit(solution)/shard_map/ppermute | solution.py:390
  240.2 205.3 %reduce-scatter.9.cloned.1.call-start = ((), (), s32[]{:S(2)}) async-start(), calls=%async_computation.11 | async-start | bytes 5242880 | tf_op jit(solution)/shard_map/reduce_scatter | solution.py:358
  353.7 123.4 %reduce-scatter.11.cloned.1.call-start = ((), (), s32[]{:S(2)}) async-start(), calls=%async_computation.12 | async-start | bytes 5242880 | tf_op jit(solution)/shard_map/reduce_scatter | solution.py:358
  369.6 182.8 %reduce-scatter.13.cloned.1.call-start = ((), (), s32[]{:S(2)}) async-start(), calls=%async_computation.13 | async-start | bytes 1310720 | tf_op jit(solution)/shard_map/reduce_scatter | solution.py:358
  405.8 37.1 %collective-permute-start.39 = (bf16[3,576,128]{2,1,0:T(8,128)(2,1)}, bf16[3,576,128]{2,1,0:T(8,128)(2,1)}, u32[]{:S(2)}, u32[]{:S(2)}) collective-permute-start(bf16[3,576,128]{2,1,0:T(8,128)(2,1)} %get-tuple-element.312), channel_id=1, source_target_pairs={{0,16},{8,24},{16,0},{24,8},{1,17},{9,25},{17,1},{25,9},{2,18},{10... | collective-permute-start | bytes 1327112 | tf_op jit(solution)/shard_map/ppermute | solution.py:205
  405.8 37.1 %collective-permute-start.38 = (bf16[3,576,128]{2,1,0:T(8,128)(2,1)S(1)}, bf16[3,576,128]{2,1,0:T(8,128)(2,1)}, u32[]{:S(2)}, u32[]{:S(2)}) collective-permute-start(bf16[3,576,128]{2,1,0:T(8,128)(2,1)S(1)} %get-tuple-element.313), channel_id=1, source_target_pairs={{0,8},{8,0},{16,24},{24,16},{1,9},{9,1},{17,25},{25,17},{2,10},{10... | collective-permute-start | bytes 1327112 | tf_op jit(solution)/shard_map/ppermute | solution.py:205
  465.3 87.2 %reduce-scatter.17.cloned.1.call-start = ((), (), s32[]{:S(2)}) async-start(), calls=%async_computation.15 | async-start | bytes 655360 | tf_op jit(solution)/shard_map/reduce_scatter | solution.py:358
  493.7 73.5 %reduce-scatter.15.cloned.1.call-start = ((), (), s32[]{:S(2)}) async-start(), calls=%async_computation.14 | async-start | bytes 3932160 | tf_op jit(solution)/shard_map/reduce_scatter | solution.py:358
  494.7 42.8 %collective-permute-start.46 = (bf16[1024,512]{1,0:T(8,128)(2,1)}, bf16[1024,512]{1,0:T(8,128)(2,1)}, u32[]{:S(2)}, u32[]{:S(2)}) collective-permute-start(bf16[1024,512]{1,0:T(8,128)(2,1)} %fusion.44), channel_id=1, source_target_pairs={{8,16},{16,8},{9,17},{17,9},{10,18},{18,10},{11,19},{19,11},{12,20... | collective-permute-start | bytes 3145736 | tf_op jit(solution)/shard_map/ppermute | solution.py:374
  496.5 41.0 %collective-permute-start.47 = (bf16[1024,512]{1,0:T(8,128)(2,1)}, bf16[1024,512]{1,0:T(8,128)(2,1)}, u32[]{:S(2)}, u32[]{:S(2)}) collective-permute-start(bf16[1024,512]{1,0:T(8,128)(2,1)} %pad_maximum_fusion.19), channel_id=1, source_target_pairs={{0,8},{24,16},{1,9},{25,17},{2,10},{26,18},{3,11},{27,19},{4,12},{... | collective-permute-start | bytes 3145736 | tf_op jit(solution)/shard_map/ppermute | solution.py:374
  503.1 222.6 %reduce-scatter.21.cloned.1.call-start = ((), (), s32[]{:S(2)}) async-start(), calls=%async_computation.17 | async-start | bytes 1310720 | tf_op jit(solution)/shard_map/reduce_scatter | solution.py:358
  572.1 153.6 %reduce-scatter.19.cloned.1.call-start = ((), (), s32[]{:S(2)}) async-start(), calls=%async_computation.16 | async-start | bytes 5242880 | tf_op jit(solution)/shard_map/reduce_scatter | solution.py:358
  572.1 45.6 %collective-permute-start.51 = (bf16[1024,512]{1,0:T(8,128)(2,1)}, bf16[1024,512]{1,0:T(8,128)(2,1)}, u32[]{:S(2)}, u32[]{:S(2)}) collective-permute-start(bf16[1024,512]{1,0:T(8,128)(2,1)} %fusion.25), channel_id=1, source_target_pairs={{16,24},{8,0},{17,25},{9,1},{18,26},{10,2},{19,27},{11,3},{20,28},... | collective-permute-start | bytes 3145736 | tf_op jit(solution)/shard_map/ppermute | solution.py:374
  573.4 44.3 %collective-permute-start.52 = (bf16[1024,512]{1,0:T(8,128)(2,1)}, bf16[1024,512]{1,0:T(8,128)(2,1)S(1)}, u32[]{:S(2)}, u32[]{:S(2)}) collective-permute-start(bf16[1024,512]{1,0:T(8,128)(2,1)} %fusion.45), channel_id=1, source_target_pairs={{8,16},{16,8},{9,17},{17,9},{10,18},{18,10},{11,19},{19,11},{12,20... | collective-permute-start | bytes 3145736 | tf_op jit(solution)/shard_map/ppermute | solution.py:374
  574.2 43.6 %collective-permute-start.53 = (bf16[2,512,512]{2,1,0:T(8,128)(2,1)}, bf16[2,512,512]{2,1,0:T(8,128)(2,1)}, u32[]{:S(2)}, u32[]{:S(2)}) collective-permute-start(bf16[2,512,512]{2,1,0:T(8,128)(2,1)} %dynamic-slice_bitcast_fusion.1), channel_id=1, source_target_pairs={{0,2},{1,3},{2,0},{3,1},{4,6},{5,7},{6,4},{7,5},{8,10},{9,11},{10,... | collective-permute-start | bytes 3145736 | tf_op jit(solution)/shard_map/ppermute | solution.py:348
  575.6 42.1 %collective-permute-start.54 = (bf16[2,512,512]{2,1,0:T(8,128)(2,1)}, bf16[2,512,512]{2,1,0:T(8,128)(2,1)}, u32[]{:S(2)}, u32[]{:S(2)}) collective-permute-start(bf16[2,512,512]{2,1,0:T(8,128)(2,1)} %dynamic-slice_bitcast_fusion), channel_id=1, source_target_pairs={{0,1},{1,0},{2,3},{3,2},{4,5},{5,4},{6,7},{7,6},{8,9},{9,8},{10,11... | collective-permute-start | bytes 3145736 | tf_op jit(solution)/shard_map/ppermute | solution.py:348
  576.3 42.5 %collective-permute-start.55 = (bf16[1088,512]{1,0:T(8,128)(2,1)S(1)}, bf16[1088,512]{1,0:T(8,128)(2,1)}, u32[]{:S(2)}, u32[]{:S(2)}) collective-permute-start(bf16[1088,512]{1,0:T(8,128)(2,1)S(1)} %constant_dynamic-update-slice_fusion.18), channel_id=1, source_target_pairs={{0,8},{24,16},{1,9},{25,17},{2,10},{26,18},{3,11},{27,19},{4,12},{... | collective-permute-start | bytes 3342344 | tf_op jit(solution)/shard_map/ppermute | solution.py:374
  617.3 149.8 %reduce-scatter.23.cloned.1.call-start = ((), (), s32[]{:S(2)}) async-start(), calls=%async_computation.18 | async-start | bytes 655360 | tf_op jit(solution)/shard_map/reduce_scatter | solution.py:358
  629.8 36.9 %collective-permute-start.59 = (bf16[1024,512]{1,0:T(8,128)(2,1)S(1)}, bf16[1024,512]{1,0:T(8,128)(2,1)}, u32[]{:S(2)}, u32[]{:S(2)}) collective-permute-start(bf16[1024,512]{1,0:T(8,128)(2,1)S(1)} %fusion.27.refs_4_.refs_5_), channel_id=1, source_target_pairs={{0,4},{4,0},{1,5},{5,1},{2,6},{6,2},{3,7},{7,3},{8,12},{12,8},{9,1... | collective-permute-start | bytes 3145736 | tf_op jit(solution)/shard_map/ppermute | solution.py:210
  631.6 33.7 %collective-permute-start.57 = (bf16[3,576,128]{2,1,0:T(8,128)(2,1)}, bf16[3,576,128]{2,1,0:T(8,128)(2,1)S(1)}, u32[]{:S(2)}, u32[]{:S(2)}) collective-permute-start(bf16[3,576,128]{2,1,0:T(8,128)(2,1)} %get-tuple-element.308), channel_id=1, source_target_pairs={{0,16},{8,24},{16,0},{24,8},{1,17},{9,25},{17,1},{25,9},{2,18},{10... | collective-permute-start | bytes 1327112 | tf_op jit(solution)/shard_map/ppermute | solution.py:205
  631.6 33.7 %collective-permute-start.56 = (bf16[3,576,128]{2,1,0:T(8,128)(2,1)}, bf16[3,576,128]{2,1,0:T(8,128)(2,1)S(1)}, u32[]{:S(2)}, u32[]{:S(2)}) collective-permute-start(bf16[3,576,128]{2,1,0:T(8,128)(2,1)} %get-tuple-element.309), channel_id=1, source_target_pairs={{0,8},{8,0},{16,24},{24,16},{1,9},{9,1},{17,25},{25,17},{2,10},{10... | collective-permute-start | bytes 1327112 | tf_op jit(solution)/shard_map/ppermute | solution.py:205
  634.9 31.8 %collective-permute-start.60 = (bf16[512,512]{1,0:T(8,128)(2,1)}, bf16[512,512]{1,0:T(8,128)(2,1)S(1)}, u32[]{:S(2)}, u32[]{:S(2)}) collective-permute-start(bf16[512,512]{1,0:T(8,128)(2,1)} %dynamic-slice_bitcast_fusion.7), channel_id=1, source_target_pairs={{0,1},{1,0},{2,3},{3,2},{4,5},{5,4},{6,7},{7,6},{8,9},{9,8},{10,11... | collective-permute-start | bytes 1572872 | tf_op jit(solution)/shard_map/ppermute | solution.py:348
  691.2 34.4 %collective-permute-start.63 = (bf16[1024,512]{1,0:T(8,128)(2,1)}, bf16[1024,512]{1,0:T(8,128)(2,1)}, u32[]{:S(2)}, u32[]{:S(2)}) collective-permute-start(bf16[1024,512]{1,0:T(8,128)(2,1)} %fusion.28), channel_id=1, source_target_pairs={{16,24},{8,0},{17,25},{9,1},{18,26},{10,2},{19,27},{11,3},{20,28},... | collective-permute-start | bytes 3145736 | tf_op jit(solution)/shard_map/ppermute | solution.py:374
  692.7 33.0 %collective-permute-start.65 = (bf16[1024,512]{1,0:T(8,128)(2,1)}, bf16[1024,512]{1,0:T(8,128)(2,1)}, u32[]{:S(2)}, u32[]{:S(2)}) collective-permute-start(bf16[1024,512]{1,0:T(8,128)(2,1)} %pad_maximum_fusion.20), channel_id=1, source_target_pairs={{0,8},{24,16},{1,9},{25,17},{2,10},{26,18},{3,11},{27,19},{4,12},{... | collective-permute-start | bytes 3145736 | tf_op jit(solution)/shard_map/ppermute | solution.py:374
  734.6 38.5 %collective-permute-start.67 = (bf16[1088,512]{1,0:T(8,128)(2,1)}, bf16[1088,512]{1,0:T(8,128)(2,1)}, u32[]{:S(2)}, u32[]{:S(2)}) collective-permute-start(bf16[1088,512]{1,0:T(8,128)(2,1)} %fusion.22), channel_id=1, source_target_pairs={{16,24},{8,0},{17,25},{9,1},{18,26},{10,2},{19,27},{11,3},{20,28},... | collective-permute-start | bytes 3342344 | tf_op jit(solution)/shard_map/ppermute | solution.py:374
  738.0 29.1 %collective-permute-start.66 = (bf16[1024,512]{1,0:T(8,128)(2,1)S(1)}, bf16[1024,512]{1,0:T(8,128)(2,1)S(1)}, u32[]{:S(2)}, u32[]{:S(2)}) collective-permute-start(bf16[1024,512]{1,0:T(8,128)(2,1)S(1)} %fusion.30.refs_8_.refs_9_.refs_10_.refs_11_), channel_id=1, source_target_pairs={{0,4},{4,0},{1,5},{5,1},{2,6},{6,2},{3,7},{7,3},{8,12},{12,8},{9,1... | collective-permute-start | bytes 3145736 | tf_op jit(solution)/shard_map/ppermute | solution.py:210
  738.1 29.0 %collective-permute-start.68 = (bf16[1024,512]{1,0:T(8,128)(2,1)}, bf16[1024,512]{1,0:T(8,128)(2,1)}, u32[]{:S(2)}, u32[]{:S(2)}) collective-permute-start(bf16[1024,512]{1,0:T(8,128)(2,1)} %fusion.46), channel_id=1, source_target_pairs={{8,16},{16,8},{9,17},{17,9},{10,18},{18,10},{11,19},{19,11},{12,20... | collective-permute-start | bytes 3145736 | tf_op jit(solution)/shard_map/ppermute | solution.py:374
  739.7 33.4 %collective-permute-start.69 = (bf16[1024,512]{1,0:T(8,128)(2,1)}, bf16[1024,512]{1,0:T(8,128)(2,1)}, u32[]{:S(2)}, u32[]{:S(2)}) collective-permute-start(bf16[1024,512]{1,0:T(8,128)(2,1)} %pad_maximum_fusion.21), channel_id=1, source_target_pairs={{0,8},{24,16},{1,9},{25,17},{2,10},{26,18},{3,11},{27,19},{4,12},{... | collective-permute-start | bytes 3145736 | tf_op jit(solution)/shard_map/ppermute | solution.py:374
  757.6 37.6 %collective-permute-start.84 = (bf16[1024,512]{1,0:T(8,128)(2,1)}, bf16[1024,512]{1,0:T(8,128)(2,1)}, u32[]{:S(2)}, u32[]{:S(2)}) collective-permute-start(bf16[1024,512]{1,0:T(8,128)(2,1)} %slice_dynamic-update-slice_fusion), channel_id=1, source_target_pairs={{0,8},{24,16},{1,9},{25,17},{2,10},{26,18},{3,11},{27,19},{4,12},{... | collective-permute-start | bytes 3145736 | tf_op jit(solution)/shard_map/ppermute | solution.py:374
  809.9 29.9 %collective-permute-start.75 = (bf16[1024,512]{1,0:T(8,128)(2,1)S(1)}, bf16[1024,512]{1,0:T(8,128)(2,1)S(1)}, u32[]{:S(2)}, u32[]{:S(2)}) collective-permute-start(bf16[1024,512]{1,0:T(8,128)(2,1)S(1)} %fusion.34), channel_id=1, source_target_pairs={{16,24},{8,0},{17,25},{9,1},{18,26},{10,2},{19,27},{11,3},{20,28},... | collective-permute-start | bytes 3145736 | tf_op jit(solution)/shard_map/ppermute | solution.py:374
  813.0 48.9 %collective-permute-start.86 = (bf16[1024,512]{1,0:T(8,128)(2,1)S(1)}, bf16[1024,512]{1,0:T(8,128)(2,1)S(1)}, u32[]{:S(2)}, u32[]{:S(2)}) collective-permute-start(bf16[1024,512]{1,0:T(8,128)(2,1)S(1)} %fusion.39), channel_id=1, source_target_pairs={{16,24},{8,0},{17,25},{9,1},{18,26},{10,2},{19,27},{11,3},{20,28},... | collective-permute-start | bytes 3145736 | tf_op jit(solution)/shard_map/ppermute | solution.py:374
  818.0 47.5 %collective-permute-start.31 = (f32[288,1024]{1,0:T(8,128)S(1)}, f32[288,1024]{1,0:T(8,128)S(1)}, u32[]{:S(2)}, u32[]{:S(2)}) collective-permute-start(f32[288,1024]{1,0:T(8,128)S(1)} %slice.532), channel_id=1, source_target_pairs={{0,4},{4,0},{1,5},{5,1},{2,6},{6,2},{3,7},{7,3},{8,12},{12,8},{9,1... | collective-permute-start | bytes 3538952 | tf_op jit(solution)/shard_map/ppermute | solution.py:210
  841.7 36.6 %collective-permute-start.77 = (bf16[1024,512]{1,0:T(8,128)(2,1)S(1)}, bf16[1024,512]{1,0:T(8,128)(2,1)S(1)}, u32[]{:S(2)}, u32[]{:S(2)}) collective-permute-start(bf16[1024,512]{1,0:T(8,128)(2,1)S(1)} %fusion.36.refs_0_.refs_1_.refs_2_.refs_3_), channel_id=1, source_target_pairs={{0,4},{4,0},{1,5},{5,1},{2,6},{6,2},{3,7},{7,3},{8,12},{12,8},{9,1... | collective-permute-start | bytes 3145736 | tf_op jit(solution)/shard_map/ppermute | solution.py:210
  (209 other events, 2299.0 us)
Sparse Core Ops, SparseCore 0:
  15.7 46.8 all-gather.9
  65.0 59.0 all-gather.11
  125.9 62.5 all-gather.15
  190.2 60.6 all-gather.13
  253.1 53.0 all-gather.17
  353.8 50.9 reduce-scatter.8
  408.6 52.6 reduce-scatter.10
  465.4 26.5 reduce-scatter.12
  495.1 24.7 reduce-scatter.16
  523.3 43.9 reduce-scatter.14
  572.2 35.1 reduce-scatter.20
  617.4 60.8 reduce-scatter.18
  738.1 28.9 reduce-scatter.22
